TPU v7x, 32 devices: a whole 2x2x4 slice. The times are simulated.
32 devices in a mesh: dp: 8 (over y, x, core), stream: 4 (over z).
Axes of the slice: x: 2, y: 2, z: 4, core: 2. Of those that a mesh axis runs over, the one named last changes fastest.
Arguments:
- visual: bfloat16 [8, 8, 256, 1024], P('dp', None, 'stream'), may hold values from -6 to 6
- conditioning: bfloat16 [8, 8, 2, 1024], P('dp', 'stream'), may hold values from -6 to 6
- d_visual: bfloat16 [8, 8, 256, 1024], P('dp', None, 'stream'), may hold values from -6 to 6
- d_conditioning: bfloat16 [8, 8, 2, 1024], P('dp', 'stream'), may hold values from -6 to 6
- episode_frames: int32 [8, 3], P('dp'), may hold values from 1 to 5, 8 in all within a row
- patch_mask: int32 [8, 8, 256], P('dp'), may hold values 0 or 1
- ln1_gain: bfloat16 [1024], replicated, may hold values from 0.5 to 1.5
- ln1_bias: bfloat16 [1024], replicated, may hold values from -1.75 to 1.75
- w_qkv: bfloat16 [1024, 3072], replicated, may hold values from -0.1875 to 0.1875
- b_qkv: bfloat16 [3072], replicated, may hold values from -1.75 to 1.75
- w_proj: bfloat16 [1024, 1024], replicated, may hold values from -0.75 to 0.75
- b_proj: bfloat16 [1024], replicated, may hold values from -1.75 to 1.75
- ln2_gain: bfloat16 [1024], replicated, may hold values from 0.5 to 1.5
- ln2_bias: bfloat16 [1024], replicated, may hold values from -1.75 to 1.75
- w_in: bfloat16 [1024, 4096], replicated, may hold values from -0.1875 to 0.1875
- b_in: bfloat16 [4096], replicated, may hold values from -1.75 to 1.75
- w_out: bfloat16 [4096, 1024], replicated, may hold values from -0.09375 to 0.09375
- b_out: bfloat16 [1024], replicated, may hold values from -1.75 to 1.75
Outputs:
- out_visual: bfloat16 [8, 8, 256, 1024], P('dp', None, 'stream')
- out_conditioning: bfloat16 [8, 8, 2, 1024], P('dp', 'stream')
- grad_visual: float32 [8, 8, 256, 1024], P('dp', None, 'stream')
- grad_conditioning: float32 [8, 8, 2, 1024], P('dp', 'stream')
- grad_ln1_gain: float32 [1024], P(('dp', 'stream'))
- grad_ln1_bias: float32 [1024], P(('dp', 'stream'))
- grad_w_qkv: float32 [1024, 3072], P(('dp', 'stream'))
- grad_b_query_key: float32 [2048], P(('dp', 'stream'))
- grad_b_value: float32 [1024], P(('dp', 'stream'))
- grad_w_proj: float32 [1024, 1024], P(('dp', 'stream'))
- grad_b_proj: float32 [1024], P(('dp', 'stream'))
- grad_ln2_gain: float32 [1024], P(('dp', 'stream'))
- grad_ln2_bias: float32 [1024], P(('dp', 'stream'))
- grad_w_in: float32 [1024, 4096], P(('dp', 'stream'))
- grad_b_in: float32 [4096], P(('dp', 'stream'))
- grad_w_out: float32 [4096, 1024], P(('dp', 'stream'))
- grad_b_out: float32 [1024], P(('dp', 'stream'))
Inputs may be any that keep to these rules, and one draw needn't show every extreme that they name: `episode_frames`: each row holds the frame counts of the 3 episodes packed in one sequence; they sum to 8, and the longest holds exactly 5. `patch_mask`: 1 marks a visual row that may be attended to.
All inputs are finite; a program needn't handle non-finite values. No bound on the sum of `patch_mask` on one device may be relied on, other than what follows from the above.
Results may differ from a plain program's by a relative error of at most 0.035.
Values may be sent and summed in bfloat16 or wider, within the bound.
A program may use at most 192 MiB of HBM per device.

v0:
```python
import math

import jax
import jax.numpy as jnp
from jax import lax
from jax.sharding import PartitionSpec as P

D = 1024
HEADS = 16
HEAD_DIM = 64
GRID = 16
COND = 2
FRAMES = 8


def layer_norm(values, norm_gain, norm_shift):
    centre = values - jnp.mean(values, axis=-1, keepdims=True)
    spread = jnp.mean(centre * centre, axis=-1, keepdims=True)
    return centre * lax.rsqrt(spread + 1e-06) * norm_gain + norm_shift


def exact_gelu(values):
    return jax.nn.gelu(values, approximate=False)


def rotary_tables(times, grid_rows, grid_cols, half_dim):
    pair_ids = jnp.arange(half_dim, dtype=jnp.int32)
    exponent = jnp.where(pair_ids < 30, (pair_ids % 10).astype(jnp.float32) / 10.0, 0.0)
    inverse_freq = jnp.exp(-math.log(10000.0) * exponent)
    zeros_pos = jnp.zeros_like(times)
    position = jnp.where(
        pair_ids[None, :] < 10,
        times[:, None],
        jnp.where(
            pair_ids[None, :] < 20,
            grid_rows[:, None],
            jnp.where(pair_ids[None, :] < 30, grid_cols[:, None], zeros_pos[:, None]),
        ),
    )
    angles = position * inverse_freq[None, :]
    return (jnp.cos(angles), jnp.sin(angles))


def rotate(values, cosine_table, sine_table):
    shaped = values.reshape(values.shape[0], values.shape[1], -1, 2)
    first_part = shaped[..., 0]
    second_part = shaped[..., 1]
    cosine_rows = cosine_table[:, None, :]
    sine_rows = sine_table[:, None, :]
    turned_first = first_part * cosine_rows - second_part * sine_rows
    turned_second = first_part * sine_rows + second_part * cosine_rows
    return jnp.stack([turned_first, turned_second], axis=-1).reshape(values.shape)


def episode_of(lengths, frame_ids):
    episode_ends = jnp.cumsum(lengths, axis=-1)
    reached = episode_ends[:, None, :] <= frame_ids[None, :, None]
    episode = jnp.sum(reached.astype(jnp.int32), axis=-1)
    episode_start = jnp.sum(jnp.where(reached, lengths[:, None, :], 0), axis=-1)
    return (episode, frame_ids[None, :] - episode_start)


def row_layout(device_ids, local_rows, visual_rows, patch_part, frame_part):
    positions = jnp.arange(local_rows, dtype=jnp.int32)[None, :]
    devices = device_ids[:, None]
    is_visual = positions < visual_rows
    frame_ids = jnp.where(
        is_visual, positions // patch_part, devices * frame_part + (positions - visual_rows) // COND
    )
    patch_ids = devices * patch_part + positions % patch_part
    grid_rows = jnp.where(is_visual, patch_ids // GRID, 0)
    grid_cols = jnp.where(is_visual, patch_ids % GRID, 0)
    return (frame_ids.reshape(-1), grid_rows.reshape(-1), grid_cols.reshape(-1))


def per_device(
    visual,
    conditioning,
    d_visual,
    d_conditioning,
    episode_frames,
    patch_mask,
    ln1_gain,
    ln1_bias,
    w_qkv,
    b_qkv,
    w_proj,
    b_proj,
    ln2_gain,
    ln2_bias,
    w_in,
    b_in,
    w_out,
    b_out,
):
    streams = lax.axis_size("stream")
    member = lax.axis_index("stream")
    seq_count = visual.shape[0]
    patch_part = visual.shape[2]
    frame_part = conditioning.shape[1]
    visual_rows = FRAMES * patch_part
    extra_rows = frame_part * COND
    local_rows = visual_rows + extra_rows
    all_rows = streams * local_rows
    score_scale = HEAD_DIM ** (-0.5)
    inputs = (
        jnp.concatenate(
            [
                visual.reshape(seq_count, visual_rows, D),
                conditioning.reshape(seq_count, extra_rows, D),
            ],
            axis=1,
        )
        .astype(jnp.float32)
        .reshape(seq_count * local_rows, D)
    )
    key_frames, key_grid_rows, key_grid_cols = row_layout(
        jnp.arange(streams, dtype=jnp.int32), local_rows, visual_rows, patch_part, frame_part
    )
    query_frames, query_grid_rows, query_grid_cols = row_layout(
        member.reshape(1), local_rows, visual_rows, patch_part, frame_part
    )
    key_episode, key_times = episode_of(episode_frames, key_frames)
    query_episode, query_times = episode_of(episode_frames, query_frames)
    visible = (
        patch_mask.reshape(seq_count, FRAMES, streams, patch_part)
        .transpose(0, 2, 1, 3)
        .reshape(seq_count, streams, visual_rows)
    )
    visible = (
        jnp.concatenate(
            [visible, jnp.ones((seq_count, streams, extra_rows), jnp.int32)], axis=2
        ).reshape(seq_count, all_rows)
        == 1
    )
    allowed = (
        (query_episode[:, :, None] == key_episode[:, None, :])
        & (key_frames[None, None, :] <= query_frames[None, :, None])
        & visible[:, None, :]
    )
    cosine_table, sine_table = rotary_tables(
        query_times.reshape(-1).astype(jnp.float32),
        jnp.tile(query_grid_rows, seq_count).astype(jnp.float32),
        jnp.tile(query_grid_cols, seq_count).astype(jnp.float32),
        HEAD_DIM // 2,
    )
    gain_one = ln1_gain.astype(jnp.float32)
    shift_one = ln1_bias.astype(jnp.float32)
    gain_two = ln2_gain.astype(jnp.float32)
    shift_two = ln2_bias.astype(jnp.float32)
    normed_one = layer_norm(inputs, gain_one, shift_one).astype(jnp.bfloat16)
    projected = jnp.dot(normed_one, w_qkv, preferred_element_type=jnp.float32) + b_qkv.astype(
        jnp.float32
    )
    queries = (
        rotate(projected[:, :D].reshape(-1, HEADS, HEAD_DIM), cosine_table, sine_table)
        .astype(jnp.bfloat16)
        .reshape(seq_count, local_rows, D)
    )
    keys_own = (
        rotate(projected[:, D : 2 * D].reshape(-1, HEADS, HEAD_DIM), cosine_table, sine_table)
        .astype(jnp.bfloat16)
        .reshape(seq_count, local_rows, D)
    )
    values_own = projected[:, 2 * D :].astype(jnp.bfloat16).reshape(seq_count, local_rows, D)
    keys_all, values_all = (
        lax.all_gather(keys_own, "stream", axis=1, tiled=True),
        lax.all_gather(values_own, "stream", axis=1, tiled=True),
    )

    def head_slice(array, head_id):
        return lax.dynamic_slice_in_dim(array, head_id * HEAD_DIM, HEAD_DIM, 2)

    def masked_scores(query_head, key_head):
        scores = (
            jnp.einsum("sqd,skd->sqk", query_head, key_head, preferred_element_type=jnp.float32)
            * score_scale
        )
        return jnp.where(allowed, scores, -1e30)

    def attend_forward(head_id):
        value_head = head_slice(values_all, head_id)
        scores = masked_scores(head_slice(queries, head_id), head_slice(keys_all, head_id))
        row_max = jnp.max(scores, axis=-1, keepdims=True)
        shifted = jnp.exp(scores - row_max)
        row_total = jnp.sum(shifted, axis=-1, keepdims=True)
        full_weights = shifted / row_total
        attention_weights = full_weights.astype(jnp.bfloat16)
        blended = jnp.einsum(
            "sqk,skd->sqd", attention_weights, value_head, preferred_element_type=jnp.float32
        )
        log_total = (row_max + jnp.log(row_total))[..., 0]
        return (blended, log_total)

    forward_heads = lax.map(attend_forward, jnp.arange(HEADS, dtype=jnp.int32))
    head_blended = forward_heads[0]
    head_log_total = forward_heads[1]
    attended = (
        head_blended.transpose(1, 2, 0, 3).reshape(seq_count * local_rows, D).astype(jnp.bfloat16)
    )
    residual = (
        inputs
        + jnp.dot(attended, w_proj, preferred_element_type=jnp.float32)
        + b_proj.astype(jnp.float32)
    )
    normed_two = layer_norm(residual, gain_two, shift_two).astype(jnp.bfloat16)
    hidden_pre = jnp.dot(normed_two, w_in, preferred_element_type=jnp.float32) + b_in.astype(
        jnp.float32
    )
    hidden = exact_gelu(hidden_pre).astype(jnp.bfloat16)
    output = (
        residual
        + jnp.dot(hidden, w_out, preferred_element_type=jnp.float32)
        + b_out.astype(jnp.float32)
    )
    output = output.reshape(seq_count, local_rows, D)
    out_visual = output[:, :visual_rows].reshape(visual.shape).astype(jnp.bfloat16)
    out_conditioning = output[:, visual_rows:].reshape(conditioning.shape).astype(jnp.bfloat16)
    grad_output = (
        jnp.concatenate(
            [
                d_visual.reshape(seq_count, visual_rows, D),
                d_conditioning.reshape(seq_count, extra_rows, D),
            ],
            axis=1,
        )
        .astype(jnp.float32)
        .reshape(seq_count * local_rows, D)
    )
    grad_mlp = grad_output.astype(jnp.bfloat16)
    grad_w_out = jnp.einsum("rh,rd->hd", hidden, grad_mlp, preferred_element_type=jnp.float32)
    grad_b_out = jnp.sum(grad_mlp, axis=0, dtype=jnp.float32)
    grad_hidden = jnp.einsum("rd,hd->rh", grad_mlp, w_out, preferred_element_type=jnp.float32)
    gelu_back = jax.vjp(exact_gelu, hidden_pre)[1]
    grad_pre = gelu_back(grad_hidden)[0].astype(jnp.bfloat16)
    grad_w_in = jnp.einsum("rd,rh->dh", normed_two, grad_pre, preferred_element_type=jnp.float32)
    grad_b_in = jnp.sum(grad_pre, axis=0, dtype=jnp.float32)
    grad_normed_two = jnp.einsum("rh,dh->rd", grad_pre, w_in, preferred_element_type=jnp.float32)
    norm_two_back = jax.vjp(layer_norm, residual, gain_two, shift_two)[1]
    grad_res_part, grad_ln2_gain, grad_ln2_bias = norm_two_back(grad_normed_two)
    grad_residual = grad_output + grad_res_part
    grad_branch = grad_residual.astype(jnp.bfloat16)
    grad_w_proj = jnp.einsum("rd,re->de", attended, grad_branch, preferred_element_type=jnp.float32)
    grad_b_proj = jnp.sum(grad_branch, axis=0, dtype=jnp.float32)
    grad_attended = (
        jnp.einsum("re,de->rd", grad_branch, w_proj, preferred_element_type=jnp.float32)
        .astype(jnp.bfloat16)
        .reshape(seq_count, local_rows, D)
    )
    keys_back, values_back = (
        lax.all_gather(keys_own, "stream", axis=1, tiled=True),
        lax.all_gather(values_own, "stream", axis=1, tiled=True),
    )

    def attend_backward(head_id):
        query_head = head_slice(queries, head_id)
        key_head = head_slice(keys_back, head_id)
        value_head = head_slice(values_back, head_id)
        grad_head = head_slice(grad_attended, head_id)
        scores = masked_scores(query_head, key_head)
        log_total = lax.dynamic_index_in_dim(head_log_total, head_id, 0, keepdims=False)
        weights_full = jnp.exp(scores - log_total[..., None])
        grad_weights = jnp.einsum(
            "sqd,skd->sqk", grad_head, value_head, preferred_element_type=jnp.float32
        )
        inner = jnp.sum(grad_weights * weights_full, axis=-1, keepdims=True)
        grad_scores = (weights_full * (grad_weights - inner)).astype(jnp.bfloat16)
        grad_query = (
            jnp.einsum("sqk,skd->sqd", grad_scores, key_head, preferred_element_type=jnp.float32)
            * score_scale
        )
        grad_key = (
            jnp.einsum("sqk,sqd->skd", grad_scores, query_head, preferred_element_type=jnp.float32)
            * score_scale
        )
        grad_value = jnp.einsum(
            "sqk,sqd->skd",
            weights_full.astype(jnp.bfloat16),
            grad_head,
            preferred_element_type=jnp.float32,
        )
        return (grad_query, grad_key, grad_value)

    head_grad_query, head_grad_key, head_grad_value = lax.map(
        attend_backward, jnp.arange(HEADS, dtype=jnp.int32)
    )
    grad_key_all = head_grad_key.transpose(1, 2, 0, 3).reshape(seq_count, all_rows, D)
    grad_value_all = head_grad_value.transpose(1, 2, 0, 3).reshape(seq_count, all_rows, D)
    own_grad_keys, own_grad_values = (
        lax.psum_scatter(
            grad_key_all.astype(jnp.bfloat16), "stream", scatter_dimension=1, tiled=True
        ).astype(jnp.float32),
        lax.psum_scatter(
            grad_value_all.astype(jnp.bfloat16), "stream", scatter_dimension=1, tiled=True
        ).astype(jnp.float32),
    )
    own_grad_queries = head_grad_query.transpose(1, 2, 0, 3).reshape(seq_count, local_rows, D)
    grad_query_lin = (
        rotate(own_grad_queries.reshape(-1, HEADS, HEAD_DIM), cosine_table, -sine_table)
        .reshape(-1, D)
        .astype(jnp.bfloat16)
    )
    grad_key_lin = (
        rotate(own_grad_keys.reshape(-1, HEADS, HEAD_DIM), cosine_table, -sine_table)
        .reshape(-1, D)
        .astype(jnp.bfloat16)
    )
    grad_value_lin = own_grad_values.reshape(-1, D).astype(jnp.bfloat16)
    grad_projected = jnp.concatenate([grad_query_lin, grad_key_lin, grad_value_lin], axis=1)
    grad_w_qkv = jnp.einsum(
        "rd,re->de", normed_one, grad_projected, preferred_element_type=jnp.float32
    )
    grad_b_qkv = jnp.sum(grad_projected, axis=0, dtype=jnp.float32)
    grad_b_query_key = grad_b_qkv[: 2 * D]
    grad_b_value = grad_b_qkv[2 * D :]
    grad_normed_one = jnp.einsum(
        "re,de->rd", grad_projected, w_qkv, preferred_element_type=jnp.float32
    )
    norm_one_back = jax.vjp(layer_norm, inputs, gain_one, shift_one)[1]
    grad_in_part, grad_ln1_gain, grad_ln1_bias = norm_one_back(grad_normed_one)
    grad_inputs = (grad_residual + grad_in_part).reshape(seq_count, local_rows, D)
    grad_visual = grad_inputs[:, :visual_rows].reshape(visual.shape)
    grad_conditioning = grad_inputs[:, visual_rows:].reshape(conditioning.shape)
    summed = tuple(
        (
            lax.psum_scatter(grad_ln1_gain, ("dp", "stream"), scatter_dimension=0, tiled=True),
            lax.psum_scatter(grad_ln1_bias, ("dp", "stream"), scatter_dimension=0, tiled=True),
            lax.psum_scatter(grad_w_qkv, ("dp", "stream"), scatter_dimension=0, tiled=True),
            lax.psum_scatter(grad_b_query_key, ("dp", "stream"), scatter_dimension=0, tiled=True),
            lax.psum_scatter(grad_b_value, ("dp", "stream"), scatter_dimension=0, tiled=True),
            lax.psum_scatter(grad_w_proj, ("dp", "stream"), scatter_dimension=0, tiled=True),
            lax.psum_scatter(grad_b_proj, ("dp", "stream"), scatter_dimension=0, tiled=True),
            lax.psum_scatter(grad_ln2_gain, ("dp", "stream"), scatter_dimension=0, tiled=True),
            lax.psum_scatter(grad_ln2_bias, ("dp", "stream"), scatter_dimension=0, tiled=True),
            lax.psum_scatter(grad_w_in, ("dp", "stream"), scatter_dimension=0, tiled=True),
            lax.psum_scatter(grad_b_in, ("dp", "stream"), scatter_dimension=0, tiled=True),
            lax.psum_scatter(grad_w_out, ("dp", "stream"), scatter_dimension=0, tiled=True),
            lax.psum_scatter(grad_b_out, ("dp", "stream"), scatter_dimension=0, tiled=True),
        )
    )
    return (out_visual, out_conditioning, grad_visual, grad_conditioning) + summed


def solution(mesh):
    in_specs = (
        P("dp", None, "stream", None),
        P("dp", "stream", None, None),
        P("dp", None, "stream", None),
        P("dp", "stream", None, None),
        P("dp", None),
        P("dp", None, None),
        P(),
        P(),
        P(),
        P(),
        P(),
        P(),
        P(),
        P(),
        P(),
        P(),
        P(),
        P(),
    )
    out_specs = (
        P("dp", None, "stream", None),
        P("dp", "stream", None, None),
        P("dp", None, "stream", None),
        P("dp", "stream", None, None),
        P(("dp", "stream")),
        P(("dp", "stream")),
        P(("dp", "stream"), None),
        P(("dp", "stream")),
        P(("dp", "stream")),
        P(("dp", "stream"), None),
        P(("dp", "stream")),
        P(("dp", "stream")),
        P(("dp", "stream")),
        P(("dp", "stream"), None),
        P(("dp", "stream")),
        P(("dp", "stream"), None),
        P(("dp", "stream")),
    )
    return jax.shard_map(
        per_device, mesh=mesh, in_specs=in_specs, out_specs=out_specs, check_vma=False
    )
```

profile of v0, /device:TPU:0, one launch (start us, length us, event | category | flops | bytes accessed | tf_op | source)
XLA Modules:
  0.0 2092.6 jit_solution(15565116261466081727)
XLA Ops:
  12.0 6.2 convolution_add_fusion
  38.7 9.8 subtract_convert_fusion.2
  56.6 6.2 copy.57
  66.2 5.9 pad_maximum_fusion.1
  80.8 135.7 %all-gather.5.cloned.1.call-done = bf16[1,2064,1024]{2,0,1:T(2,128)(2,1)} async-done(((bf16[1,516,1024]{2,0,1:T(2,128)(2,1)}), bf16[1,2064,1024]{2,0,1:T(2,128)(2,1)}) %all-gather.5.cloned.1.call-update) | async-done | bytes 4227088 | tf_op jit(solution)/shard_map/all_gather | solution.py:167
  216.5 7.1 copy.60
  223.5 74.6 %all-gather.7.cloned.1.call-done = bf16[4,516,1024]{2,1,0:T(8,128)(2,1)} async-done(((bf16[1,516,1024]{2,1,0:T(8,128)(2,1)}), bf16[4,516,1024]{2,1,0:T(8,128)(2,1)}) %all-gather.7.cloned.1.call-update) | async-done | bytes 4227088 | tf_op jit(solution)/shard_map/all_gather | solution.py:168
  302.2 125.8 %while.30 = (s32[]{:T(128)}, bf16[16,1,516,64]{2,3,1,0:T(8,128)(2,1)}, f32[16,1,516]{2,1,0:T(1,128)S(1)}, s32[16]{0:T(128)S(1)}, bf16[1,516,1024]{2,1,0:T(8,128)...) while((s32[]{:T(128)}, ...), condition=%wide.region_9.10_spmd.clone.clone, body=%wide.region_6.9_spmd.clone.sunk.clone | while | flops 285425920 | bytes 14181615 | solution.py:195
  431.2 29.1 %multiply_convert_fusion.1 = (bf16[516,4096]{1,0:T(8,128)(2,1)}, f32[516,4096]{1,0:T(8,128)}, f32[516,4096]{1,0:T(8,128)}) fusion(f32[4096]{0:T(1024)S(1)} %convert_element_type.251, bf16[1024,4096]{1,0:T(8,128)(2,1)} %param.36, f32[516,1024]{1,0:T(8,128)S(1)} %get-tuple-element.377, f32[1024]{0:T(1024)S(1)} %convert_element_type.249, ...), kind=kOutput, calls=%fused_computation.60 | convolution fusion | flops 4470657024 | bytes 31666208 | tf_op jit(solution)/shard_map/dot_general | solution.py:207
  460.2 14.3 convert_reduce_fusion
  474.5 10.3 multiply_reduce_fusion.1
  488.3 247.8 %while.31 = (s32[]{:T(128)}, f32[16,1,516,64]{2,3,1,0:T(8,128)}, bf16[16,1,2064,64]{2,3,1,0:T(8,128)(2,1)}, bf16[16,1,2064,64]{2,3,1,0:T(8,128)(2,1)}, s32[16]{0...) while((s32[]{:T(128)}, f32[16,1,516,64]{2,3,1,0:T(8,128)}, ...), condition=%wide.region_16.17_spmd.clone.clone, body=%wide.region_14.16_spmd.clone.sunk.clone | while | flops 695625280 | bytes 35915128 | solution.py:284
  749.2 294.1 %all-reduce.16.cloned.1.call-done = (bf16[1,2064,1024]{1,2,0:T(8,128)(2,1)}, bf16[1,2064,1024]{1,2,0:T(8,128)(2,1)}) async-done(((bf16[1,2064,1024]{1,2,0:T(8,128)(2,1)}, bf16[1,2064,1024]{1,2,0:T(8,128)(2,1)}), (bf16[1,2064,1024]{1,2,0:T(8,128)(2,1)}, bf16[1,2064,1024]{1,2,0:T(8,128)(2,1)})) %all-reduce.16.cloned.1.call-update) | async-done | bytes 8454160
  1051.0 9.7 subtract_convert_fusion.1
  1064.9 5.8 pad_maximum_fusion.4
  1078.4 11.4 fusion.101
  1089.9 13.1 fusion.106
  1104.2 12.7 fusion.99
  1117.6 9.8 fusion.65
  1131.7 7.4 fusion.108
  1144.0 41.0 %all-reduce.12 = (f32[1024]{0:T(1024)S(1)}, f32[1024]{0:T(1024)S(1)}, f32[2048]{0:T(1024)S(1)}, f32[1024]{0:T(1024)S(1)}, f32[1024]{0:T(1024)S(1)}, /*index=5*/f...) all-reduce(f32[1024]{0:T(1024)S(1)} %get-tuple-element.275, ...), channel_id=5, replica_groups=mesh['dp'=8,'stream'=4] {'dp','stream'}, use_global_device_ids=true, to_apply=%region_22.23.clone | all-reduce | flops 13312 | bytes 106496
  1193.9 160.1 %reduce-scatter.7.cloned.1.call-done = f32[32,3072]{1,0:T(8,128)} async-done(((f32[1024,3072]{1,0:T(8,128)}), f32[32,3072]{1,0:T(8,128)}) %reduce-scatter.7.cloned.1.call-update) | async-done | bytes 393232 | tf_op jit(solution)/shard_map/reduce_scatter | solution.py:328
  1354.0 366.2 %reduce-scatter.11.cloned.1.call-done = f32[32,4096]{1,0:T(8,128)} async-done(((f32[1024,4096]{1,0:T(8,128)}), f32[32,4096]{1,0:T(8,128)}) %reduce-scatter.11.cloned.1.call-update) | async-done | bytes 524304 | tf_op jit(solution)/shard_map/reduce_scatter | solution.py:335
  1720.2 365.2 %reduce-scatter.13.cloned.1.call-done = f32[128,1024]{1,0:T(8,128)} async-done(((f32[4096,1024]{1,0:T(8,128)}), f32[128,1024]{1,0:T(8,128)}) %reduce-scatter.13.cloned.1.call-update) | async-done | bytes 524304 | tf_op jit(solution)/shard_map/reduce_scatter | solution.py:337
  (435 shorter events, 428.4 us)
Async XLA Ops:
  7.2 420.8 %copy-start = (bf16[1024,1024]{1,0:T(8,128)(2,1)S(1)}, bf16[1024,1024]{1,0:T(8,128)(2,1)}, u32[]{:S(2)}) copy-start(bf16[1024,1024]{1,0:T(8,128)(2,1)} %param.32) | copy-start | bytes 6291460
  7.2 209.2 %all-gather.5.cloned.1.call-start = ((), (), s32[]{:S(2)}) async-start(), calls=%async_computation.4 | async-start | bytes 10567680 | tf_op jit(solution)/shard_map/all_gather | solution.py:167
  8.2 419.8 %copy-start.19 = (bf16[4,1024]{1,0:T(4,128)(2,1)}, bf16[4,1024]{1,0:T(4,128)(2,1)S(1)}, u32[]{:S(2)}) copy-start(bf16[4,1024]{1,0:T(4,128)(2,1)S(1)} %concatenate.27) | copy-start | bytes 24580
  9.7 8.5 copy-start.21
  38.6 9.8 copy-start.16
  62.9 235.2 %all-gather.7.cloned.1.call-start = ((), (), s32[]{:S(2)}) async-start(), calls=%async_computation.9 | async-start | bytes 5324800 | tf_op jit(solution)/shard_map/all_gather | solution.py:168
  65.7 977.5 %all-reduce.16.cloned.1.call-start = ((), (), s32[]{:S(2)}) async-start(), calls=%async_computation.10 | async-start | bytes 17825792
  72.1 7.3 copy-start.36
  430.8 54.0 %copy-start.6 = (f32[516,1024]{1,0:T(8,128)}, f32[516,1024]{1,0:T(8,128)S(1)}, u32[]{:S(2)}) copy-start(f32[516,1024]{1,0:T(8,128)S(1)} %get-tuple-element.377) | copy-start | bytes 6340612
  431.2 29.1 %copy-start.12 = (bf16[1,8,64,1024]{3,2,1,0:T(8,128)(2,1)S(1)}, bf16[1,8,64,1024]{3,2,1,0:T(8,128)(2,1)}, u32[]{:S(2)}) copy-start(bf16[1,8,64,1024]{3,2,1,0:T(8,128)(2,1)} %param.24) | copy-start | bytes 3145732
  474.5 10.3 copy-start.50
  736.1 457.8 %reduce-scatter.9.cloned.1.call-start = ((), (), s32[]{:S(2)}) async-start(), calls=%async_computation.6 | async-start | bytes 4325376 | tf_op jit(solution)/shard_map/reduce_scatter | solution.py:331
  742.5 611.5 %reduce-scatter.7.cloned.1.call-start = ((), (), s32[]{:S(2)}) async-start(), calls=%async_computation.5 | async-start | bytes 12976128 | tf_op jit(solution)/shard_map/reduce_scatter | solution.py:328
  1070.7 7.6 copy-start.5
  1070.7 7.6 copy-start.20
  1070.7 7.6 copy-start.22
  1070.7 7.6 copy-start.25
  1070.7 7.6 copy-start.27
  1070.7 7.6 copy-start.39
  1089.8 630.4 %reduce-scatter.11.cloned.1.call-start = ((), (), s32[]{:S(2)}) async-start(), calls=%async_computation.7 | async-start | bytes 17301504 | tf_op jit(solution)/shard_map/reduce_scatter | solution.py:335
  1103.0 982.4 %reduce-scatter.13.cloned.1.call-start = ((), (), s32[]{:S(2)}) async-start(), calls=%async_computation.8 | async-start | bytes 17301504 | tf_op jit(solution)/shard_map/reduce_scatter | solution.py:337
  1131.7 7.5 copy-start.23
  1131.7 7.5 copy-start.29
  1142.5 942.9 %copy-start.1 = (bf16[1024,1024]{1,0:T(8,128)(2,1)S(1)}, bf16[1024,1024]{1,0:T(8,128)(2,1)}, u32[]{:S(2)}) copy-start(bf16[1024,1024]{1,0:T(8,128)(2,1)} %param.32) | copy-start | bytes 6291460
  (36 other events, 121.4 us)
Sparse Core Ops, SparseCore 0:
  63.0 153.3 all-gather.4
  218.0 80.0 all-gather.6
  736.2 306.9 all-reduce.15
  1045.9 147.9 reduce-scatter.8
  1200.4 153.6 reduce-scatter.6
  1356.9 363.2 reduce-scatter.10
  1723.2 362.1 reduce-scatter.12
where the time goes:
time: 2110 us; the launch traced here: 2090 us
  waiting for transfers between devices  1400 us (66%)
  matrix products  399 us (19%)
  local copies, waits for them, and re-layouts  103 us (5%)
  other arithmetic  81.3 us (4%)
  loops' own time  52.7 us (2%)
  blocking collectives  41 us (2%)
    reduce_scatter x1, waiting for transfers between devices, per_device(): lax.psum_scatter(grad_w_in, ('dp', 'stream'), scatter_dimension=0, tiled=...  366 us
    reduce_scatter x1, waiting for transfers between devices, per_device(): lax.psum_scatter(grad_w_out, ('dp', 'stream'), scatter_dimension=0, tiled...  365 us
    unnamed x8, waiting for transfers between devices  294 us
    reduce_scatter x1, waiting for transfers between devices, per_device(): lax.psum_scatter(grad_w_qkv, ('dp', 'stream'), scatter_dimension=0, tiled...  160 us
    all_gather x1, waiting for transfers between devices, per_device(): lax.all_gather(keys_own, 'stream', axis=1, tiled=True)  136 us
    dot_general x32, matrix products, masked_scores(): jnp.einsum('sqd,skd->sqk', query_head, key_head, preferred_element_type=j...  94.6 us
    all_gather x1, waiting for transfers between devices, per_device(): lax.all_gather(values_own, 'stream', axis=1, tiled=True)  74.6 us
    dot_general x16, matrix products, attend_forward(): jnp.einsum('sqk,skd->sqd', attention_weights, value_head, preferred_eleme...  47.1 us
  transfers between devices with their start and end apart: 7, of which 7 were waited for; matrix products, arithmetic and copies ran while one was open for 7% of the time, Pallas kernels for 0%

commit v1 on v0

v1 whole, which is shorter than its diff:
```python
import functools
import math

import jax
import jax.numpy as jnp
import numpy as np
from jax import lax
from jax.experimental import pallas as pl
from jax.experimental.pallas import tpu as pltpu
from jax.sharding import PartitionSpec as P

D = 1024
HEADS = 16
HEAD_DIM = 64
GRID = 16
COND = 2
FRAMES = 8
MOST = 5
MIDDLE = 7
STREAMS = 4
GROUP = 4
GW = GROUP * HEAD_DIM
PART = 64
PATCHES = 256
VIS = FRAMES * PART
CROWS = 16
ROWS = VIS + CROWS
WIDE = GROUP * 128
NEG = -1e30
EPS = 1e-06
F32 = jnp.float32
BF16 = jnp.bfloat16
VM = pltpu.VMEM
FULL = pl.BlockSpec(memory_space=pltpu.VMEM)
ANYM = pl.BlockSpec(memory_space=pltpu.HBM)
LIMIT = 60 * 1024 * 1024


def nn(a, b):
    return lax.dot_general(a, b, (((1,), (0,)), ((), ())), preferred_element_type=F32)


def nt(a, b):
    return lax.dot_general(a, b, (((1,), (1,)), ((), ())), preferred_element_type=F32)


def rope_constants():
    pair = np.arange(HEAD_DIM // 2)
    exponent = np.where(pair < 30, (pair % 10) / 10.0, 0.0).astype(np.float32)
    freq = np.exp(-math.log(10000.0) * exponent).astype(np.float32)
    patch = np.arange(PATCHES)
    slot_time = np.array([0, 1, 2, 3, 4, 0, 1, 0])
    is_time = (pair < 10)[None, :]
    place = np.where(
        (pair >= 20)[None, :], (patch % GRID)[:, None], (patch // GRID)[:, None]
    ) * ((pair >= 10) & (pair < 30))[None, :]
    angle_patch = (place * freq[None, :]).astype(np.float32)
    angle_time = (slot_time[:, None] * freq[None, :]).astype(np.float32)
    cos_patch = np.where(is_time, 0.0, np.cos(angle_patch))
    sin_patch = np.where(is_time, 0.0, np.sin(angle_patch))
    cos_time = np.where(is_time, np.cos(angle_time), 0.0)
    sin_time = np.where(is_time, np.sin(angle_time), 0.0)

    def spread(table, signed):
        two = np.repeat(table, 2, axis=1)
        if signed:
            two = two * np.where(np.arange(HEAD_DIM) % 2 == 0, -1.0, 1.0)[None, :]
        return np.tile(two, (1, GROUP)).astype(np.float32)

    return (
        spread(cos_patch, False),
        spread(sin_patch, True),
        spread(cos_time, False),
        spread(sin_time, True),
    )


def swap_pairs(v):
    lane = lax.broadcasted_iota(jnp.int32, v.shape, 1)
    width = v.shape[1]
    return jnp.where(lane % 2 == 0, pltpu.roll(v, width - 1, 1), pltpu.roll(v, 1, 1))


def turn(v, cosine, sine):
    return v * cosine + swap_pairs(v) * sine


def pad_heads(t, extra):
    pieces = []
    for h in range(GROUP):
        pieces += [t[:, h * HEAD_DIM : (h + 1) * HEAD_DIM], extra]
    return jnp.concatenate(pieces, axis=1)


def unpad_heads(t):
    return jnp.concatenate([t[:, h * 128 : h * 128 + HEAD_DIM] for h in range(GROUP)], axis=1)


def head(t, h):
    return t[:, h * 128 : (h + 1) * 128]


def first_slot(i):
    return jnp.where(i < MOST, 0, jnp.where(i < MIDDLE, MOST, MIDDLE))


def cond_tables(cs_col, ct, st):
    cosine = jnp.zeros((PART, GW), F32)
    sine = jnp.zeros((PART, GW), F32)
    for j in range(FRAMES):
        here = cs_col == j
        cosine = cosine + jnp.where(here, ct[j : j + 1, :], 0.0)
        sine = sine + jnp.where(here, st[j : j + 1, :], 0.0)
    lane = lax.broadcasted_iota(jnp.int32, (PART, GW), 1) % HEAD_DIM
    return jnp.where(lane < 20, cosine, 1.0), sine


def forward_kernel(
    perm, x_ref, wq_ref, wk_ref, wv_ref, bq_ref, bk_ref, bv_ref, g_ref, b_ref,
    cg_ref, sg_ref, ct_ref, st_ref, bias_ref, csc_ref, csr_ref,
    a_ref, q_ref, k_ref, v_ref, qc_ref, kc_ref, vc_ref, lse_ref, lsec_ref, o_ref,
    vt_ref,
):
    gain, shift = g_ref[...], b_ref[...]
    bq, bk, bv = bq_ref[...], bk_ref[...], bv_ref[...]
    cs_col, cs_row = csc_ref[...], csr_ref[...]
    bias_t = jnp.transpose(bias_ref[...])
    col_id = lax.broadcasted_iota(jnp.int32, (PATCHES, FRAMES), 1)

    def project(x, cosine, sine):
        x = x.astype(F32)
        centre = x - jnp.mean(x, axis=1, keepdims=True)
        spread = jnp.mean(centre * centre, axis=1, keepdims=True)
        a = (centre * lax.rsqrt(spread + EPS) * gain + shift).astype(BF16)
        q = turn(nn(a, wq_ref[...]) + bq, cosine, sine)
        k = turn(nn(a, wk_ref[...]) + bk, cosine, sine)
        v = nn(a, wv_ref[...]) + bv
        return a, (q.astype(BF16).astype(F32) * 0.125).astype(BF16), k.astype(BF16), v

    def lanes(rows):
        return lax.broadcasted_iota(jnp.int32, (rows, 64), 1)

    xc = x_ref[:, VIS:, :].reshape(PART, D)
    a, q, k, v = project(xc, *cond_tables(cs_col, ct_ref[...], st_ref[...]))
    a_ref[:, VIS:, :] = a.reshape(STREAMS, CROWS, D)
    one = jnp.where(lanes(PART) == 0, 1.0, 0.0).astype(BF16)
    zero = jnp.zeros((PART, 64), BF16)
    qc_ref[...] = pad_heads(q, one)
    kc_ref[...] = pad_heads(k, zero)
    vc_ref[...] = pad_heads(v.astype(BF16), zero)
    vct = jnp.transpose(v).astype(BF16)

    def slot(i, carry):
        f = perm[i]
        start = pl.multiple_of(f * PART, PART)
        x = x_ref[:, pl.ds(start, PART), :].reshape(PATCHES, D)
        cosine = cg_ref[...] + ct_ref[pl.ds(i, 1), :]
        sine = sg_ref[...] + st_ref[pl.ds(i, 1), :]
        a, q, k, v = project(x, cosine, sine)
        a_ref[:, pl.ds(start, PART), :] = a.reshape(STREAMS, PART, D)
        lane = lanes(PATCHES)
        bias = jnp.sum(jnp.where(col_id == f, bias_t, 0.0), axis=1, keepdims=True)
        q_ref[i] = pad_heads(q, jnp.where(lane == 0, 1.0, 0.0).astype(BF16))
        k_ref[i] = pad_heads(k, jnp.where(lane == 0, bias, 0.0).astype(BF16))
        v_ref[i] = pad_heads(v.astype(BF16), jnp.zeros((PATCHES, 64), BF16))
        vt_ref[i] = jnp.transpose(v).astype(BF16)
        lo = first_slot(i)
        near = (cs_col >= lo) & (cs_col <= i)
        tops, totals, blends = [], [], []
        for h in range(GROUP):
            s = jnp.where(near, nt(head(kc_ref, h), head(q_ref[i], h)), NEG)
            top = jnp.max(s, axis=0, keepdims=True)
            p = jnp.exp(s - top)
            tops.append(top)
            totals.append(jnp.sum(p, axis=0, keepdims=True))
            blends.append(nn(vct[h * HEAD_DIM : (h + 1) * HEAD_DIM], p.astype(BF16)))

        def step(j, state):
            tops, totals, blends = state
            new = ([], [], [])
            for h in range(GROUP):
                s = nt(k_ref[j, :, h * 128 : (h + 1) * 128], q_ref[i, :, h * 128 : (h + 1) * 128])
                top = jnp.maximum(tops[h], jnp.max(s, axis=0, keepdims=True))
                p = jnp.exp(s - top)
                keep = jnp.exp(tops[h] - top)
                new[0].append(top)
                new[1].append(totals[h] * keep + jnp.sum(p, axis=0, keepdims=True))
                vt = vt_ref[j, h * HEAD_DIM : (h + 1) * HEAD_DIM, :]
                new[2].append(blends[h] * keep + nn(vt, p.astype(BF16)))
            return new

        tops, totals, blends = lax.fori_loop(lo, i + 1, step, (tops, totals, blends))
        o = jnp.transpose(jnp.concatenate([blends[h] / totals[h] for h in range(GROUP)], axis=0))
        o_ref[:, pl.ds(start, PART), :] = o.astype(BF16).reshape(STREAMS, PART, GW)
        lse_ref[i] = jnp.concatenate([tops[h] + jnp.log(totals[h]) for h in range(GROUP)] * 2, axis=0)
        return carry

    lax.fori_loop(0, FRAMES, slot, 0)

    lo_col = first_slot(cs_col)
    near = (cs_row >= lo_col) & (cs_row <= cs_col)
    tops, totals, blends = [], [], []
    for h in range(GROUP):
        s = jnp.where(near, nt(head(qc_ref, h), head(kc_ref, h)), NEG)
        top = jnp.max(s, axis=1, keepdims=True)
        p = jnp.exp(s - top)
        tops.append(top)
        totals.append(jnp.sum(p, axis=1, keepdims=True))
        blends.append(nn(p.astype(BF16), head(vc_ref, h)))

    def cond_step(j, state):
        tops, totals, blends = state
        near = (lo_col <= j) & (cs_col >= j)
        new = ([], [], [])
        for h in range(GROUP):
            s = nt(head(qc_ref, h), k_ref[j, :, h * 128 : (h + 1) * 128])
            s = jnp.where(near, s, NEG)
            top = jnp.maximum(tops[h], jnp.max(s, axis=1, keepdims=True))
            p = jnp.exp(s - top)
            keep = jnp.exp(tops[h] - top)
            new[0].append(top)
            new[1].append(totals[h] * keep + jnp.sum(p, axis=1, keepdims=True))
            new[2].append(blends[h] * keep + nn(p.astype(BF16), v_ref[j, :, h * 128 : (h + 1) * 128]))
        return new

    tops, totals, blends = lax.fori_loop(0, FRAMES, cond_step, (tops, totals, blends))
    o = jnp.concatenate([(blends[h] / totals[h])[:, :HEAD_DIM] for h in range(GROUP)], axis=1)
    o_ref[:, VIS:, :] = o.astype(BF16).reshape(STREAMS, CROWS, GW)
    lane = lax.broadcasted_iota(jnp.int32, (PART, 128), 1)
    lsec = jnp.zeros((PART, 128), F32)
    for h in range(GROUP):
        lsec = lsec + jnp.where(lane == h, tops[h] + jnp.log(totals[h]), 0.0)
    lsec_ref[...] = lsec


def whole(shape):
    return pl.BlockSpec(shape, lambda i, s: (0,) * len(shape))


def attend_forward(scalars, x, w_qkv, b_qkv, gain, shift, tables, bias, cs_col, cs_row):
    def weight(part):
        return pl.BlockSpec((D, GW), lambda i, s: (0, s[8] + part * GROUP))

    def offset(part):
        return pl.BlockSpec((1, GW), lambda i, s: (0, s[8] + part * GROUP))

    shapes = (
        ((STREAMS, ROWS, D), BF16),
        ((FRAMES, PATCHES, WIDE), BF16),
        ((FRAMES, PATCHES, WIDE), BF16),
        ((FRAMES, PATCHES, WIDE), BF16),
        ((PART, WIDE), BF16),
        ((PART, WIDE), BF16),
        ((PART, WIDE), BF16),
        ((FRAMES, 8, PATCHES), F32),
        ((PART, 128), F32),
        ((STREAMS, ROWS, GW), BF16),
    )
    ops = (x, w_qkv, w_qkv, w_qkv, b_qkv, b_qkv, b_qkv, gain, shift) + tables + (bias, cs_col, cs_row)
    specs = [whole(x.shape), weight(0), weight(1), weight(2), offset(0), offset(1), offset(2)]
    specs += [whole(t.shape) for t in ops[7:]]
    return pl.pallas_call(
        forward_kernel,
        name="attend_forward",
        out_shape=tuple(jax.ShapeDtypeStruct(s, t) for s, t in shapes),
        grid_spec=pltpu.PrefetchScalarGridSpec(
            num_scalar_prefetch=1,
            grid=(1,),
            in_specs=specs,
            out_specs=tuple(whole(s) for s, _ in shapes),
            scratch_shapes=[VM((FRAMES, GW, PATCHES), BF16)],
        ),
        compiler_params=pltpu.CompilerParams(vmem_limit_bytes=LIMIT),
        cost_estimate=pl.CostEstimate(flops=8 * 10**9, bytes_accessed=2 * 10**7, transcendentals=6 * 10**6),
    )(scalars, *ops)


def backward_kernel(
    perm, q_ref, k_ref, v_ref, qc_ref, kc_ref, vc_ref, lse_ref, lsec_ref, o_ref, do_ref,
    cg_ref, sg_ref, ct_ref, st_ref, csc_ref, csr_ref,
    g_ref, dk_ref, dv_ref, dkc_ref, dvc_ref, kt_ref,
):
    cs_col, cs_row = csc_ref[...], csr_ref[...]
    dk_ref[...] = jnp.zeros_like(dk_ref)
    dv_ref[...] = jnp.zeros_like(dv_ref)
    dkc_ref[...] = jnp.zeros_like(dkc_ref)
    dvc_ref[...] = jnp.zeros_like(dvc_ref)
    kct = jnp.transpose(unpad_heads(kc_ref[...].astype(F32))).astype(BF16)

    def slot(i, carry):
        f = perm[i]
        start = pl.multiple_of(f * PART, PART)
        do = do_ref[:, pl.ds(start, PART), :].reshape(PATCHES, GW)
        o = o_ref[:, pl.ds(start, PART), :].reshape(PATCHES, GW)
        prod = jnp.transpose(do.astype(F32) * o.astype(F32))
        deltas = [
            jnp.sum(prod[h * HEAD_DIM : (h + 1) * HEAD_DIM], axis=0, keepdims=True)
            for h in range(GROUP)
        ]
        dop = pad_heads(do, jnp.zeros((PATCHES, 64), BF16))
        kt_ref[i] = jnp.transpose(unpad_heads(k_ref[i].astype(F32))).astype(BF16)
        lo = first_slot(i)
        near = (cs_col >= lo) & (cs_col <= i)
        dqs = []
        for h in range(GROUP):
            cols = slice(h * 128, (h + 1) * 128)
            q = q_ref[i, :, cols]
            s = jnp.where(near, nt(kc_ref[:, cols], q), NEG)
            p = jnp.exp(s - lse_ref[i, h : h + 1, :])
            dp = nt(vc_ref[:, cols], dop[:, cols])
            ds = (p * (dp - deltas[h])).astype(BF16)
            dvc_ref[:, cols] += nn(p.astype(BF16), dop[:, cols])
            dkc_ref[:, cols] += nn(ds, q)
            dqs.append(nn(kct[h * HEAD_DIM : (h + 1) * HEAD_DIM], ds))

        def step(j, dqs):
            new = []
            for h in range(GROUP):
                cols = slice(h * 128, (h + 1) * 128)
                q = q_ref[i, :, cols]
                p = jnp.exp(nt(k_ref[j, :, cols], q) - lse_ref[i, h : h + 1, :])
                dp = nt(v_ref[j, :, cols], dop[:, cols])
                ds = (p * (dp - deltas[h])).astype(BF16)
                dv_ref[j, :, cols] += nn(p.astype(BF16), dop[:, cols])
                dk_ref[j, :, cols] += nn(ds, q)
                new.append(dqs[h] + nn(kt_ref[j, h * HEAD_DIM : (h + 1) * HEAD_DIM, :], ds))
            return new

        dqs = lax.fori_loop(lo, i + 1, step, dqs)
        dq = jnp.transpose(jnp.concatenate(dqs, axis=0)) * 0.125
        cosine = cg_ref[...] + ct_ref[pl.ds(i, 1), :]
        sine = sg_ref[...] + st_ref[pl.ds(i, 1), :]
        dq = turn(dq, cosine, -sine).astype(BF16).reshape(STREAMS, PART, GW)
        g_ref[:, pl.ds(start, PART), 0:GW] = dq
        return carry

    lax.fori_loop(0, FRAMES, slot, 0)

    doc = do_ref[:, VIS:, :].reshape(PART, GW)
    oc = o_ref[:, VIS:, :].reshape(PART, GW)
    docp = pad_heads(doc, jnp.zeros((PART, 64), BF16))
    prod = doc.astype(F32) * oc.astype(F32)
    lo_col = first_slot(cs_col)
    near = (cs_row >= lo_col) & (cs_row <= cs_col)
    deltas = [
        jnp.sum(prod[:, h * HEAD_DIM : (h + 1) * HEAD_DIM], axis=1, keepdims=True)
        for h in range(GROUP)
    ]
    lses = [lsec_ref[:, h : h + 1] for h in range(GROUP)]
    dqs = []
    for h in range(GROUP):
        cols = slice(h * 128, (h + 1) * 128)
        s = jnp.where(near, nt(qc_ref[:, cols], kc_ref[:, cols]), NEG)
        p = jnp.exp(s - lses[h])
        ds = p * (nt(docp[:, cols], vc_ref[:, cols]) - deltas[h])
        dvc_ref[:, cols] += nn(jnp.transpose(p).astype(BF16), docp[:, cols])
        dkc_ref[:, cols] += nn(jnp.transpose(ds).astype(BF16), qc_ref[:, cols])
        dqs.append(nn(ds.astype(BF16), kc_ref[:, cols]))

    def cond_step(j, dqs):
        near = (lo_col <= j) & (cs_col >= j)
        new = []
        for h in range(GROUP):
            cols = slice(h * 128, (h + 1) * 128)
            s = jnp.where(near, nt(qc_ref[:, cols], k_ref[j, :, cols]), NEG)
            p = jnp.exp(s - lses[h])
            ds = p * (nt(docp[:, cols], v_ref[j, :, cols]) - deltas[h])
            dv_ref[j, :, cols] += nn(jnp.transpose(p).astype(BF16), docp[:, cols])
            dk_ref[j, :, cols] += nn(jnp.transpose(ds).astype(BF16), qc_ref[:, cols])
            new.append(dqs[h] + nn(ds.astype(BF16), k_ref[j, :, cols]))
        return new

    dqs = lax.fori_loop(0, FRAMES, cond_step, dqs)
    cosine, sine = cond_tables(cs_col, ct_ref[...], st_ref[...])
    valid = cs_col < FRAMES
    dq = jnp.concatenate([t[:, :HEAD_DIM] for t in dqs], axis=1) * 0.125
    for part, t in ((0, turn(dq, cosine, -sine)), (1, turn(unpad_heads(dkc_ref[...]), cosine, -sine)), (2, unpad_heads(dvc_ref[...]))):
        t = jnp.where(valid, t, 0.0).astype(BF16)
        g_ref[:, VIS:, part * GW : (part + 1) * GW] = t.reshape(STREAMS, CROWS, GW)

    def finish(i, carry):
        start = pl.multiple_of(perm[i] * PART, PART)
        cosine = cg_ref[...] + ct_ref[pl.ds(i, 1), :]
        sine = sg_ref[...] + st_ref[pl.ds(i, 1), :]
        dk = turn(unpad_heads(dk_ref[i]), cosine, -sine)
        g_ref[:, pl.ds(start, PART), GW : 2 * GW] = dk.astype(BF16).reshape(STREAMS, PART, GW)
        dv = unpad_heads(dv_ref[i])
        g_ref[:, pl.ds(start, PART), 2 * GW :] = dv.astype(BF16).reshape(STREAMS, PART, GW)
        return carry

    lax.fori_loop(0, FRAMES, finish, 0)


def attend_backward(scalars, saved, o, do, tables, cs_col, cs_row):
    ops = tuple(saved) + (o, do) + tables + (cs_col, cs_row)
    out = (STREAMS, ROWS, 3 * GW)
    return pl.pallas_call(
        backward_kernel,
        name="attend_backward",
        out_shape=jax.ShapeDtypeStruct(out, BF16),
        grid_spec=pltpu.PrefetchScalarGridSpec(
            num_scalar_prefetch=1,
            grid=(1,),
            in_specs=[whole(t.shape) for t in ops],
            out_specs=whole(out),
            scratch_shapes=[
                VM((FRAMES, PATCHES, WIDE), F32),
                VM((FRAMES, PATCHES, WIDE), F32),
                VM((PART, WIDE), F32),
                VM((PART, WIDE), F32),
                VM((FRAMES, GW, PATCHES), BF16),
            ],
        ),
        compiler_params=pltpu.CompilerParams(vmem_limit_bytes=LIMIT),
        cost_estimate=pl.CostEstimate(flops=10**10, bytes_accessed=2 * 10**7, transcendentals=6 * 10**6),
    )(scalars, *ops)


def where_am_i():
    d, z = lax.axis_index("dp"), lax.axis_index("stream")
    return d // 2, d % 2, z // 2, z % 2, z


def greet_column():
    p, c, q, r, z = where_am_i()
    barrier = pltpu.get_barrier_semaphore()
    for core in range(2):
        for chip in range(STREAMS):
            @pl.when((core != c) | (chip != z))
            def _():
                pl.semaphore_signal(
                    barrier, inc=1, device_id=(2 * p + core, chip),
                    device_id_type=pl.DeviceIdType.MESH,
                )
    pl.semaphore_wait(barrier, 2 * STREAMS - 1)


def remote(src, dst, send, recv, device):
    return pltpu.make_async_remote_copy(
        src_ref=src, dst_ref=dst, send_sem=send, recv_sem=recv, device_id=device,
        device_id_type=pl.DeviceIdType.MESH,
    )


def comm_call(kernel, name, ident, outs, scratch, *ops):
    return pl.pallas_call(
        kernel,
        name=name,
        out_shape=tuple(jax.ShapeDtypeStruct(s, t) for s, t in outs),
        in_specs=[ANYM] * len(ops),
        out_specs=tuple(ANYM for _ in outs),
        scratch_shapes=scratch,
        compiler_params=pltpu.CompilerParams(
            collective_id=ident, has_side_effects=True, vmem_limit_bytes=LIMIT
        ),
    )(*ops)


def dma(*shape):
    return pltpu.SemaphoreType.DMA(shape)


HALF = VIS // 2


def gather_kernel(x_ref, m_ref, xa_ref, ma_ref, send, recv, csend, crecv, fsend, frecv, lsem, msem):
    p, c, q, r, z = where_am_i()
    greet_column()
    tail = pl.ds(VIS, CROWS)
    for core in range(2):
        rows = pl.ds(core * HALF, HALF)
        for side in range(2):
            n = core * 2 + side
            mine = (core == c) & (2 * c + side == z)
            device = (2 * p + core, 2 * c + side)

            @pl.when(mine)
            def _():
                pltpu.make_async_copy(x_ref.at[rows], xa_ref.at[z, rows], lsem.at[0]).start()
                pltpu.make_async_copy(x_ref.at[tail], xa_ref.at[z, tail], lsem.at[1]).start()

            @pl.when(jnp.logical_not(mine))
            def _():
                remote(x_ref.at[rows], xa_ref.at[z, rows], send.at[n], recv.at[z], device).start()
                remote(x_ref.at[tail], xa_ref.at[z, tail], csend.at[n], crecv.at[z], device).start()

    other = (2 * p + 1 - c, z)

    @pl.when(q == c)
    def _():
        remote(m_ref, ma_ref, msem.at[0], msem.at[1], other).start()
        pltpu.make_async_copy(m_ref, ma_ref, msem.at[2]).start()

    rows = pl.ds(c * HALF, HALF)
    for s in range(STREAMS):
        mine = (q == c) & (s == z)

        @pl.when(mine)
        def _():
            pltpu.make_async_copy(x_ref.at[rows], xa_ref.at[s, rows], lsem.at[0]).wait()
            pltpu.make_async_copy(x_ref.at[tail], xa_ref.at[s, tail], lsem.at[1]).wait()

        @pl.when(jnp.logical_not(mine))
        def _():
            remote(x_ref.at[rows], xa_ref.at[s, rows], send.at[0], recv.at[s], other).wait_recv()
            remote(x_ref.at[tail], xa_ref.at[s, tail], csend.at[0], crecv.at[s], other).wait_recv()

        remote(xa_ref.at[s, rows], xa_ref.at[s, rows], fsend.at[s], frecv.at[s], other).start()
    rest = pl.ds((1 - c) * HALF, HALF)
    for s in range(STREAMS):
        copy = remote(xa_ref.at[s, rest], xa_ref.at[s, rest], fsend.at[s], frecv.at[s], other)
        copy.wait_send()
        copy.wait_recv()
    for core in range(2):
        for side in range(2):
            n = core * 2 + side

            @pl.when((core != c) | (2 * c + side != z))
            def _():
                remote(x_ref.at[rows], xa_ref.at[0, rows], send.at[n], recv.at[0], other).wait_send()
                remote(x_ref.at[tail], xa_ref.at[0, tail], csend.at[n], crecv.at[0], other).wait_send()

    @pl.when(q == c)
    def _():
        remote(m_ref, ma_ref, msem.at[0], msem.at[1], other).wait_send()
        pltpu.make_async_copy(m_ref, ma_ref, msem.at[2]).wait()

    @pl.when(q != c)
    def _():
        remote(m_ref, ma_ref, msem.at[0], msem.at[1], other).wait_recv()


def gather_rows(x, meta):
    return comm_call(
        gather_kernel, "gather_rows", 0,
        (((STREAMS, ROWS, D), BF16), (meta.shape, F32)),
        [dma(4), dma(4), dma(4), dma(4), dma(4), dma(4), dma(2), dma(3)],
        x, meta,
    )


def to_owner_kernel(o_ref, out_ref, send, recv, lsem):
    p, c, q, r, z = where_am_i()
    greet_column()
    group = 2 * r + c
    place = pl.ds(pl.multiple_of(group * GW, GW), GW)
    for s in range(STREAMS):
        mine = (q == c) & (s == z)

        @pl.when(mine)
        def _():
            pltpu.make_async_copy(o_ref.at[s], out_ref.at[:, place], lsem).start()

        @pl.when(jnp.logical_not(mine))
        def _():
            remote(o_ref.at[s], out_ref.at[:, place], send.at[s], recv.at[group], (2 * p + q, s)).start()
    for s in range(STREAMS):
        mine = (q == c) & (s == z)

        @pl.when(mine)
        def _():
            pltpu.make_async_copy(o_ref.at[s], out_ref.at[:, place], lsem).wait()

        @pl.when(jnp.logical_not(mine))
        def _():
            remote(o_ref.at[s], out_ref.at[:, place], send.at[s], recv.at[group], (2 * p + q, s)).wait_send()
    for side in range(2):
        for core in range(2):
            g = 2 * side + core

            @pl.when((core != c) | (2 * c + side != z))
            def _():
                cols = pl.ds(g * GW, GW)
                remote(o_ref.at[0], out_ref.at[:, cols], send.at[0], recv.at[g], (2 * p + q, 0)).wait_recv()


def to_owner(o):
    return comm_call(
        to_owner_kernel, "to_owner", 1, (((ROWS, D), BF16),), [dma(4), dma(4), pltpu.SemaphoreType.DMA], o
    )[0]


def to_heads_kernel(d_ref, out_ref, send, recv, lsem):
    p, c, q, r, z = where_am_i()
    greet_column()
    for side in range(2):
        for core in range(2):
            g = 2 * side + core
            cols = pl.ds(g * GW, GW)
            mine = (core == c) & (2 * c + side == z)

            @pl.when(mine)
            def _():
                pltpu.make_async_copy(d_ref.at[:, cols], out_ref.at[z], lsem).start()

            @pl.when(jnp.logical_not(mine))
            def _():
                remote(d_ref.at[:, cols], out_ref.at[z], send.at[g], recv.at[z], (2 * p + core, 2 * c + side)).start()
    for side in range(2):
        for core in range(2):
            g = 2 * side + core
            cols = pl.ds(g * GW, GW)
            mine = (core == c) & (2 * c + side == z)

            @pl.when(mine)
            def _():
                pltpu.make_async_copy(d_ref.at[:, cols], out_ref.at[z], lsem).wait()

            @pl.when(jnp.logical_not(mine))
            def _():
                remote(d_ref.at[:, cols], out_ref.at[z], send.at[g], recv.at[z], (2 * p + core, 2 * c + side)).wait_send()
    for s in range(STREAMS):
        @pl.when((q != c) | (s != z))
        def _():
            remote(d_ref.at[:, pl.ds(0, GW)], out_ref.at[s], send.at[0], recv.at[s], (2 * p + q, s)).wait_recv()


def to_heads(d):
    return comm_call(
        to_heads_kernel, "to_heads", 2, (((STREAMS, ROWS, GW), BF16),), [dma(4), dma(4), pltpu.SemaphoreType.DMA], d
    )[0]


def sum_rows_kernel(
    d_ref, out_ref, dsend, drecv, send, recv, csend, crecv, lsem, near, mine_buf, own, land, tail, total
):
    p, c, q, r, z = where_am_i()
    greet_column()
    other = (2 * p + 1 - c, z)
    rows = pl.ds(c * HALF, HALF)
    rest = pl.ds((1 - c) * HALF, HALF)
    last = pl.ds(VIS, CROWS)
    for s in range(STREAMS):
        remote(d_ref.at[s, rest], near.at[s], dsend.at[s], drecv.at[s], other).start()
        pltpu.make_async_copy(d_ref.at[s, rows], mine_buf.at[s], lsem.at[s]).start()
    group = 2 * r + c
    for s in range(STREAMS):
        mine = (q == c) & (s == z)

        @pl.when(mine)
        def _():
            pltpu.make_async_copy(d_ref.at[s, last], tail.at[group], lsem.at[4]).start()

        @pl.when(jnp.logical_not(mine))
        def _():
            remote(d_ref.at[s, last], tail.at[group], csend.at[s], crecv.at[group], (2 * p + q, s)).start()
    for s in range(STREAMS):
        mine = (q == c) & (s == z)
        pltpu.make_async_copy(d_ref.at[s, rows], mine_buf.at[s], lsem.at[s]).wait()
        remote(d_ref.at[s, rest], near.at[s], dsend.at[s], drecv.at[s], other).wait_recv()
        for t in range(HALF // 64):
            part = pl.ds(t * 64, 64)
            both = near[s, part].astype(F32) + mine_buf[s, part].astype(F32)
            own[s, part] = both.astype(BF16)

        @pl.when(mine)
        def _():
            pltpu.make_async_copy(own.at[s], land.at[r, rows], lsem.at[5]).start()

        @pl.when(jnp.logical_not(mine))
        def _():
            remote(own.at[s], land.at[r, rows], send.at[s], recv.at[r, c], (2 * p + q, s)).start()
    for s in range(STREAMS):
        mine = (q == c) & (s == z)
        remote(d_ref.at[s, rest], near.at[s], dsend.at[s], drecv.at[s], other).wait_send()

        @pl.when(mine)
        def _():
            pltpu.make_async_copy(d_ref.at[s, last], tail.at[group], lsem.at[4]).wait()
            pltpu.make_async_copy(own.at[s], land.at[r, rows], lsem.at[5]).wait()

        @pl.when(jnp.logical_not(mine))
        def _():
            remote(d_ref.at[s, last], tail.at[group], csend.at[s], crecv.at[group], (2 * p + q, s)).wait_send()
            remote(own.at[s], land.at[r, rows], send.at[s], recv.at[r, c], (2 * p + q, s)).wait_send()
    for side in range(2):
        for core in range(2):
            @pl.when((core != c) | (2 * c + side != z))
            def _():
                part = pl.ds(core * HALF, HALF)
                remote(own.at[0], land.at[side, part], send.at[0], recv.at[side, core], other).wait_recv()
                g = 2 * side + core
                remote(d_ref.at[0, last], tail.at[g], csend.at[0], crecv.at[g], other).wait_recv()
    for t in range(VIS // 64):
        part = pl.ds(t * 64, 64)
        total[part] = land[0, part].astype(F32) + land[1, part].astype(F32)
    ends = [tail[g].astype(F32) for g in range(4)]
    total[last] = (ends[0] + ends[1]) + (ends[2] + ends[3])
    done = pltpu.make_async_copy(total, out_ref, lsem.at[6])
    done.start()
    done.wait()


def sum_rows(d):
    return comm_call(
        sum_rows_kernel, "sum_rows", 3, (((ROWS, D), F32),),
        [
            dma(4), dma(4), dma(4), dma(2, 2), dma(4), dma(4), dma(7),
            VM((STREAMS, HALF, D), BF16), VM((STREAMS, HALF, D), BF16), VM((STREAMS, HALF, D), BF16),
            VM((2, VIS, D), BF16), VM((4, CROWS, D), BF16), VM((ROWS, D), F32),
        ],
        d,
    )[0]


def layer_norm(values, norm_gain, norm_shift):
    centre = values - jnp.mean(values, axis=-1, keepdims=True)
    spread = jnp.mean(centre * centre, axis=-1, keepdims=True)
    return centre * lax.rsqrt(spread + EPS) * norm_gain + norm_shift


def norm_parts(values):
    centre = values - jnp.mean(values, axis=-1, keepdims=True)
    scale = lax.rsqrt(jnp.mean(centre * centre, axis=-1, keepdims=True) + EPS)
    return centre * scale, scale


def norm_back(normed, scale, gain, grad):
    g = grad * gain
    return scale * (
        g - jnp.mean(g, axis=-1, keepdims=True) - normed * jnp.mean(g * normed, axis=-1, keepdims=True)
    )


def own_meta(lengths, mask):
    frames = jnp.arange(FRAMES, dtype=jnp.int32)
    ends = jnp.cumsum(lengths)
    reached = ends[None, :] <= frames[:, None]
    begin = jnp.sum(jnp.where(reached, lengths[None, :], 0), axis=1)
    length = jnp.sum(
        jnp.where((jnp.sum(reached, axis=1)[:, None] == jnp.arange(3)[None, :]), lengths[None, :], 0), axis=1
    )
    base = jnp.where(length == MOST, 0, jnp.where(length == MIDDLE - MOST, MOST, MIDDLE))
    slot = base + frames - begin
    perm = jnp.sum(jnp.where(slot[:, None] == frames[None, :], frames[:, None], 0), axis=0)
    stream = jnp.arange(STREAMS)[:, None]
    row = jnp.arange(CROWS)[None, :]
    part = FRAMES // STREAMS
    frame = jnp.where(row < part * COND, part * stream + row // COND, FRAMES)
    cslot = jnp.sum(jnp.where(frame[..., None] == frames, slot[None, None, :], 0), axis=-1)
    cslot = jnp.where(frame < FRAMES, cslot, 99).reshape(1, PART)
    bias = jnp.where(mask == 1, 0.0, NEG).astype(F32)
    line = jnp.concatenate([perm[None].astype(F32), cslot.astype(F32), jnp.zeros((1, PATCHES - PART - FRAMES), F32)], axis=1)
    return jnp.concatenate([bias, jnp.broadcast_to(line, (8, PATCHES))], axis=0)


def per_device(
    visual, conditioning, d_visual, d_conditioning, episode_frames, patch_mask,
    ln1_gain, ln1_bias, w_qkv, b_qkv, w_proj, b_proj, ln2_gain, ln2_bias, w_in, b_in, w_out, b_out,
):
    d, z = lax.axis_index("dp"), lax.axis_index("stream")
    group = 2 * (z % 2) + d % 2
    blank = jnp.zeros((CROWS - conditioning.shape[1] * COND, D), BF16)

    def chunk(rows, extra):
        return jnp.concatenate([rows.reshape(VIS, D), extra.reshape(-1, D), blank], axis=0)

    x = chunk(visual, conditioning)
    dy = chunk(d_visual, d_conditioning)
    gain_one, shift_one = ln1_gain.astype(F32), ln1_bias.astype(F32)
    gain_two, shift_two = ln2_gain.astype(F32), ln2_bias.astype(F32)
    x_all, meta = gather_rows(x, own_meta(episode_frames[0], patch_mask[0]))
    bias = meta[:FRAMES]
    perm = meta[FRAMES, :FRAMES].astype(jnp.int32)
    cslot = meta[FRAMES, FRAMES : FRAMES + PART].astype(jnp.int32)
    cs_col, cs_row = cslot.reshape(PART, 1), cslot.reshape(1, PART)
    scalars = jnp.concatenate([perm, group.reshape(1).astype(jnp.int32)])
    tables = tuple(jnp.asarray(t) for t in rope_constants())
    a, *saved, o = attend_forward(
        scalars, x_all, w_qkv, b_qkv.astype(F32).reshape(1, -1), gain_one.reshape(1, -1),
        shift_one.reshape(1, -1), tables, bias, cs_col, cs_row,
    )
    attended = to_owner(o)

    inputs = x.astype(F32)
    residual = inputs + jnp.dot(attended, w_proj, preferred_element_type=F32) + b_proj.astype(F32)
    normed_two, scale_two = norm_parts(residual)
    n = (normed_two * gain_two + shift_two).astype(BF16)
    u = jnp.dot(n, w_in, preferred_element_type=F32) + b_in.astype(F32)
    phi = 0.5 * (1.0 + lax.erf(u * (2.0**-0.5)))
    hidden = (u * phi).astype(BF16)
    slope = phi + u * (jnp.exp(-0.5 * u * u) * ((2.0 * math.pi) ** -0.5))
    output = residual + jnp.dot(hidden, w_out, preferred_element_type=F32) + b_out.astype(F32)
    out_visual = output[:VIS].astype(BF16).reshape(visual.shape)
    out_conditioning = output[VIS : VIS + conditioning.shape[1] * COND].astype(BF16).reshape(conditioning.shape)

    dy32 = dy.astype(F32)
    grad_b_out = jnp.sum(dy32, axis=0)
    grad_hidden = jnp.einsum("rd,hd->rh", dy, w_out, preferred_element_type=F32)
    grad_u = (grad_hidden * slope).astype(BF16)
    grad_b_in = jnp.sum(grad_u, axis=0, dtype=F32)
    grad_n = jnp.einsum("rh,dh->rd", grad_u, w_in, preferred_element_type=F32)
    grad_ln2_gain = jnp.sum(grad_n * normed_two, axis=0)
    grad_ln2_bias = jnp.sum(grad_n, axis=0)
    grad_h = dy32 + norm_back(normed_two, scale_two, gain_two, grad_n)
    grad_hb = grad_h.astype(BF16)
    grad_b_proj = jnp.sum(grad_hb, axis=0, dtype=F32)
    grad_o = jnp.einsum("re,de->rd", grad_hb, w_proj, preferred_element_type=F32).astype(BF16)
    grad_o_heads = to_heads(grad_o)
    grad_qkv = attend_backward(scalars, saved, o, grad_o_heads, tables, cs_col, cs_row)

    flat = grad_qkv.reshape(STREAMS * ROWS, 3 * GW)
    role_w = jnp.concatenate(
        [lax.dynamic_slice_in_dim(w_qkv, part * D + group * GW, GW, 1) for part in range(3)], axis=1
    )
    partial = jnp.einsum("re,de->rd", flat, role_w, preferred_element_type=F32).astype(BF16)
    grad_a = sum_rows(partial.reshape(STREAMS, ROWS, D))
    normed_one, scale_one = norm_parts(inputs)
    grad_ln1_gain = jnp.sum(grad_a * normed_one, axis=0)
    grad_ln1_bias = jnp.sum(grad_a, axis=0)
    grad_x = grad_h + norm_back(normed_one, scale_one, gain_one, grad_a)
    grad_visual = grad_x[:VIS].reshape(visual.shape)
    grad_conditioning = grad_x[VIS : VIS + conditioning.shape[1] * COND].reshape(conditioning.shape)

    role_grad = jnp.einsum("rd,re->de", a.reshape(STREAMS * ROWS, D), flat, preferred_element_type=F32)
    role_bias = jnp.sum(flat, axis=0, dtype=F32)
    grad_w_qkv = jnp.zeros((D, 3 * D), BF16)
    grad_b_qkv = jnp.zeros((3 * D,), F32)
    for part in range(3):
        cut = slice(part * GW, (part + 1) * GW)
        at = part * D + group * GW
        grad_w_qkv = lax.dynamic_update_slice_in_dim(grad_w_qkv, role_grad[:, cut].astype(BF16), at, 1)
        grad_b_qkv = lax.dynamic_update_slice_in_dim(grad_b_qkv, role_bias[cut], at, 0)
    grad_w_in = jnp.einsum("rd,rh->dh", n, grad_u, preferred_element_type=F32)
    grad_w_out = jnp.einsum("rh,rd->hd", hidden, dy, preferred_element_type=F32)
    grad_w_proj = jnp.einsum("rd,re->de", attended, grad_hb, preferred_element_type=F32)

    def reduce(g, kind):
        return lax.psum_scatter(g.astype(kind), ("dp", "stream"), scatter_dimension=0, tiled=True).astype(F32)

    return (
        out_visual, out_conditioning, grad_visual, grad_conditioning,
        reduce(grad_ln1_gain, F32), reduce(grad_ln1_bias, F32), reduce(grad_w_qkv, BF16),
        reduce(grad_b_qkv[: 2 * D], F32), reduce(grad_b_qkv[2 * D :], F32), reduce(grad_w_proj, BF16),
        reduce(grad_b_proj, F32), reduce(grad_ln2_gain, F32), reduce(grad_ln2_bias, F32), reduce(grad_w_in, BF16),
        reduce(grad_b_in, F32), reduce(grad_w_out, BF16), reduce(grad_b_out, F32),
    )


def solution(mesh):
    rows = P("dp", None, "stream", None)
    extra = P("dp", "stream", None, None)
    vector = P(("dp", "stream"))
    matrix = P(("dp", "stream"), None)
    in_specs = (rows, extra, rows, extra, P("dp", None), P("dp", None, None)) + (P(),) * 12
    out_specs = (
        rows, extra, rows, extra, vector, vector, matrix, vector, vector, matrix, vector, vector, vector, matrix,
        vector, matrix, vector,
    )
    return jax.shard_map(per_device, mesh=mesh, in_specs=in_specs, out_specs=out_specs, check_vma=False)
```

time: 2110 us -> 856 us (0.41)
  waiting for transfers between devices: 1400 us -> 369 us
  matrix products: 399 us -> 85.7 us
  Pallas kernels: 0 us -> 276 us
  local copies, waits for them, and re-layouts: 103 us -> 24.7 us
  other arithmetic: 81.3 us -> 25.8 us
  loops' own time: 52.7 us -> 0 us
    reduce_scatter x4, waiting for transfers between devices: 894 us -> 369 us  [reduce(): lax.psum_scatter(g.astype(kind), ('dp', 'stream'), scatter_dimension=0, t...]
    dot_general x124 -> x11, matrix products: 399 us -> 85.7 us  [the longest x1 11.7 us: per_device(): u = jnp.dot(n, w_in, preferred_element_type=F32) + b_in.astype(F32)]
    unnamed x8 -> x4, waiting for transfers between devices: 294 us -> 0.07 us
    pallas_call x0 -> x6, Pallas kernels: none -> 276 us  [the longest x4 165 us: comm_call(): pl.pallas_call(kernel, name=name, out_shape=tuple((jax.ShapeDtypeStruct(s...]
    all_gather x2 -> x0, waiting for transfers between devices: 210 us -> none  [the longest x1 136 us: per_device(): lax.all_gather(keys_own, 'stream', axis=1, tiled=True)]
    another operation x2 -> x0, loops' own time: 52.7 us -> none  [the longest x1 41.9 us: per_device(): lax.map(attend_backward, jnp.arange(HEADS, dtype=jnp.int32))]
    another operation x11 -> x1, other arithmetic: 42 us -> 0.95 us
    convert_element_type x7 -> x2, local copies, waits for them, and re-layouts: 22.8 us -> 0.79 us  [the longest x1 0.71 us: per_device(): cslot = meta[FRAMES, FRAMES:FRAMES + PART].astype(jnp.int32)]
  transfers between devices with their start and end apart: 7 -> 4, of which waited for: 7 -> 2; matrix products, arithmetic and copies ran while one was open for 7% -> 9% of each run, Pallas kernels for 0% -> 16%
where the time goes in v1:
time: 856 us; the launch traced here: 851 us
  waiting for transfers between devices  369 us (43%)
  Pallas kernels  276 us (32%)
  matrix products  85.7 us (10%)
  blocking collectives  54.5 us (6%)
  other arithmetic  25.8 us (3%)
  local copies, waits for them, and re-layouts  24.7 us (3%)
  between operations  14.6 us (2%)
    reduce_scatter x4, waiting for transfers between devices, reduce(): lax.psum_scatter(g.astype(kind), ('dp', 'stream'), scatter_dimension=0, t...  369 us
    pallas_call x4, Pallas kernels, comm_call(): pl.pallas_call(kernel, name=name, out_shape=tuple((jax.ShapeDtypeStruct(s...  165 us
    pallas_call x1, Pallas kernels, attend_forward(): pl.pallas_call(forward_kernel, name='attend_forward', out_shape=tuple((ja...  58.7 us
    unnamed x1, blocking collectives  54.5 us
    pallas_call x1, Pallas kernels, attend_backward(): pl.pallas_call(backward_kernel, name='attend_backward', out_shape=jax.Sha...  52.1 us
  transfers between devices with their start and end apart: 4, of which 2 were waited for; matrix products, arithmetic and copies ran while one was open for 9% of the time, Pallas kernels for 16%

profile of v1, /device:TPU:0, one launch (start us, length us, event | category | flops | bytes accessed | tf_op | source)
XLA Modules:
  0.0 850.6 jit_solution(17254266920421266033)
XLA Ops:
  11.8 2.5 convert_reduce_fusion.2
  14.3 51.8 %gather_rows.1 = (bf16[4,528,1024]{2,1,0:T(8,128)(2,1)}, f32[16,256]{1,0:T(8,128)}) custom-call(bf16[528,1024]{1,0:T(8,128)(2,1)} %get-tuple-element.63.x_ref, f32[16,256]{1,0:T(8,128)} %pad_maximum_fusion.m_ref), custom_call_target="tpu_custom_call" | custom-call | tf_op jit(solution)/shard_map/gather_rows/pallas_call | solution.py:446
  72.4 58.7 %attend_forward.1 = (bf16[4,528,1024]{2,1,0:T(8,128)(2,1)}, bf16[8,256,512]{2,1,0:T(8,128)(2,1)}, bf16[8,256,512]{2,1,0:T(8,128)(2,1)}, bf16[8,256,512]{2,1,0:T(...) custom-call(s32[9]{0:T(128)} %pad_add_fusion.perm, ...), custom_call_target="tpu_custom_call" | custom-call | flops 8000000000 | bytes 20000000 | tf_op jit(solution)/shard_map/attend_forward/pallas_call | solution.py:262
  131.2 27.0 %to_owner.1 = bf16[528,1024]{1,0:T(8,128)(2,1)} custom-call(bf16[4,528,256]{2,1,0:T(8,128)(2,1)} %get-tuple-element.31.o_ref), custom_call_target="tpu_custom_call" | custom-call | tf_op jit(solution)/shard_map/to_owner/pallas_call | solution.py:446
  158.3 2.6 fusion.30
  162.7 11.7 %multiply_convert_fusion = (bf16[528,4096]{1,0:T(8,128)(2,1)}, f32[528,4096]{1,0:T(8,128)}) fusion(f32[4096]{0:T(1024)S(1)} %convert_element_type.142, bf16[1024,4096]{1,0:T(8,128)(2,1)} %param.36, f32[528,1024]{1,0:T(8,128)} %copy-done.4, f32[1024]{0:T(1024)S(1)} %convert_element_type.140, f32[1024]{0:T(1024)S(1)} %convert_element_type.139, ...), kind=kOutput, calls=%fused_computation.8 | convolution fusion | flops 4444864512 | bytes 23556224 | tf_op jit(solution)/shard_map/dot_general | solution.py:779
  174.5 11.2 %convert_reduce_fusion = (f32[4096]{0:T(1024)S(1)}, bf16[528,4096]{1,0:T(8,128)(2,1)S(1)}) fusion(f32[528,4096]{1,0:T(8,128)} %get-tuple-element.73, f32[4096]{0:T(1024)S(1)} %convert_element_type.142, bf16[4096,1024]{1,0:T(8,128)(2,1)} %param.38, bf16[4,1024]{1,0:T(4,128)(2,1)S(1)} %reshape.363, bf16[512,1024]{1,0:T(8,128)(2,1)S(1)} %bitcast.45, ...), kind=kOutput, calls=%fused_computation.7 | convolution fusion | flops 4460539904 | bytes 22455328 | tf_op jit(solution)/shard_map/rd,hd->rh/dot_general | solution.py:789
  185.7 9.3 %multiply_reduce_fusion = (f32[1024]{0:T(1024)S(1)}, f32[528]{0:T(1024)S(1)}, f32[528]{0:T(1024)S(1)}, f32[1024]{0:T(1024)S(1)}, f32[528,1024]{1,0:T(8,128)S(1)}) fusion(f32[528,1024]{1,0:T(8,128)S(1)} %copy-done.5, f32[528]{0:T(1024)S(1)} %add_rsqrt_fusion.1, f32[528]{0:T(1024)S(1)} %broadcast_multiply_fusion.5, f32[1024]{0:T(1024)S(1)} %convert_element_type.139, ...), kind=kOutput, calls=%fused_computation.32 | convolution fusion | flops 4434048000 | bytes 17060096 | tf_op jit(solution)/shard_map/rh,dh->rd/dot_general | solution.py:792
  197.8 3.1 convolution_convert_fusion.3
  201.1 3.9 convolution_convert_fusion.4.d_ref
  205.0 31.3 %to_heads.1.do_ref = bf16[4,528,256]{2,1,0:T(8,128)(2,1)} custom-call(bf16[528,1024]{1,0:T(8,128)(2,1)} %convolution_convert_fusion.4.d_ref), custom_call_target="tpu_custom_call" | custom-call | tf_op jit(solution)/shard_map/to_heads/pallas_call | solution.py:446
  236.3 52.1 %attend_backward.1 = bf16[4,528,768]{2,1,0:T(8,128)(2,1)} custom-call(s32[9]{0:T(128)} %pad_add_fusion.perm, bf16[8,256,512]{2,1,0:T(8,128)(2,1)} %get-tuple-element.32.q_ref, bf16[8,256,512]{2,1,0:T(8,128)(2,1)} %get-tuple-element.33.k_ref, bf16[8,256,512]{2,1,0:T(8,128)(2,1)} %get-tuple-element.34.v_ref, bf16[64,512]{1,0:T(8,128)(2,1)} %get-tuple-element.35.qc_ref, ...), custom_call_target="tpu_custom_call" | custom-call | flops 10000000000 | bytes 20000000 | tf_op jit(solution)/shard_map/attend_backward/pallas_call | solution.py:397
  288.4 7.2 bitcast_convert_fusion
  295.6 3.4 broadcast_in_dim.143
  302.0 11.6 %convolution_convert_fusion.1 = bf16[1024,4096]{1,0:T(8,128)(2,1)} fusion(bf16[528,4096]{1,0:T(8,128)(2,1)} %copy-done.23, f32[528,1024]{1,0:T(8,128)} %copy-done.4, f32[1024]{0:T(1024)S(1)} %convert_element_type.140, f32[1024]{0:T(1024)S(1)} %convert_element_type.139, f32[528]{0:T(1024)S(1)} %add_rsqrt_fusion.1, f32[528]{0:T(1024)S(1)} %broadcast_multiply_fusion.5), kind=kOutput, calls=%fused_computation.11 | convolution fusion | flops 4436082688 | bytes 14889088 | tf_op jit(solution)/shard_map/rd,rh->dh/dot_general | solution.py:824
  314.8 11.4 %convolution_convert_fusion = bf16[4096,1024]{1,0:T(8,128)(2,1)} fusion(bf16[528,4096]{1,0:T(8,128)(2,1)} %get-tuple-element.72, bf16[4,1024]{1,0:T(4,128)(2,1)S(1)} %reshape.363, bf16[512,1024]{1,0:T(8,128)(2,1)S(1)} %bitcast.47, bf16[528]{0:T(1024)(128)(2,1)S(1)} %pad.15.clone), kind=kOutput, calls=%fused_computation.10 | convolution fusion | flops 4436623360 | bytes 13771808 | tf_op jit(solution)/shard_map/rh,rd->hd/dot_general | solution.py:825
  326.2 2.6 convert_reduce_fusion.1
  330.6 5.4 convolution_convert_fusion.2
  336.0 54.9 %sum_rows.1 = f32[528,1024]{1,0:T(8,128)} custom-call(bf16[4,528,1024]{2,1,0:T(8,128)(2,1)} %bitcast.40), custom_call_target="tpu_custom_call" | custom-call | tf_op jit(solution)/shard_map/sum_rows/pallas_call | solution.py:446
  391.4 3.0 fusion.15
  397.6 8.2 add_convert_fusion
  406.9 54.5 %all-reduce.9 = (f32[1024]{0:T(1024)S(1)}, f32[1024]{0:T(1024)S(1)}, f32[2048]{0:T(1024)S(1)}, f32[1024]{0:T(1024)S(1)}, f32[1024]{0:T(1024)S(1)}, /*index=5*/f3...) all-reduce(f32[1024]{0:T(1024)S(1)} %get-tuple-element.43, ...), channel_id=2, replica_groups=mesh['dp'=8,'stream'=4] {'dp','stream'}, use_global_device_ids=true, to_apply=%region_15.16.clone | all-reduce | flops 13312 | bytes 106496
  471.1 185.2 %reduce-scatter.9.cloned.1.call-done = bf16[32,4096]{1,0:T(8,128)(2,1)} async-done(((bf16[1024,4096]{1,0:T(8,128)(2,1)}), bf16[32,4096]{1,0:T(8,128)(2,1)}) %reduce-scatter.9.cloned.1.call-update) | async-done | bytes 262160 | tf_op jit(solution)/shard_map/reduce_scatter | solution.py:829
  658.1 183.9 %reduce-scatter.11.cloned.1.call-done = bf16[128,1024]{1,0:T(8,128)(2,1)} async-done(((bf16[4096,1024]{1,0:T(8,128)(2,1)}), bf16[128,1024]{1,0:T(8,128)(2,1)}) %reduce-scatter.11.cloned.1.call-update) | async-done | bytes 262160 | tf_op jit(solution)/shard_map/reduce_scatter | solution.py:829
  (139 shorter events, 39.3 us)
Async XLA Ops:
  7.2 151.1 %copy-start = (bf16[1024,1024]{1,0:T(8,128)(2,1)S(1)}, bf16[1024,1024]{1,0:T(8,128)(2,1)}, u32[]{:S(2)}) copy-start(bf16[1024,1024]{1,0:T(8,128)(2,1)} %param.32) | copy-start | bytes 6291460
  7.2 62.9 %copy-start.17 = (bf16[1024]{0:T(1024)(128)(2,1)S(1)}, bf16[1024]{0:T(1024)(128)(2,1)}, u32[]{:S(2)}) copy-start(bf16[1024]{0:T(1024)(128)(2,1)} %param.28) | copy-start | bytes 6148
  7.2 63.4 %copy-start.16 = (bf16[3072]{0:T(1024)(128)(2,1)S(1)}, bf16[3072]{0:T(1024)(128)(2,1)}, u32[]{:S(2)}) copy-start(bf16[3072]{0:T(1024)(128)(2,1)} %param.31) | copy-start | bytes 18436
  7.2 64.0 %copy-start.18 = (bf16[1024]{0:T(1024)(128)(2,1)S(1)}, bf16[1024]{0:T(1024)(128)(2,1)}, u32[]{:S(2)}) copy-start(bf16[1024]{0:T(1024)(128)(2,1)} %param.29) | copy-start | bytes 6148
  7.2 460.6 %reduce-scatter.7.cloned.1.call-start = ((), (), s32[]{:S(2)}) async-start(), calls=%async_computation.5 | async-start | bytes 2162688 | tf_op jit(solution)/shard_map/reduce_scatter | solution.py:829
  131.2 27.0 %copy-start.19 = (bf16[1024]{0:T(1024)(128)(2,1)S(1)}, bf16[1024]{0:T(1024)(128)(2,1)}, u32[]{:S(2)}) copy-start(bf16[1024]{0:T(1024)(128)(2,1)} %param.33) | copy-start | bytes 6148
  131.2 27.1 %copy-start.2 = (bf16[528,1024]{1,0:T(8,128)(2,1)S(1)}, bf16[528,1024]{1,0:T(8,128)(2,1)}, u32[]{:S(2)}) copy-start(bf16[528,1024]{1,0:T(8,128)(2,1)} %get-tuple-element.63.x_ref) | copy-start | bytes 3244036
  160.9 1.7 copy-start.21
  161.0 1.7 copy-start.15
  162.7 11.7 %copy-start.11 = (bf16[1,8,64,1024]{3,2,1,0:T(8,128)(2,1)S(1)}, bf16[1,8,64,1024]{3,2,1,0:T(8,128)(2,1)}, u32[]{:S(2)}) copy-start(bf16[1,8,64,1024]{3,2,1,0:T(8,128)(2,1)} %param.24) | copy-start | bytes 3145732
  174.5 11.2 %copy-start.5 = (f32[528,1024]{1,0:T(8,128)S(1)}, f32[528,1024]{1,0:T(8,128)}, u32[]{:S(2)}) copy-start(f32[528,1024]{1,0:T(8,128)} %copy-done.4) | copy-start | bytes 6488068
  185.7 9.3 %copy-start.23 = (bf16[528,4096]{1,0:T(8,128)(2,1)}, bf16[528,4096]{1,0:T(8,128)(2,1)S(1)}, u32[]{:S(2)}) copy-start(bf16[528,4096]{1,0:T(8,128)(2,1)S(1)} %get-tuple-element.76) | copy-start | bytes 12976132
  195.0 2.8 copy-start.10
  201.0 268.4 %reduce-scatter.5.cloned.1.call-start = ((), (), s32[]{:S(2)}) async-start(), calls=%async_computation.4 | async-start | bytes 6488064 | tf_op jit(solution)/shard_map/reduce_scatter | solution.py:829
  301.7 354.6 %reduce-scatter.9.cloned.1.call-start = ((), (), s32[]{:S(2)}) async-start(), calls=%async_computation.6 | async-start | bytes 8650752 | tf_op jit(solution)/shard_map/reduce_scatter | solution.py:829
  313.6 528.5 %reduce-scatter.11.cloned.1.call-start = ((), (), s32[]{:S(2)}) async-start(), calls=%async_computation.7 | async-start | bytes 8650752 | tf_op jit(solution)/shard_map/reduce_scatter | solution.py:829
  326.2 4.4 copy-start.9
  336.0 55.4 %copy-start.13 = (f32[1024]{0:T(1024)S(1)}, f32[1024]{0:T(1024)}, u32[]{:S(2)}) copy-start(f32[1024]{0:T(1024)} %convert_element_type.135) | copy-start | bytes 12292
  390.9 3.5 copy-start.3
  390.9 3.5 copy-start.8
  391.4 5.4 slice-start
  394.4 2.4 slice-start.1
  395.2 2.5 copy-start.6
  397.6 446.2 %copy-start.1 = (bf16[1024,1024]{1,0:T(8,128)(2,1)S(1)}, bf16[1024,1024]{1,0:T(8,128)(2,1)}, u32[]{:S(2)}) copy-start(bf16[1024,1024]{1,0:T(8,128)(2,1)} %param.32) | copy-start | bytes 6291460
  (6 other events, 8.9 us)
Sparse Core Ops, SparseCore 0:
  201.1 150.5 reduce-scatter.6
  358.3 110.7 reduce-scatter.4
  471.4 184.8 reduce-scatter.8
  658.5 183.4 reduce-scatter.10

commit v2 on v1

--- a/solution.py
+++ b/solution.py
@@ -703,6 +703,365 @@
     )[0]
 
 
+CHUNKS = 9
+CUT = D // 2
+QCUT = 3 * GW // 2
+
+
+def add_up(*terms):
+    total = terms[0].astype(F32)
+    for t in terms[1:]:
+        total = total + t.astype(F32)
+    return total
+
+
+def reduce_kernel(
+    nx, ny, rb,
+    go_ref, gi_ref, gp_ref, gq_ref, v_ref,
+    oo_ref, oi_ref, op_ref, oq_ref, ov_ref,
+    mine, rd, r2a, r2b, s2a, s2b, r3a, r3b, s3, r4, s4, r5, fin,
+    q1, rq1a, rq1b, sq1a, sq1b, rq2a, rq2b, sq2, rq3, sq3, vm, vd, vx, vy, vz1, vz2,
+    lsem, ds, dr, as2, ar2, bs2, br2, as3, ar3, bs3, br3, s4s, s4r, s5s, s5r,
+    qs1a, qr1a, qs1b, qr1b, qs2a, qr2a, qs2b, qr2b, qs3, qr3, qs4, qr4, vs, vr, vsx, vrx, vsy, vry, osem,
+):
+    d, z = lax.axis_index("dp"), lax.axis_index("stream")
+    p, c, hi, lo = d // 2, d % 2, z // 2, z % 2
+    x, y = p % nx, p // nx
+    near = (d + 1 - 2 * c, z)
+    z_one = (d, z + 1 - 2 * lo)
+    z_two = (d, z + 2 - 4 * hi)
+    slant = (d + 1 - 2 * c, z + 1 - 2 * lo)
+
+    def along_x(n):
+        return lax.rem(x + n, nx)
+
+    def along_y(n):
+        return lax.rem(y + n, ny)
+
+    def x_device(n):
+        return ((y * nx + along_x(n)) * 2 + c, z)
+
+    def y_device(n):
+        return ((along_y(n) * nx + x) * 2 + c, z)
+
+    barrier = pltpu.get_barrier_semaphore()
+    friends = [near, z_one, z_two, slant]
+    friends += [x_device(n) for n in range(1, nx)] + [y_device(n) for n in range(1, ny)]
+    for device in friends:
+        pl.semaphore_signal(barrier, inc=1, device_id=device, device_id_type=pl.DeviceIdType.MESH)
+    pl.semaphore_wait(barrier, len(friends))
+
+    first, second = pl.ds(0, CUT), pl.ds(CUT, CUT)
+
+    def source(k, core):
+        if k < 4:
+            return go_ref.at[:, :, core, :, k]
+        if k < 8:
+            return gi_ref.at[:, :, core, :, :, pl.ds((k - 4) * D, D)]
+        return gp_ref.at[:, :, core]
+
+    def core_copy(k):
+        return remote(source(k, 1 - c), rd.at[k], ds.at[k], dr.at[k], near)
+
+    def own_copy(k):
+        return pltpu.make_async_copy(source(k, c), mine.at[k], lsem.at[k])
+
+    def a2(k, n):
+        return remote(mine.at[k, :, along_x(n), :, :, first], r2a.at[k, n - 1], as2.at[k, n - 1], ar2.at[k, n - 1], x_device(n))
+
+    def b2(k, n):
+        return remote(mine.at[k, along_y(n), :, :, :, second], r2b.at[k, n - 1], bs2.at[k, n - 1], br2.at[k, n - 1], y_device(n))
+
+    def a3(k, n):
+        return remote(s2a.at[k, along_y(n)], r3a.at[k, n - 1], as3.at[k, n - 1], ar3.at[k, n - 1], y_device(n))
+
+    def b3(k, n):
+        return remote(s2b.at[k, along_x(n)], r3b.at[k, n - 1], bs3.at[k, n - 1], br3.at[k, n - 1], x_device(n))
+
+    def c4(k):
+        return remote(s3.at[k, :, 1 - lo], r4.at[k], s4s.at[k], s4r.at[k], z_one)
+
+    def c5(k):
+        return remote(s4.at[k, 1 - hi], r5.at[k], s5s.at[k], s5r.at[k], z_two)
+
+    qa, qb = pl.ds(0, QCUT), pl.ds(QCUT, QCUT)
+
+    def q1a(n):
+        return remote(q1.at[:, along_x(n), :, :, qa], rq1a.at[n - 1], qs1a.at[n - 1], qr1a.at[n - 1], x_device(n))
+
+    def q1b(n):
+        return remote(q1.at[along_y(n), :, :, :, qb], rq1b.at[n - 1], qs1b.at[n - 1], qr1b.at[n - 1], y_device(n))
+
+    def q2a(n):
+        return remote(sq1a.at[along_y(n)], rq2a.at[n - 1], qs2a.at[n - 1], qr2a.at[n - 1], y_device(n))
+
+    def q2b(n):
+        return remote(sq1b.at[along_x(n)], rq2b.at[n - 1], qs2b.at[n - 1], qr2b.at[n - 1], x_device(n))
+
+    def q3():
+        return remote(sq2.at[:, 1 - hi], rq3, qs3, qr3, z_two)
+
+    group = 2 * lo + c
+    mates = [(near, 1, 0), (z_one, 0, 1), (slant, 1, 1)]
+
+    def q4(n, part):
+        device, core, side = mates[n]
+        to_core = c + core - 2 * c * core
+        to_side = lo + side - 2 * lo * side
+        place = pl.ds(pl.multiple_of(part * D + group * GW, GW), GW)
+        return remote(
+            sq3.at[to_core, to_side, :, pl.ds(part * GW, GW)], oq_ref.at[:, place],
+            qs4.at[n, part], qr4.at[n, part], device,
+        )
+
+    def q4_own(part):
+        place = pl.ds(pl.multiple_of(part * D + group * GW, GW), GW)
+        return pltpu.make_async_copy(sq3.at[c, lo, :, pl.ds(part * GW, GW)], oq_ref.at[:, place], lsem.at[CHUNKS + 2 + part])
+
+    def v_core():
+        return remote(v_ref.at[:, :, 1 - c], vd, vs.at[0], vr.at[0], near)
+
+    def v_x(n):
+        return remote(vm.at[:, along_x(n)], vx.at[n - 1], vsx.at[n - 1], vrx.at[n - 1], x_device(n))
+
+    def v_y(n):
+        return remote(vm.at[along_y(n), x], vy.at[n - 1], vsy.at[n - 1], vry.at[n - 1], y_device(n))
+
+    def v_z1():
+        return remote(vm.at[y, x, :, 1 - lo], vz1, vs.at[1], vr.at[1], z_one)
+
+    def v_z2():
+        return remote(vm.at[y, x, 1 - hi, lo], vz2, vs.at[2], vr.at[2], z_two)
+
+    q_own = pltpu.make_async_copy(gq_ref, q1, lsem.at[CHUNKS])
+    v_own = pltpu.make_async_copy(v_ref.at[:, :, c], vm, lsem.at[CHUNKS + 1])
+    v_own.start()
+    v_core().start()
+    q_own.start()
+    for k in range(CHUNKS):
+        core_copy(k).start()
+        own_copy(k).start()
+    q_own.wait()
+    for n in range(1, nx):
+        q1a(n).start()
+    for n in range(1, ny):
+        q1b(n).start()
+
+    def at(k, value, body):
+        pl.when(k == value)(body)
+
+    def q_second():
+        for n in range(1, nx):
+            q1a(n).wait_recv()
+        for n in range(1, ny):
+            q1b(n).wait_recv()
+        for b in range(ny):
+            sq1a[b] = add_up(q1[b, x, :, :, 0:QCUT], *[rq1a[n, b] for n in range(nx - 1)]).astype(BF16)
+        for n in range(1, ny):
+            q2a(n).start()
+        for b in range(nx):
+            sq1b[b] = add_up(q1[y, b, :, :, QCUT:], *[rq1b[n, b] for n in range(ny - 1)]).astype(BF16)
+        for n in range(1, nx):
+            q2b(n).start()
+
+    def q_third():
+        for n in range(1, ny):
+            q2a(n).wait_recv()
+        for n in range(1, nx):
+            q2b(n).wait_recv()
+        left = add_up(sq1a[y], *[rq2a[n] for n in range(ny - 1)]).astype(BF16)
+        right = add_up(sq1b[x], *[rq2b[n] for n in range(nx - 1)]).astype(BF16)
+        sq2[:, :, :, :, 0:QCUT] = left.reshape(2, 2, 2, rb, QCUT)
+        sq2[:, :, :, :, QCUT:] = right.reshape(2, 2, 2, rb, QCUT)
+        q3().start()
+
+    def q_fourth():
+        q3().wait_recv()
+        sq3[...] = add_up(sq2[:, hi], rq3[...])
+        for part in range(3):
+            for n in range(3):
+                q4(n, part).start()
+            q4_own(part).start()
+
+    def v_first():
+        v_own.wait()
+        v_core().wait_recv()
+        vm[...] = vm[...] + vd[...]
+        for n in range(1, nx):
+            v_x(n).start()
+
+    def v_second():
+        for n in range(1, nx):
+            v_x(n).wait_recv()
+        for b in range(ny):
+            vm[b, x] = add_up(vm[b, x], *[vx[n, b] for n in range(nx - 1)])
+        for n in range(1, ny):
+            v_y(n).start()
+
+    def v_third():
+        for n in range(1, ny):
+            v_y(n).wait_recv()
+        vm[y, x] = add_up(vm[y, x], *[vy[n] for n in range(ny - 1)])
+        v_z1().start()
+
+    def v_fourth():
+        v_z1().wait_recv()
+        vm[y, x, :, lo] = vm[y, x, :, lo] + vz1[...]
+        v_z2().start()
+
+    def turn_loop(k, carry):
+        @pl.when(k < CHUNKS)
+        def _():
+            own_copy_k = pltpu.make_async_copy(gp_ref.at[:, :, c], mine.at[k], lsem.at[k])
+            own_copy_k.wait()
+            remote(gp_ref.at[:, :, 1 - c], rd.at[k], ds.at[k], dr.at[k], near).wait_recv()
+            for b in range(ny):
+                for e in range(nx):
+                    mine[k, b, e] = add_up(mine[k, b, e], rd[k, b, e]).astype(BF16)
+            for n in range(1, nx):
+                a2(k, n).start()
+            for n in range(1, ny):
+                b2(k, n).start()
+
+        at(k, 0, v_first)
+        at(k, 1, v_second)
+        at(k, 2, v_third)
+        at(k, 3, v_fourth)
+        at(k, 1, q_second)
+        at(k, 3, q_third)
+        at(k, 5, q_fourth)
+
+        @pl.when((k >= 1) & (k < CHUNKS + 1))
+        def _():
+            j = k - 1
+            for n in range(1, nx):
+                a2(j, n).wait_recv()
+            for b in range(ny):
+                s2a[j, b] = add_up(mine[j, b, x, :, :, 0:CUT], *[r2a[j, n, b] for n in range(nx - 1)]).astype(BF16)
+            for n in range(1, ny):
+                a3(j, n).start()
+            for n in range(1, ny):
+                b2(j, n).wait_recv()
+            for b in range(nx):
+                s2b[j, b] = add_up(mine[j, y, b, :, :, CUT:], *[r2b[j, n, b] for n in range(ny - 1)]).astype(BF16)
+            for n in range(1, nx):
+                b3(j, n).start()
+
+        @pl.when((k >= 2) & (k < CHUNKS + 2))
+        def _():
+            j = k - 2
+            for n in range(1, ny):
+                a3(j, n).wait_recv()
+            for n in range(1, nx):
+                b3(j, n).wait_recv()
+            left = add_up(s2a[j, y], *[r3a[j, n] for n in range(ny - 1)]).astype(BF16)
+            right = add_up(s2b[j, x], *[r3b[j, n] for n in range(nx - 1)]).astype(BF16)
+            s3[j, :, :, :, 0:CUT] = left.reshape(2, 2, rb, CUT)
+            s3[j, :, :, :, CUT:] = right.reshape(2, 2, rb, CUT)
+            c4(j).start()
+
+        @pl.when((k >= 3) & (k < CHUNKS + 3))
+        def _():
+            j = k - 3
+            c4(j).wait_recv()
+            s4[j] = add_up(s3[j, :, lo], r4[j]).astype(BF16)
+            c5(j).start()
+
+        @pl.when(k >= 4)
+        def _():
+            j = k - 4
+            c5(j).wait_recv()
+            fin[j] = add_up(s4[j, hi], r5[j])
+
+        return carry
+
+    lax.fori_loop(0, CHUNKS + 4, turn_loop, 0)
+    v_z2().wait_recv()
+    vm[y, x, hi, lo] = vm[y, x, hi, lo] + vz2[...]
+    outs = [pltpu.make_async_copy(fin.at[k], oo_ref.at[k], osem.at[k]) for k in range(4)]
+    outs += [
+        pltpu.make_async_copy(fin.at[4 + k], oi_ref.at[:, pl.ds(k * D, D)], osem.at[4 + k]) for k in range(4)
+    ]
+    outs += [pltpu.make_async_copy(fin.at[8], op_ref, osem.at[8])]
+    outs += [pltpu.make_async_copy(vm.at[y, x, hi, lo], ov_ref, osem.at[9])]
+    for copy in outs:
+        copy.start()
+
+    def drain(k, carry):
+        remote(gp_ref.at[:, :, 1 - c], rd.at[k], ds.at[k], dr.at[k], near).wait_send()
+        for n in range(1, nx):
+            a2(k, n).wait_send()
+            b3(k, n).wait_send()
+        for n in range(1, ny):
+            b2(k, n).wait_send()
+            a3(k, n).wait_send()
+        c4(k).wait_send()
+        c5(k).wait_send()
+        return carry
+
+    lax.fori_loop(0, CHUNKS, drain, 0)
+    for n in range(1, nx):
+        q1a(n).wait_send()
+        q2b(n).wait_send()
+        v_x(n).wait_send()
+    for n in range(1, ny):
+        q1b(n).wait_send()
+        q2a(n).wait_send()
+        v_y(n).wait_send()
+    q3().wait_send()
+    v_core().wait_send()
+    v_z1().wait_send()
+    v_z2().wait_send()
+    for part in range(3):
+        q4_own(part).wait()
+        for n in range(3):
+            q4(n, part).wait_send()
+            q4(n, part).wait_recv()
+    for copy in outs:
+        copy.wait()
+
+
+def reduce_grads(g_out, g_in, g_proj, g_qkv, vectors):
+    cores = lax.axis_size("dp") // 2
+    nx = 1 << ((cores.bit_length() - 1) // 2)
+    ny = cores // nx
+    rb = D // (cores * 2 * STREAMS)
+
+    def v(*shape):
+        return VM(shape, BF16)
+
+    def vf(*shape):
+        return VM(shape, F32)
+
+    n = CHUNKS
+    scratch = [
+        v(n, ny, nx, STREAMS, rb, D), v(n, ny, nx, STREAMS, rb, D),
+        v(n, nx - 1, ny, STREAMS, rb, CUT), v(n, ny - 1, nx, STREAMS, rb, CUT),
+        v(n, ny, STREAMS, rb, CUT), v(n, nx, STREAMS, rb, CUT),
+        v(n, ny - 1, STREAMS, rb, CUT), v(n, nx - 1, STREAMS, rb, CUT),
+        v(n, 2, 2, rb, D), v(n, 2, rb, D), v(n, 2, rb, D), v(n, rb, D), vf(n, rb, D),
+        v(ny, nx, 8, rb, 3 * GW), v(nx - 1, ny, 8, rb, QCUT), v(ny - 1, nx, 8, rb, QCUT),
+        v(ny, 8, rb, QCUT), v(nx, 8, rb, QCUT), v(ny - 1, 8, rb, QCUT), v(nx - 1, 8, rb, QCUT),
+        v(2, 2, 2, rb, 3 * GW), v(2, 2, rb, 3 * GW), vf(2, 2, rb, 3 * GW),
+        vf(ny, nx, 2, 2, 8, 128), vf(ny, nx, 2, 2, 8, 128), vf(nx - 1, ny, 2, 2, 8, 128),
+        vf(ny - 1, 2, 2, 8, 128), vf(2, 8, 128), vf(8, 128),
+        dma(n + 5), dma(n), dma(n),
+        dma(n, nx - 1), dma(n, nx - 1), dma(n, ny - 1), dma(n, ny - 1),
+        dma(n, ny - 1), dma(n, ny - 1), dma(n, nx - 1), dma(n, nx - 1),
+        dma(n), dma(n), dma(n), dma(n),
+        dma(nx - 1), dma(nx - 1), dma(ny - 1), dma(ny - 1), dma(ny - 1), dma(ny - 1), dma(nx - 1), dma(nx - 1),
+        pltpu.SemaphoreType.DMA, pltpu.SemaphoreType.DMA, dma(3, 3), dma(3, 3),
+        dma(3), dma(3), dma(nx - 1), dma(nx - 1), dma(ny - 1), dma(ny - 1), dma(10),
+    ]
+    outs = (((4, rb, D), F32), ((rb, 4 * D), F32), ((rb, D), F32), ((rb, 3 * D), F32), ((8, 128), F32))
+    return comm_call(
+        functools.partial(reduce_kernel, nx, ny, rb), "reduce_grads", 4, outs, scratch,
+        g_out.reshape(ny, nx, 2, STREAMS, 4, rb, D), g_in.reshape(ny, nx, 2, STREAMS, rb, 4 * D),
+        g_proj.reshape(ny, nx, 2, STREAMS, rb, D), g_qkv.reshape(ny, nx, 8, rb, 3 * GW),
+        vectors.reshape(ny, nx, 2, 2, 2, 8, 128),
+    )
+
+
 def layer_norm(values, norm_gain, norm_shift):
     centre = values - jnp.mean(values, axis=-1, keepdims=True)
     spread = jnp.mean(centre * centre, axis=-1, keepdims=True)
@@ -814,26 +1173,31 @@
 
     role_grad = jnp.einsum("rd,re->de", a.reshape(STREAMS * ROWS, D), flat, preferred_element_type=F32)
     role_bias = jnp.sum(flat, axis=0, dtype=F32)
-    grad_w_qkv = jnp.zeros((D, 3 * D), BF16)
-    grad_b_qkv = jnp.zeros((3 * D,), F32)
-    for part in range(3):
-        cut = slice(part * GW, (part + 1) * GW)
-        at = part * D + group * GW
-        grad_w_qkv = lax.dynamic_update_slice_in_dim(grad_w_qkv, role_grad[:, cut].astype(BF16), at, 1)
-        grad_b_qkv = lax.dynamic_update_slice_in_dim(grad_b_qkv, role_bias[cut], at, 0)
-    grad_w_in = jnp.einsum("rd,rh->dh", n, grad_u, preferred_element_type=F32)
-    grad_w_out = jnp.einsum("rh,rd->hd", hidden, dy, preferred_element_type=F32)
-    grad_w_proj = jnp.einsum("rd,re->de", attended, grad_hb, preferred_element_type=F32)
-
-    def reduce(g, kind):
-        return lax.psum_scatter(g.astype(kind), ("dp", "stream"), scatter_dimension=0, tiled=True).astype(F32)
-
+    grad_b_qkv = jnp.zeros((3, HEADS // GROUP, GW), F32)
+    grad_b_qkv = lax.dynamic_update_slice_in_dim(grad_b_qkv, role_bias.reshape(3, 1, GW), group, 1).reshape(3 * D)
+    grad_w_in = jnp.einsum("rd,rh->dh", n, grad_u, preferred_element_type=F32).astype(BF16)
+    grad_w_out = jnp.einsum("rh,rd->hd", hidden, dy, preferred_element_type=F32).astype(BF16)
+    grad_w_proj = jnp.einsum("rd,re->de", attended, grad_hb, preferred_element_type=F32).astype(BF16)
+    owners = lax.axis_size("dp") * STREAMS
+    pieces = [
+        grad_ln1_gain, grad_ln1_bias, grad_b_qkv[: 2 * D], grad_b_qkv[2 * D :], grad_b_proj,
+        grad_ln2_gain, grad_ln2_bias, grad_b_in, grad_b_out,
+    ]
+    sizes = [t.shape[0] // owners for t in pieces]
+    packed = jnp.concatenate([t.reshape(owners, -1) for t in pieces], axis=1)
+    packed = jnp.pad(packed, ((0, 0), (0, 1024 - sum(sizes))))
+    red_out, red_in, red_proj, red_qkv, red_small = reduce_grads(
+        grad_w_out, grad_w_in, grad_w_proj, role_grad.astype(BF16), packed
+    )
+    small = []
+    start = 0
+    for size in sizes:
+        small.append(lax.slice_in_dim(red_small.reshape(-1), start, start + size, axis=0))
+        start += size
     return (
         out_visual, out_conditioning, grad_visual, grad_conditioning,
-        reduce(grad_ln1_gain, F32), reduce(grad_ln1_bias, F32), reduce(grad_w_qkv, BF16),
-        reduce(grad_b_qkv[: 2 * D], F32), reduce(grad_b_qkv[2 * D :], F32), reduce(grad_w_proj, BF16),
-        reduce(grad_b_proj, F32), reduce(grad_ln2_gain, F32), reduce(grad_ln2_bias, F32), reduce(grad_w_in, BF16),
-        reduce(grad_b_in, F32), reduce(grad_w_out, BF16), reduce(grad_b_out, F32),
+        small[0], small[1], red_qkv, small[2], small[3], red_proj, small[4], small[5], small[6], red_in,
+        small[7], red_out.reshape(-1, D), small[8],
     )
 
 

time: 856 us -> 515 us (0.60)
  waiting for transfers between devices: 369 us -> 0 us
  Pallas kernels: 276 us -> 385 us
  blocking collectives: 54.5 us -> 0 us
  between operations: 14.6 us -> 1.32 us
    reduce_scatter x4 -> x0, waiting for transfers between devices: 369 us -> none  [reduce(): lax.psum_scatter(g.astype(kind), ('dp', 'stream'), scatter_dimension=0, t...]
    pallas_call x4 -> x5, Pallas kernels: 165 us -> 274 us  [comm_call(): pl.pallas_call(kernel, name=name, out_shape=tuple((jax.ShapeDtypeStruct(s...]
    unnamed x1 -> x0, blocking collectives: 54.5 us -> none
  transfers between devices with their start and end apart: 4 -> 0, of which waited for: 2 -> 0; matrix products, arithmetic and copies ran while one was open for 9% -> 0% of each run, Pallas kernels for 16% -> 0%
where the time goes in v2:
time: 515 us; the launch traced here: 510 us
  Pallas kernels  385 us (75%)
  matrix products  84.6 us (16%)
  other arithmetic  21 us (4%)
  local copies, waits for them, and re-layouts  18.5 us (4%)
    pallas_call x5, Pallas kernels, comm_call(): pl.pallas_call(kernel, name=name, out_shape=tuple((jax.ShapeDtypeStruct(s...  274 us
    pallas_call x1, Pallas kernels, attend_forward(): pl.pallas_call(forward_kernel, name='attend_forward', out_shape=tuple((ja...  58.7 us
    pallas_call x1, Pallas kernels, attend_backward(): pl.pallas_call(backward_kernel, name='attend_backward', out_shape=jax.Sha...  52 us
    dot_general x1, matrix products, per_device(): jnp.einsum('rd,rh->dh', n, grad_u, preferred_element_type=F32).astype(BF16)  11.7 us
    dot_general x1, matrix products, per_device(): grad_hidden = jnp.einsum('rd,hd->rh', dy, w_out, preferred_element_type=F32)  11.4 us

profile of v2, /device:TPU:0, one launch (start us, length us, event | category | flops | bytes accessed | tf_op | source)
XLA Modules:
  0.0 510.3 jit_solution(5001265431082969398)
XLA Ops:
  5.2 2.5 convert_reduce_fusion.2
  7.7 51.8 %gather_rows.1 = (bf16[4,528,1024]{2,1,0:T(8,128)(2,1)}, f32[16,256]{1,0:T(8,128)}) custom-call(bf16[528,1024]{1,0:T(8,128)(2,1)} %get-tuple-element.64.x_ref, f32[16,256]{1,0:T(8,128)} %pad_maximum_fusion.m_ref), custom_call_target="tpu_custom_call" | custom-call | tf_op jit(solution)/shard_map/gather_rows/pallas_call | solution.py:446
  65.8 58.7 %attend_forward.1 = (bf16[4,528,1024]{2,1,0:T(8,128)(2,1)}, bf16[8,256,512]{2,1,0:T(8,128)(2,1)}, bf16[8,256,512]{2,1,0:T(8,128)(2,1)}, bf16[8,256,512]{2,1,0:T(...) custom-call(s32[9]{0:T(128)} %pad_add_fusion.perm, ...), custom_call_target="tpu_custom_call" | custom-call | flops 8000000000 | bytes 20000000 | tf_op jit(solution)/shard_map/attend_forward/pallas_call | solution.py:262
  124.6 27.0 %to_owner.1 = bf16[528,1024]{1,0:T(8,128)(2,1)} custom-call(bf16[4,528,256]{2,1,0:T(8,128)(2,1)} %get-tuple-element.36.o_ref), custom_call_target="tpu_custom_call" | custom-call | tf_op jit(solution)/shard_map/to_owner/pallas_call | solution.py:446
  151.7 2.8 fusion.31
  155.4 8.8 %multiply_convert_fusion = (bf16[528,4096]{1,0:T(8,128)(2,1)}, f32[528,4096]{1,0:T(8,128)}) fusion(f32[4096]{0:T(1024)S(1)} %convert_element_type.132, bf16[1024,4096]{1,0:T(8,128)(2,1)S(1)} %bitcast.82, f32[528,1024]{1,0:T(8,128)S(1)} %get-tuple-element.79, f32[1024]{0:T(1024)S(1)} %convert_element_type.130, f32[1024]{0:T(1024)S(1)} %convert_element_type.129, ...), kind=kOutput, calls=%fused_computation.8 | convolution fusion | flops 4444864512 | bytes 23556224 | tf_op jit(solution)/shard_map/dot_general | solution.py:1138
  164.3 11.4 %convert_reduce_fusion = (f32[4096]{0:T(1024)S(1)}, bf16[528,4096]{1,0:T(8,128)(2,1)S(1)}) fusion(f32[528,4096]{1,0:T(8,128)} %get-tuple-element.81, f32[4096]{0:T(1024)S(1)} %convert_element_type.132, bf16[4096,1024]{1,0:T(8,128)(2,1)} %param.38, bf16[4,1024]{1,0:T(4,128)(2,1)S(1)} %reshape.428, bf16[512,1024]{1,0:T(8,128)(2,1)} %bitcast.62, ...), kind=kOutput, calls=%fused_computation.7 | convolution fusion | flops 4460539904 | bytes 22455328 | tf_op jit(solution)/shard_map/rd,hd->rh/dot_general | solution.py:1148
  175.8 9.3 %multiply_reduce_fusion = (f32[1024]{0:T(1024)S(1)}, f32[528]{0:T(1024)S(1)}, f32[528]{0:T(1024)S(1)}, f32[1024]{0:T(1024)S(1)}, f32[528,1024]{1,0:T(8,128)S(1)}) fusion(f32[528,1024]{1,0:T(8,128)S(1)} %copy-done.5, f32[528]{0:T(1024)S(1)} %add_rsqrt_fusion.1, f32[528]{0:T(1024)S(1)} %broadcast_multiply_fusion.5, f32[1024]{0:T(1024)S(1)} %convert_element_type.129, ...), kind=kOutput, calls=%fused_computation.32 | convolution fusion | flops 4434048000 | bytes 17060096 | tf_op jit(solution)/shard_map/rh,dh->rd/dot_general | solution.py:1151
  185.2 2.4 convert_reduce_fusion.4
  187.6 4.0 convolution_convert_fusion.4.d_ref
  191.6 25.3 %to_heads.1.do_ref = bf16[4,528,256]{2,1,0:T(8,128)(2,1)} custom-call(bf16[528,1024]{1,0:T(8,128)(2,1)} %convolution_convert_fusion.4.d_ref), custom_call_target="tpu_custom_call" | custom-call | tf_op jit(solution)/shard_map/to_heads/pallas_call | solution.py:446
  216.9 52.0 %attend_backward.1 = bf16[4,528,768]{2,1,0:T(8,128)(2,1)} custom-call(s32[9]{0:T(128)} %pad_add_fusion.perm, bf16[8,256,512]{2,1,0:T(8,128)(2,1)} %get-tuple-element.37.q_ref, bf16[8,256,512]{2,1,0:T(8,128)(2,1)} %get-tuple-element.38.k_ref, bf16[8,256,512]{2,1,0:T(8,128)(2,1)} %get-tuple-element.39.v_ref, bf16[64,512]{1,0:T(8,128)(2,1)} %get-tuple-element.40.qc_ref, ...), custom_call_target="tpu_custom_call" | custom-call | flops 10000000000 | bytes 20000000 | tf_op jit(solution)/shard_map/attend_backward/pallas_call | solution.py:397
  270.4 7.2 %convolution_convert_fusion.2 = bf16[2112,1024]{1,0:T(8,128)(2,1)} fusion(bf16[2112,768]{1,0:T(8,128)(2,1)} %bitcast.56, bf16[1024,256]{1,0:T(8,128)(2,1)S(1)} %get-tuple-element.66, bf16[1024,256]{1,0:T(8,128)(2,1)S(1)} %get-tuple-element.67, bf16[1024,256]{1,0:T(8,128)(2,1)S(1)} %get-tuple-element.65), kind=kOutput, calls=%fused_computation.13 | convolution fusion | flops 3328770048 | bytes 9142272 | tf_op jit(solution)/shard_map/re,de->rd/dot_general | solution.py:1165
  277.5 49.7 %sum_rows.1 = f32[528,1024]{1,0:T(8,128)} custom-call(bf16[4,528,1024]{2,1,0:T(8,128)(2,1)} %bitcast.55), custom_call_target="tpu_custom_call" | custom-call | tf_op jit(solution)/shard_map/sum_rows/pallas_call | solution.py:446
  327.7 2.6 fusion.15
  330.4 2.5 convert_reduce_fusion.1
  334.7 11.7 %convolution_convert_fusion = bf16[1024,4096]{1,0:T(8,128)(2,1)} fusion(bf16[528,4096]{1,0:T(8,128)(2,1)} %copy-done.23, f32[528,1024]{1,0:T(8,128)} %copy-done.4, f32[1024]{0:T(1024)S(1)} %convert_element_type.130, f32[1024]{0:T(1024)S(1)} %convert_element_type.129, f32[528]{0:T(1024)S(1)} %add_rsqrt_fusion.1, f32[528]{0:T(1024)S(1)} %broadcast_multiply_fusion.5), kind=kOutput, calls=%fused_computation.10 | convolution fusion | flops 4436082688 | bytes 14889088 | tf_op jit(solution)/shard_map/rd,rh->dh/dot_general | solution.py:1178
  346.4 5.1 %bitcast_convert_fusion = bf16[1024,768]{1,0:T(8,128)(2,1)} fusion(bf16[4,528,1024]{2,1,0:T(8,128)(2,1)S(1)} %bitcast.84, bf16[4,528,768]{2,1,0:T(8,128)(2,1)S(1)} %copy-done.6), kind=kOutput, calls=%fused_computation.17 | convolution fusion | flops 3322675200 | bytes 9142272 | tf_op jit(solution)/shard_map/rd,re->de/dot_general | solution.py:1174
  351.5 4.9 convolution_convert_fusion.3
  356.5 9.3 %convolution_convert_fusion.1 = bf16[4096,1024]{1,0:T(8,128)(2,1)} fusion(bf16[528,4096]{1,0:T(8,128)(2,1)S(1)} %bitcast.86, bf16[4,1024]{1,0:T(4,128)(2,1)S(1)} %reshape.428, bf16[512,1024]{1,0:T(8,128)(2,1)S(1)} %bitcast.64, bf16[528]{0:T(1024)(128)(2,1)S(1)} %pad.20.clone), kind=kOutput, calls=%fused_computation.11 | convolution fusion | flops 4436623360 | bytes 13771808 | tf_op jit(solution)/shard_map/rh,rd->hd/dot_general | solution.py:1179
  365.8 120.3 %reduce_grads.1 = (f32[4,32,1024]{2,1,0:T(8,128)}, f32[32,4096]{1,0:T(8,128)}, f32[32,1024]{1,0:T(8,128)}, f32[32,3072]{1,0:T(8,128)}, f32[8,128]{1,0:T(8,128)}) custom-call(bf16[2,2,2,4,4,32,1024]{6,5,4,3,2,1,0:T(8,128)(2,1)} %bitcast.54, bf16[2,2,2,4,32,4096]{5,4,3,2,1,0:T(8,128)(2,1)} %bitcast.53, bf16[2,2,2,4,32,1024]{5,4,3,2,1,0:T(8,128)(2,1)} %bitcast.57, ...), custom_call_target="tpu_custom_call" | custom-call | tf_op jit(solution)/shard_map/reduce_grads/pallas_call | solution.py:446
  490.1 2.3 fusion.14
  494.5 10.0 %add_convert_fusion = bf16[528,1024]{1,0:T(8,128)(2,1)S(1)} fusion(f32[528,1024]{1,0:T(8,128)} %copy-done.4, bf16[528,4096]{1,0:T(8,128)(2,1)} %get-tuple-element.80, bf16[4096,1024]{1,0:T(8,128)(2,1)} %param.38, f32[1024]{0:T(1024)S(1)} %convert_element_type.134), kind=kOutput, calls=%fused_computation.35 | convolution fusion | flops 4430807040 | bytes 15962112 | tf_op jit(solution)/shard_map/dot_general | solution.py:1142
  507.0 1.6 copy.50
  (137 shorter events, 25.7 us)
Async XLA Ops:
  0.7 151.0 %copy-start = (bf16[1024,1024]{1,0:T(8,128)(2,1)S(1)}, bf16[1024,1024]{1,0:T(8,128)(2,1)}, u32[]{:S(2)}) copy-start(bf16[1024,1024]{1,0:T(8,128)(2,1)} %param.32) | copy-start | bytes 6291460
  0.7 63.4 %copy-start.17 = (bf16[1024]{0:T(1024)(128)(2,1)S(1)}, bf16[1024]{0:T(1024)(128)(2,1)}, u32[]{:S(2)}) copy-start(bf16[1024]{0:T(1024)(128)(2,1)} %param.28) | copy-start | bytes 6148
  0.7 64.0 %copy-start.16 = (bf16[3072]{0:T(1024)(128)(2,1)S(1)}, bf16[3072]{0:T(1024)(128)(2,1)}, u32[]{:S(2)}) copy-start(bf16[3072]{0:T(1024)(128)(2,1)} %param.31) | copy-start | bytes 18436
  0.7 64.6 %copy-start.18 = (bf16[1024]{0:T(1024)(128)(2,1)S(1)}, bf16[1024]{0:T(1024)(128)(2,1)}, u32[]{:S(2)}) copy-start(bf16[1024]{0:T(1024)(128)(2,1)} %param.29) | copy-start | bytes 6148
  124.6 27.0 %copy-start.19 = (bf16[1024]{0:T(1024)(128)(2,1)S(1)}, bf16[1024]{0:T(1024)(128)(2,1)}, u32[]{:S(2)}) copy-start(bf16[1024]{0:T(1024)(128)(2,1)} %param.33) | copy-start | bytes 6148
  124.6 27.1 %copy-start.2 = (bf16[528,1024]{1,0:T(8,128)(2,1)S(1)}, bf16[528,1024]{1,0:T(8,128)(2,1)}, u32[]{:S(2)}) copy-start(bf16[528,1024]{1,0:T(8,128)(2,1)} %get-tuple-element.64.x_ref) | copy-start | bytes 3244036
  151.7 3.8 slice-start.1
  154.5 9.8 %copy-start.4 = (f32[528,1024]{1,0:T(8,128)}, f32[528,1024]{1,0:T(8,128)S(1)}, u32[]{:S(2)}) copy-start(f32[528,1024]{1,0:T(8,128)S(1)} %get-tuple-element.79) | copy-start | bytes 6488068
  155.4 8.9 %copy-start.15 = (bf16[1,2,2,1024]{3,2,1,0:T(2,128)(2,1)S(1)}, bf16[1,2,2,1024]{3,2,1,0:T(2,128)(2,1)}, u32[]{:S(2)}) copy-start(bf16[1,2,2,1024]{3,2,1,0:T(2,128)(2,1)} %param.25) | copy-start | bytes 24580
  164.3 11.5 %copy-start.5 = (f32[528,1024]{1,0:T(8,128)S(1)}, f32[528,1024]{1,0:T(8,128)}, u32[]{:S(2)}) copy-start(f32[528,1024]{1,0:T(8,128)} %copy-done.4) | copy-start | bytes 6488068
  175.8 9.4 %copy-start.23 = (bf16[528,4096]{1,0:T(8,128)(2,1)}, bf16[528,4096]{1,0:T(8,128)(2,1)S(1)}, u32[]{:S(2)}) copy-start(bf16[528,4096]{1,0:T(8,128)(2,1)S(1)} %get-tuple-element.84) | copy-start | bytes 12976132
  175.8 9.4 %copy-start.8 = (bf16[1,8,64,1024]{3,2,1,0:T(8,128)(2,1)S(1)}, bf16[1,8,64,1024]{3,2,1,0:T(8,128)(2,1)}, u32[]{:S(2)}) copy-start(bf16[1,8,64,1024]{3,2,1,0:T(8,128)(2,1)} %param.24) | copy-start | bytes 3145732
  277.5 50.2 %copy-start.13 = (f32[1024]{0:T(1024)S(1)}, f32[1024]{0:T(1024)}, u32[]{:S(2)}) copy-start(f32[1024]{0:T(1024)} %convert_element_type.125) | copy-start | bytes 12292
  330.4 15.9 %slice-start.2 = ((s8[4325376]{0:T(1024)(128)(4,1)}), s8[131072]{0:T(1024)(128)(4,1)S(1)}, s32[]{:S(2)}) async-start(s8[4325376]{0:T(1024)(128)(4,1)} %bitcast.83), calls=%async_computation.2 | async-start | bytes 262144
  334.7 11.7 %copy-start.6 = (bf16[4,528,768]{2,1,0:T(8,128)(2,1)S(1)}, bf16[4,528,768]{2,1,0:T(8,128)(2,1)}, u32[]{:S(2)}) copy-start(bf16[4,528,768]{2,1,0:T(8,128)(2,1)} %attend_backward.1) | copy-start | bytes 9732100
  334.7 11.7 %slice-start.3 = ((s8[4325376]{0:T(1024)(128)(4,1)}), s8[4194304]{0:T(1024)(128)(4,1)S(1)}, s32[]{:S(2)}) async-start(s8[4325376]{0:T(1024)(128)(4,1)} %bitcast.83), calls=%async_computation.3 | async-start | bytes 8388608
  346.4 5.1 %copy-start.7 = (bf16[528,1024]{1,0:T(8,128)(2,1)S(1)}, bf16[528,1024]{1,0:T(8,128)(2,1)}, u32[]{:S(2)}) copy-start(bf16[528,1024]{1,0:T(8,128)(2,1)} %to_owner.1) | copy-start | bytes 3244036
  346.4 10.1 %slice-start.4 = ((s8[4325376]{0:T(1024)(128)(4,1)}), s8[131072]{0:T(1024)(128)(4,1)S(1)}, s32[]{:S(2)}) async-start(s8[4325376]{0:T(1024)(128)(4,1)} %bitcast.85), calls=%async_computation.4 | async-start | bytes 262144
  351.5 5.0 copy-start.9
  351.5 5.0 slice-start.5
  365.8 124.3 %copy-start.3 = (f32[528,1024]{1,0:T(8,128)S(1)}, f32[528,1024]{1,0:T(8,128)}, u32[]{:S(2)}) copy-start(f32[528,1024]{1,0:T(8,128)} %sum_rows.1) | copy-start | bytes 6488068
  494.5 15.6 %copy-start.1 = (bf16[1024,1024]{1,0:T(8,128)(2,1)S(1)}, bf16[1024,1024]{1,0:T(8,128)(2,1)}, u32[]{:S(2)}) copy-start(bf16[1024,1024]{1,0:T(8,128)(2,1)} %param.32) | copy-start | bytes 6291460
  504.6 4.0 copy-start.11
  504.6 4.8 copy-start.10
  (6 other events, 9.7 us)

commit v3 on v0

v3 whole, which is shorter than its diff:
```python
import functools
import math

import jax
import jax.numpy as jnp
import numpy as np
from jax import lax
from jax.experimental import pallas as pl
from jax.experimental.pallas import tpu as pltpu
from jax.sharding import PartitionSpec as P

D = 1024
HEADS = 16
HEAD_DIM = 64
GRID = 16
COND = 2
FRAMES = 8
MOST = 5
MIDDLE = 7
STREAMS = 4
GROUP = 4
GW = GROUP * HEAD_DIM
PART = 64
PATCHES = 256
VIS = FRAMES * PART
CROWS = 16
ROWS = VIS + CROWS
WIDE = GROUP * 128
NEG = -1e30
EPS = 1e-06
F32 = jnp.float32
BF16 = jnp.bfloat16
VM = pltpu.VMEM
FULL = pl.BlockSpec(memory_space=pltpu.VMEM)
ANYM = pl.BlockSpec(memory_space=pltpu.HBM)
LIMIT = 60 * 1024 * 1024


def nn(a, b):
    return lax.dot_general(a, b, (((1,), (0,)), ((), ())), preferred_element_type=F32)


def nt(a, b):
    return lax.dot_general(a, b, (((1,), (1,)), ((), ())), preferred_element_type=F32)


def rope_constants():
    pair = np.arange(HEAD_DIM // 2)
    exponent = np.where(pair < 30, (pair % 10) / 10.0, 0.0).astype(np.float32)
    freq = np.exp(-math.log(10000.0) * exponent).astype(np.float32)
    patch = np.arange(PATCHES)
    slot_time = np.array([0, 1, 2, 3, 4, 0, 1, 0])
    is_time = (pair < 10)[None, :]
    place = np.where(
        (pair >= 20)[None, :], (patch % GRID)[:, None], (patch // GRID)[:, None]
    ) * ((pair >= 10) & (pair < 30))[None, :]
    angle_patch = (place * freq[None, :]).astype(np.float32)
    angle_time = (slot_time[:, None] * freq[None, :]).astype(np.float32)
    cos_patch = np.where(is_time, 0.0, np.cos(angle_patch))
    sin_patch = np.where(is_time, 0.0, np.sin(angle_patch))
    cos_time = np.where(is_time, np.cos(angle_time), 0.0)
    sin_time = np.where(is_time, np.sin(angle_time), 0.0)

    def spread(table, signed):
        two = np.repeat(table, 2, axis=1)
        if signed:
            two = two * np.where(np.arange(HEAD_DIM) % 2 == 0, -1.0, 1.0)[None, :]
        return np.tile(two, (1, GROUP)).astype(np.float32)

    return (
        spread(cos_patch, False),
        spread(sin_patch, True),
        spread(cos_time, False),
        spread(sin_time, True),
    )


def swap_pairs(v):
    lane = lax.broadcasted_iota(jnp.int32, v.shape, 1)
    width = v.shape[1]
    return jnp.where(lane % 2 == 0, pltpu.roll(v, width - 1, 1), pltpu.roll(v, 1, 1))


def turn(v, cosine, sine):
    return v * cosine + swap_pairs(v) * sine


def pad_heads(t, extra):
    pieces = []
    for h in range(GROUP):
        pieces += [t[:, h * HEAD_DIM : (h + 1) * HEAD_DIM], extra]
    return jnp.concatenate(pieces, axis=1)


def pad_right(t):
    extra = jnp.zeros((t.shape[0], HEAD_DIM), t.dtype)
    pieces = []
    for h in range(GROUP):
        pieces += [extra, t[:, h * HEAD_DIM : (h + 1) * HEAD_DIM]]
    return jnp.concatenate(pieces, axis=1)


def unpad_heads(t):
    return jnp.concatenate([t[:, h * 128 : h * 128 + HEAD_DIM] for h in range(GROUP)], axis=1)


def head(t, h):
    return t[:, h * 128 : (h + 1) * 128]


def first_slot(i):
    return jnp.where(i < MOST, 0, jnp.where(i < MIDDLE, MOST, MIDDLE))


def cond_tables(cs_col, ct, st):
    cosine = jnp.zeros((PART, GW), F32)
    sine = jnp.zeros((PART, GW), F32)
    for j in range(FRAMES):
        here = cs_col == j
        cosine = cosine + jnp.where(here, ct[j : j + 1, :], 0.0)
        sine = sine + jnp.where(here, st[j : j + 1, :], 0.0)
    lane = lax.broadcasted_iota(jnp.int32, (PART, GW), 1) % HEAD_DIM
    return jnp.where(lane < 20, cosine, 1.0), sine


def read_meta(meta_ref):
    bias_t = jnp.transpose(meta_ref[0:FRAMES])
    cs_row = meta_ref[FRAMES : FRAMES + 1, 0:PART].astype(jnp.int32)
    cs_col = jnp.transpose(meta_ref[FRAMES:, :])[0:PART, 0:1].astype(jnp.int32)
    return cs_col, cs_row, bias_t


def place_kernel(perm, xv_ref, xc_ref, dv_ref, dc_ref, x_ref, dy_ref, sem):
    copies = []
    for n, (rows, out) in enumerate(((xv_ref, x_ref), (dv_ref, dy_ref))):
        for i in range(FRAMES):
            copies.append(pltpu.make_async_copy(rows.at[perm[i]], out.at[pl.ds(i * PART, PART)], sem.at[n, i]))
    for copy in copies:
        copy.start()
    for extra, out in ((xc_ref, x_ref), (dc_ref, dy_ref)):
        out[VIS:, :] = jnp.zeros((CROWS, D), BF16)
        out[VIS : VIS + extra.shape[0], :] = extra[...]
    for copy in copies:
        copy.wait()


def place_rows(perm, visual, extra, d_visual, d_extra):
    return pl.pallas_call(
        place_kernel,
        name="place_rows",
        out_shape=(jax.ShapeDtypeStruct((ROWS, D), BF16),) * 2,
        in_specs=[pl.BlockSpec(memory_space=pltpu.SMEM), ANYM, FULL, ANYM, FULL],
        out_specs=(FULL, FULL),
        scratch_shapes=[pltpu.SemaphoreType.DMA((2, FRAMES))],
    )(perm, visual.reshape(FRAMES, PART, D), extra.reshape(-1, D), d_visual.reshape(FRAMES, PART, D), d_extra.reshape(-1, D))


def restore_kernel(slot, y_ref, g_ref, yo_ref, go_ref, sem):
    copies = []
    for f in range(FRAMES):
        rows = pl.ds(pl.multiple_of(slot[f] * PART, PART), PART)
        copies.append(pltpu.make_async_copy(y_ref.at[rows], yo_ref.at[f], sem.at[0, f]))
        copies.append(pltpu.make_async_copy(g_ref.at[rows], go_ref.at[f], sem.at[1, f]))
    for copy in copies:
        copy.start()
    for copy in copies:
        copy.wait()


def restore_rows(slot, y, g):
    shape = (FRAMES, PART, D)
    return pl.pallas_call(
        restore_kernel,
        name="restore_rows",
        out_shape=(jax.ShapeDtypeStruct(shape, BF16), jax.ShapeDtypeStruct(shape, F32)),
        in_specs=[pl.BlockSpec(memory_space=pltpu.SMEM), ANYM, ANYM],
        out_specs=(FULL, FULL),
        scratch_shapes=[pltpu.SemaphoreType.DMA((2, FRAMES))],
    )(slot, y, g)


def where_am_i():
    d, z = lax.axis_index("dp"), lax.axis_index("stream")
    return d // 2, d % 2, z // 2, z % 2, z


def greet_column():
    p, c, q, r, z = where_am_i()
    barrier = pltpu.get_barrier_semaphore()
    for core in range(2):
        for chip in range(STREAMS):
            @pl.when((core != c) | (chip != z))
            def _():
                pl.semaphore_signal(
                    barrier, inc=1, device_id=(2 * p + core, chip),
                    device_id_type=pl.DeviceIdType.MESH,
                )
    pl.semaphore_wait(barrier, 2 * STREAMS - 1)


def remote(src, dst, send, recv, device):
    return pltpu.make_async_remote_copy(
        src_ref=src, dst_ref=dst, send_sem=send, recv_sem=recv, device_id=device,
        device_id_type=pl.DeviceIdType.MESH,
    )


def comm_call(kernel, name, ident, outs, scratch, far, close=(), near_outs=()):
    return pl.pallas_call(
        kernel,
        name=name,
        out_shape=tuple(jax.ShapeDtypeStruct(s, t) for s, t in tuple(outs) + tuple(near_outs)),
        in_specs=[ANYM] * len(far) + [FULL] * len(close),
        out_specs=tuple(ANYM for _ in outs) + tuple(FULL for _ in near_outs),
        scratch_shapes=scratch,
        compiler_params=pltpu.CompilerParams(
            collective_id=ident, has_side_effects=True, vmem_limit_bytes=LIMIT
        ),
    )(*far, *close)


def dma(*shape):
    return pltpu.SemaphoreType.DMA(shape)


HALF = VIS // 2


PIECE = HALF // 2


def forward_kernel(
    x_hbm, w_hbm, m_hbm, par_ref, cg_ref, sg_ref, ct_ref, st_ref,
    att_ref, xa_out, a_out, q_out, k_out, v_out, o_out,
    meta_ref, qc_ref, kc_ref, vc_ref, lse_ref, lsec_ref,
    xa, a_ref, q_ref, k_ref, v_ref, o_ref, vt_ref, w, bias_ref,
    isem, whole_s, whole_r, far_s, far_r, pass_s, near_s, near_r, tail_s, tail_r, msem, out_s, out_r, out_l, keep,
):
    p, c, q, r, z = where_am_i()
    group = 2 * r + c
    in_pair = q == c
    away = q != c
    inner = z == 1 + q
    z_one, z_two, z_three = z + 1 - 2 * r, z + 2 - 4 * q, STREAMS - 1 - z
    other = (2 * p + 1 - c, z)
    across = (2 * p + c, z_one)
    loads = []
    for part in range(3):
        cols = pl.ds(pl.multiple_of(part * D + group * GW, GW), GW)
        loads.append(pltpu.make_async_copy(w_hbm.at[:, cols], w.at[part], isem.at[part]))
    for copy in loads:
        copy.start()
    own_rows = pltpu.make_async_copy(x_hbm, xa.at[z], isem.at[3])

    @pl.when(in_pair)
    def _():
        own_rows.start()

    greet_column()
    tail = pl.ds(VIS, CROWS)

    def piece(half, g):
        return pl.ds(pl.multiple_of(half * HALF + g * PIECE, PIECE), PIECE)

    def whole_copy():
        return remote(x_hbm, xa.at[z], whole_s, whole_r, other)

    def far_copy(half, g):
        rows = piece(half, g)
        return remote(x_hbm.at[rows], xa.at[z, rows], far_s.at[half, g], far_r.at[z, g], (2 * p + half, 1 + c))

    def own_pass(g):
        rows = piece(c, g)
        return remote(x_hbm.at[rows], xa.at[z, rows], pass_s.at[z, g], far_r.at[z, g], across)

    def far_pass(s, g):
        rows = piece(c, g)
        return remote(xa.at[s, rows], xa.at[s, rows], pass_s.at[s, g], far_r.at[s, g], across)

    def near_copy(s, g, half):
        rows = piece(half, g)
        return remote(xa.at[s, rows], xa.at[s, rows], near_s.at[s, g], near_r.at[s, g], other)

    def tail_copy(half, side):
        n = half * 2 + side
        return remote(x_hbm.at[tail], xa.at[z, tail], tail_s.at[n], tail_r.at[z], (2 * p + half, 2 * c + side))

    def tail_needed(half, side):
        return jnp.logical_not((2 * c + side == z))

    def meta_copy():
        return remote(m_hbm, meta_ref, msem.at[0], msem.at[1], other)

    def meta_own():
        return pltpu.make_async_copy(m_hbm, meta_ref, msem.at[2])

    @pl.when(in_pair)
    def _():
        meta_own().start()
        meta_copy().start()
        whole_copy().start()
        own_pass(0).start()
        own_pass(1).start()

    for half in range(2):
        @pl.when(away)
        def _():
            far_copy(half, 0).start()

        for side in range(2):
            @pl.when(tail_needed(half, side))
            def _():
                tail_copy(half, side).start()

    def arrive(s, g, relay):
        far_pass(s, g).wait_recv()
        near_copy(s, g, c).start()
        if relay:
            @pl.when(inner)
            def _():
                far_pass(s, g).start()

    gain, shift = par_ref[0:1], par_ref[1:2]
    cut = pl.ds(pl.multiple_of(group * GW, GW), GW)
    lane64 = lax.broadcasted_iota(jnp.int32, (PATCHES, 64), 1)
    one = jnp.where(lane64 == 0, 1.0, 0.0).astype(BF16)

    def project(x, cosine, sine):
        x = x.astype(F32)
        centre = x - jnp.mean(x, axis=1, keepdims=True)
        spread = jnp.mean(centre * centre, axis=1, keepdims=True)
        a = (centre * lax.rsqrt(spread + EPS) * gain + shift).astype(BF16)
        q = turn(nn(a, w[0]) + par_ref[2:3, cut], cosine, sine)
        k = turn(nn(a, w[1]) + par_ref[3:4, cut], cosine, sine)
        v = (nn(a, w[2]) + par_ref[4:5, cut]).astype(BF16)
        return a, (q.astype(BF16).astype(F32) * 0.125).astype(BF16), k.astype(BF16), v

    def unit(t, carry):
        @pl.when(t == 0)
        def _():
            for copy in loads:
                copy.wait()

            @pl.when(in_pair)
            def _():
                own_rows.wait()
                meta_own().wait()

            @pl.when(away)
            def _():
                whole_copy().wait_recv()
                far_pass(z, 0).start()
                far_pass(z, 1).start()
                meta_copy().wait_recv()

            bias_ref[...] = jnp.transpose(meta_ref[0:FRAMES])

        @pl.when(t == 2)
        def _():
            arrive(z_one, 0, False)
            arrive(z_one, 1, False)

            @pl.when(away)
            def _():
                for half in range(2):
                    far_copy(half, 0).wait_send()
                    far_copy(half, 1).start()

            arrive(z_two, 0, True)
            arrive(z_three, 0, True)
            near_copy(z_one, 0, 1 - c).wait_recv()
            near_copy(z_one, 1, 1 - c).wait_recv()

        @pl.when(t == 4)
        def _():
            near_copy(z_two, 0, 1 - c).wait_recv()
            near_copy(z_three, 0, 1 - c).wait_recv()

        @pl.when(t == 6)
        def _():
            arrive(z_two, 1, True)
            arrive(z_three, 1, True)
            near_copy(z_two, 1, 1 - c).wait_recv()
            near_copy(z_three, 1, 1 - c).wait_recv()

        g = jnp.where(t < 4, t % 2, (t - 4) // 2)
        s = jnp.where(t < 2, z, jnp.where(t < 4, z_one, jnp.where(t % 2 == 0, z_two, z_three)))
        x = jnp.concatenate([xa[s, piece(0, g)], xa[s, piece(1, g)]], axis=0)
        place = pl.ds(pl.multiple_of(s * PART, PART), PART)
        cosine, sine, bias = [], [], []
        ids = lax.broadcasted_iota(jnp.int32, (PART, FRAMES), 1)
        for n in range(4):
            i = 2 * g + n % 2 + 4 * (n // 2)
            cosine.append(cg_ref[place] + ct_ref[pl.ds(i, 1), :])
            sine.append(sg_ref[place] + st_ref[pl.ds(i, 1), :])
            bias.append(jnp.sum(jnp.where(ids == i, bias_ref[place], 0.0), axis=1, keepdims=True))
        a, qs, ks, vs = project(x, jnp.concatenate(cosine, axis=0), jnp.concatenate(sine, axis=0))
        a_ref[s, piece(0, g)] = a[:PIECE]
        a_ref[s, piece(1, g)] = a[PIECE:]
        bias = jnp.concatenate(bias, axis=0)
        qs = pad_heads(qs, one)
        ks = pad_heads(ks, jnp.where(lane64 == 0, bias, 0.0).astype(BF16))
        vs = pad_right(vs)
        for n in range(4):
            i = 2 * g + n % 2 + 4 * (n // 2)
            rows = slice(n * PART, (n + 1) * PART)
            q_ref[i, place] = qs[rows]
            k_ref[i, place] = ks[rows]
            v_ref[i, place] = vs[rows]
        return carry

    lax.fori_loop(0, 8, unit, 0)

    for s in range(STREAMS):
        @pl.when(s != z)
        def _():
            remote(x_hbm.at[tail], xa.at[s, tail], tail_s.at[0], tail_r.at[s], other).wait_recv()
    cs_col, cs_row, _ = read_meta(meta_ref)
    a, qs, ks, vs = project(xa[:, VIS:, :].reshape(PART, D), *cond_tables(cs_col, ct_ref[...], st_ref[...]))
    a_ref[:, VIS:, :] = a.reshape(STREAMS, CROWS, D)
    qc_ref[...] = pad_heads(qs, one[:PART])
    kc_ref[...] = pad_heads(ks, jnp.zeros((PART, 64), BF16))
    vc_ref[...] = pad_right(vs)
    vct = jnp.transpose(vs.astype(F32)).astype(BF16)
    saves = [(xa, xa_out), (a_ref, a_out), (q_ref, q_out), (k_ref, k_out), (v_ref, v_out)]
    saves = [pltpu.make_async_copy(src, dst, keep.at[n]) for n, (src, dst) in enumerate(saves)]
    for copy in saves:
        copy.start()

    def out_rows(i):
        return pl.ds(pl.multiple_of(i * PART, PART), PART)

    def out_copy(s, n, rows):
        place = pl.ds(pl.multiple_of(group * GW, GW), GW)
        return remote(o_ref.at[s, rows], att_ref.at[rows, place], out_s.at[s, n], out_r.at[group, n], (2 * p + q, s))

    def out_own(s, n, rows):
        place = pl.ds(pl.multiple_of(group * GW, GW), GW)
        return pltpu.make_async_copy(o_ref.at[s, rows], att_ref.at[rows, place], out_l.at[n])

    def send_out(n, rows):
        for s in range(STREAMS):
            mine = in_pair & (s == z)

            @pl.when(mine)
            def _():
                out_own(s, n, rows).start()

            @pl.when(jnp.logical_not(mine))
            def _():
                out_copy(s, n, rows).start()

    def slot(i, carry):
        vt_ref[i] = jnp.transpose(unpad_right(v_ref[i].astype(F32))).astype(BF16)
        low = first_slot(i)
        near = (cs_col >= low) & (cs_col <= i)
        tops, totals, blends = [], [], []
        for h in range(GROUP):
            s = jnp.where(near, nt(head(kc_ref, h), q_ref[i, :, h * 128 : (h + 1) * 128]), NEG)
            top = jnp.max(s, axis=0, keepdims=True)
            pt = jnp.exp(s - top)
            tops.append(top)
            totals.append(jnp.sum(pt, axis=0, keepdims=True))
            blends.append(nn(vct[h * HEAD_DIM : (h + 1) * HEAD_DIM], pt.astype(BF16)))

        def step(j, state):
            tops, totals, blends = state
            new = ([], [], [])
            for h in range(GROUP):
                s = nt(k_ref[j, :, h * 128 : (h + 1) * 128], q_ref[i, :, h * 128 : (h + 1) * 128])
                top = jnp.maximum(tops[h], jnp.max(s, axis=0, keepdims=True))
                pt = jnp.exp(s - top)
                stay = jnp.exp(tops[h] - top)
                new[0].append(top)
                new[1].append(totals[h] * stay + jnp.sum(pt, axis=0, keepdims=True))
                vt = vt_ref[j, h * HEAD_DIM : (h + 1) * HEAD_DIM, :]
                new[2].append(blends[h] * stay + nn(vt, pt.astype(BF16)))
            return new

        tops, totals, blends = lax.fori_loop(low, i + 1, step, (tops, totals, blends))
        o = jnp.transpose(jnp.concatenate([blends[h] / totals[h] for h in range(GROUP)], axis=0))
        o_ref[:, out_rows(i), :] = o.astype(BF16).reshape(STREAMS, PART, GW)
        lse_ref[i] = jnp.concatenate([tops[h] + jnp.log(totals[h]) for h in range(GROUP)] * 2, axis=0)
        send_out(i, out_rows(i))
        return carry

    lo_col = first_slot(cs_col)

    def cond_queries():
        near = (cs_row >= lo_col) & (cs_row <= cs_col)
        tops, totals, blends = [], [], []
        for h in range(GROUP):
            s = jnp.where(near, nt(head(qc_ref, h), head(kc_ref, h)), NEG)
            top = jnp.max(s, axis=1, keepdims=True)
            pt = jnp.exp(s - top)
            tops.append(top)
            totals.append(jnp.sum(pt, axis=1, keepdims=True))
            blends.append(nn(pt.astype(BF16), head(vc_ref, h)))

        def cond_step(j, state):
            tops, totals, blends = state
            near = (lo_col <= j) & (cs_col >= j)
            new = ([], [], [])
            for h in range(GROUP):
                s = nt(head(qc_ref, h), k_ref[j, :, h * 128 : (h + 1) * 128])
                s = jnp.where(near, s, NEG)
                top = jnp.maximum(tops[h], jnp.max(s, axis=1, keepdims=True))
                pt = jnp.exp(s - top)
                stay = jnp.exp(tops[h] - top)
                new[0].append(top)
                new[1].append(totals[h] * stay + jnp.sum(pt, axis=1, keepdims=True))
                new[2].append(blends[h] * stay + nn(pt.astype(BF16), v_ref[j, :, h * 128 : (h + 1) * 128]))
            return new

        tops, totals, blends = lax.fori_loop(0, FRAMES, cond_step, (tops, totals, blends))
        o = jnp.concatenate([(blends[h] / totals[h])[:, HEAD_DIM:] for h in range(GROUP)], axis=1)
        o_ref[:, VIS:, :] = o.astype(BF16).reshape(STREAMS, CROWS, GW)
        lane = lax.broadcasted_iota(jnp.int32, (PART, 128), 1)
        lsec = jnp.zeros((PART, 128), F32)
        for h in range(GROUP):
            lsec = lsec + jnp.where(lane == h, tops[h] + jnp.log(totals[h]), 0.0)
        lsec_ref[...] = lsec
        send_out(FRAMES, tail)

    cond_queries()
    lax.fori_loop(0, FRAMES, slot, 0)
    last = pltpu.make_async_copy(o_ref, o_out, keep.at[5])
    last.start()

    def settle(n, rows):
        for s in range(STREAMS):
            mine = in_pair & (s == z)

            @pl.when(mine)
            def _():
                out_own(s, n, rows).wait()

            @pl.when(jnp.logical_not(mine))
            def _():
                out_copy(s, n, rows).wait_send()
        for g in range(4):
            @pl.when((g % 2 != c) | (2 * c + g // 2 != z))
            def _():
                place = pl.ds(g * GW, GW)
                remote(o_ref.at[0, rows], att_ref.at[rows, place], out_s.at[0, n], out_r.at[g, n], other).wait_recv()

    def settle_slot(i, carry):
        settle(i, out_rows(i))
        return carry

    lax.fori_loop(0, FRAMES, settle_slot, 0)
    settle(FRAMES, tail)

    @pl.when(in_pair)
    def _():
        meta_copy().wait_send()
        whole_copy().wait_send()
        own_pass(0).wait_send()
        own_pass(1).wait_send()

    @pl.when(away)
    def _():
        far_pass(z, 0).wait_send()
        far_pass(z, 1).wait_send()
        far_copy(0, 1).wait_send()
        far_copy(1, 1).wait_send()

    for half in range(2):
        for side in range(2):
            @pl.when(tail_needed(half, side))
            def _():
                tail_copy(half, side).wait_send()
    for g in range(2):
        for s in (z_one, z_two, z_three):
            near_copy(s, g, c).wait_send()
        for s in (z_two, z_three):
            @pl.when(inner)
            def _():
                far_pass(s, g).wait_send()
    for copy in saves:
        copy.wait()
    last.wait()


def attend_forward(x, w_qkv, meta, params, tables):
    def v16(*shape):
        return VM(shape, BF16)

    wide = (FRAMES, PATCHES, WIDE)
    rows = (STREAMS, ROWS, D)
    outs = (
        ((ROWS, D), BF16), (rows, BF16), (rows, BF16), (wide, BF16), (wide, BF16), (wide, BF16),
        ((STREAMS, ROWS, GW), BF16),
    )
    near_outs = (
        (meta.shape, F32), ((PART, WIDE), BF16), ((PART, WIDE), BF16), ((PART, WIDE), BF16),
        ((FRAMES, 8, PATCHES), F32), ((PART, 128), F32),
    )
    scratch = [
        v16(*rows), v16(*rows), v16(*wide), v16(*wide), v16(*wide), v16(STREAMS, ROWS, GW), v16(FRAMES, GW, PATCHES),
        v16(3, D, GW), VM((PATCHES, FRAMES), F32),
        dma(4), pltpu.SemaphoreType.DMA, pltpu.SemaphoreType.DMA, dma(2, 2), dma(4, 2), dma(4, 2), dma(4, 2), dma(4, 2),
        dma(4), dma(4), dma(3), dma(4, 9), dma(4, 9), dma(9), dma(6),
    ]
    return comm_call(
        forward_kernel, "attend_forward", 0, outs, scratch, (x, w_qkv, meta), (params,) + tables, near_outs
    )
CHUNKS = 9
CUT = D // 2
QCUT = 3 * GW // 2


def add_up(*terms):
    total = terms[0].astype(F32)
    for t in terms[1:]:
        total = total + t.astype(F32)
    return total


def grid_shape():
    cores = lax.axis_size("dp") // 2
    nx = 1 << ((cores.bit_length() - 1) // 2)
    return nx, cores // nx, D // (cores * 2 * STREAMS)


class Place:
    def __init__(self, nx, ny):
        d, z = lax.axis_index("dp"), lax.axis_index("stream")
        self.nx, self.ny, self.d, self.z = nx, ny, d, z
        self.p, self.c, self.hi, self.lo = d // 2, d % 2, z // 2, z % 2
        self.x, self.y = self.p % nx, self.p // nx
        self.near = (d + 1 - 2 * self.c, z)
        self.z_one = (d, z + 1 - 2 * self.lo)
        self.z_two = (d, z + 2 - 4 * self.hi)
        self.slant = (d + 1 - 2 * self.c, z + 1 - 2 * self.lo)

    def along_x(self, n):
        return lax.rem(self.x + n, self.nx)

    def along_y(self, n):
        return lax.rem(self.y + n, self.ny)

    def x_device(self, n):
        return ((self.y * self.nx + self.along_x(n)) * 2 + self.c, self.z)

    def y_device(self, n):
        return ((self.along_y(n) * self.nx + self.x) * 2 + self.c, self.z)

    def greet(self):
        barrier = pltpu.get_barrier_semaphore()
        p, c, z, nx, ny = self.p, self.c, self.z, self.nx, self.ny
        for core in range(2):
            for chip in range(STREAMS):
                @pl.when((core != c) | (chip != z))
                def _():
                    pl.semaphore_signal(
                        barrier, inc=1, device_id=(2 * p + core, chip), device_id_type=pl.DeviceIdType.MESH
                    )
        others = [self.x_device(n) for n in range(1, nx)] + [self.y_device(n) for n in range(1, ny)]
        for device in others:
            pl.semaphore_signal(barrier, inc=1, device_id=device, device_id_type=pl.DeviceIdType.MESH)
        pl.semaphore_wait(barrier, 2 * STREAMS - 1 + len(others))


class Reducer:
    def __init__(self, at, rb, count, sources, refs):
        self.at, self.rb, self.count, self.sources = at, rb, count, sources
        (self.mine, self.rd, self.r2a, self.r2b, self.r3a, self.r3b, self.s3, self.r4, self.s4, self.r5, self.fin,
         self.lsem, self.ds, self.dr, self.as2, self.ar2, self.bs2, self.br2, self.as3, self.ar3, self.bs3, self.br3,
         self.s4s, self.s4r, self.s5s, self.s5r) = refs

    @staticmethod
    def scratch(n, nx, ny, rb):
        def v(*shape):
            return VM(shape, BF16)

        return [
            v(n, ny, nx, STREAMS, rb, D), v(n, ny, nx, STREAMS, rb, D),
            v(n, nx - 1, ny, STREAMS, rb, CUT), v(n, ny - 1, nx, STREAMS, rb, CUT),
            v(n, ny - 1, STREAMS, rb, CUT), v(n, nx - 1, STREAMS, rb, CUT),
            v(n, 2, 2, rb, D), v(n, 2, rb, D), v(n, 2, rb, D), v(n, rb, D), VM((n, rb, D), F32),
            dma(n), dma(n), dma(n),
            dma(n, nx - 1), dma(n, nx - 1), dma(n, ny - 1), dma(n, ny - 1),
            dma(n, ny - 1), dma(n, ny - 1), dma(n, nx - 1), dma(n, nx - 1),
            dma(n), dma(n), dma(n), dma(n),
        ]

    def issue(self, k):
        c = self.at.c
        begin = 0
        for size, get in self.sources:
            start = begin
            begin += size

            @pl.when((k >= start) & (k < start + size))
            def _():
                t = k - start
                remote(get(t, 1 - c), self.rd.at[k], self.ds.at[k], self.dr.at[k], self.at.near).start()
                pltpu.make_async_copy(get(t, c), self.mine.at[k], self.lsem.at[k]).start()

    def core(self, k):
        return remote(self.rd.at[k], self.rd.at[k], self.ds.at[k], self.dr.at[k], self.at.near)

    def a2(self, k, n):
        at = self.at
        src = self.mine.at[k, :, at.along_x(n), :, :, pl.ds(0, CUT)]
        return remote(src, self.r2a.at[k, n - 1], self.as2.at[k, n - 1], self.ar2.at[k, n - 1], at.x_device(n))

    def b2(self, k, n):
        at = self.at
        src = self.mine.at[k, at.along_y(n), :, :, :, pl.ds(CUT, CUT)]
        return remote(src, self.r2b.at[k, n - 1], self.bs2.at[k, n - 1], self.br2.at[k, n - 1], at.y_device(n))

    def a3(self, k, n):
        at = self.at
        src = self.r2a.at[k, 0, at.along_y(n)]
        return remote(src, self.r3a.at[k, n - 1], self.as3.at[k, n - 1], self.ar3.at[k, n - 1], at.y_device(n))

    def b3(self, k, n):
        at = self.at
        src = self.r2b.at[k, 0, at.along_x(n)]
        return remote(src, self.r3b.at[k, n - 1], self.bs3.at[k, n - 1], self.br3.at[k, n - 1], at.x_device(n))

    def c4(self, k):
        return remote(self.s3.at[k, :, 1 - self.at.lo], self.r4.at[k], self.s4s.at[k], self.s4r.at[k], self.at.z_one)

    def c5(self, k):
        return remote(self.s4.at[k, 1 - self.at.hi], self.r5.at[k], self.s5s.at[k], self.s5r.at[k], self.at.z_two)

    def tick(self, t, carry=0):
        at, rb, count = self.at, self.rb, self.count
        nx, ny, x, y = at.nx, at.ny, at.x, at.y

        @pl.when(t < count)
        def _():
            k = t
            pltpu.make_async_copy(self.rd.at[k], self.mine.at[k], self.lsem.at[k]).wait()
            self.core(k).wait_recv()
            self.issue(k + 2)
            for b in range(ny):
                for e in range(nx):
                    self.mine[k, b, e] = add_up(self.mine[k, b, e], self.rd[k, b, e]).astype(BF16)
            for n in range(1, nx):
                self.a2(k, n).start()
            for n in range(1, ny):
                self.b2(k, n).start()

        @pl.when((t >= 2) & (t < count + 2))
        def _():
            k = t - 2
            for n in range(1, nx):
                self.a2(k, n).wait_recv()
            for b in range(ny):
                self.r2a[k, 0, b] = add_up(
                    self.mine[k, b, x, :, :, 0:CUT], *[self.r2a[k, n, b] for n in range(nx - 1)]
                ).astype(BF16)
            for n in range(1, ny):
                self.a3(k, n).start()
            for n in range(1, ny):
                self.b2(k, n).wait_recv()
            for b in range(nx):
                self.r2b[k, 0, b] = add_up(
                    self.mine[k, y, b, :, :, CUT:], *[self.r2b[k, n, b] for n in range(ny - 1)]
                ).astype(BF16)
            for n in range(1, nx):
                self.b3(k, n).start()

        @pl.when((t >= 4) & (t < count + 4))
        def _():
            k = t - 4
            for n in range(1, ny):
                self.a3(k, n).wait_recv()
            for n in range(1, nx):
                self.b3(k, n).wait_recv()
            left = add_up(self.r2a[k, 0, y], *[self.r3a[k, n] for n in range(ny - 1)]).astype(BF16)
            right = add_up(self.r2b[k, 0, x], *[self.r3b[k, n] for n in range(nx - 1)]).astype(BF16)
            self.s3[k, :, :, :, 0:CUT] = left.reshape(2, 2, rb, CUT)
            self.s3[k, :, :, :, CUT:] = right.reshape(2, 2, rb, CUT)
            self.c4(k).start()

        @pl.when((t >= 5) & (t < count + 5))
        def _():
            k = t - 5
            self.c4(k).wait_recv()
            self.s4[k] = add_up(self.s3[k, :, at.lo], self.r4[k]).astype(BF16)
            self.c5(k).start()

        @pl.when((t >= 6) & (t < count + 6))
        def _():
            k = t - 6
            self.c5(k).wait_recv()
            self.fin[k] = add_up(self.s4[k, at.hi], self.r5[k])

        return carry

    def start(self):
        self.issue(0)
        self.issue(1)

    def drain(self):
        def one(k, carry):
            self.core(k).wait_send()
            for n in range(1, self.at.nx):
                self.a2(k, n).wait_send()
                self.b3(k, n).wait_send()
            for n in range(1, self.at.ny):
                self.b2(k, n).wait_send()
                self.a3(k, n).wait_send()
            self.c4(k).wait_send()
            self.c5(k).wait_send()
            return carry

        lax.fori_loop(0, self.count, one, 0)


def backward_kernel(
    nx, ny, rb,
    go_ref, gi_ref, gp_ref, d_ref, q_hbm, k_hbm, v_hbm, o_hbm,
    qc_ref, kc_ref, vc_ref, lse_ref, lsec_ref, cg_ref, sg_ref, ct_ref, st_ref, meta_ref,
    oo_ref, oi_ref, op_ref, g_out,
    q_ref, k_ref, v_ref, o_ref, do_ref, g_ref, acc, accc, kt_ref, right,
    osem, isem, *refs,
):
    at = Place(nx, ny)
    p, c, q, r, z = at.p, at.c, at.hi, at.lo, at.z
    at.greet()
    reducer = Reducer(
        at, rb, CHUNKS,
        (
            (4, lambda t, core: go_ref.at[:, :, core, :, t]),
            (4, lambda t, core: gi_ref.at[:, :, core, :, :, pl.ds(pl.multiple_of(t * D, D), D)]),
            (1, lambda t, core: gp_ref.at[:, :, core]),
        ),
        refs,
    )

    reducer.start()
    loads = [(q_hbm, q_ref), (k_hbm, k_ref), (v_hbm, v_ref), (o_hbm, o_ref), (d_ref, do_ref)]
    loads = [pltpu.make_async_copy(src, dst, isem.at[n]) for n, (src, dst) in enumerate(loads)]
    for copy in loads:
        copy.start()

    lax.fori_loop(0, 2, reducer.tick, 0)
    cs_col, cs_row, _ = read_meta(meta_ref)
    acc[...] = jnp.zeros_like(acc)
    accc[...] = jnp.zeros_like(accc)
    kct = jnp.transpose(unpad_heads(kc_ref[...].astype(F32))).astype(BF16)
    for copy in loads:
        copy.wait()
    def slot(i):
        start = pl.multiple_of(i * PART, PART)
        do = do_ref[:, pl.ds(start, PART), :].reshape(PATCHES, GW)
        o = o_ref[:, pl.ds(start, PART), :].reshape(PATCHES, GW)
        prod = jnp.transpose(do.astype(F32) * o.astype(F32))
        deltas = [
            jnp.sum(prod[h * HEAD_DIM : (h + 1) * HEAD_DIM], axis=0, keepdims=True) for h in range(GROUP)
        ]
        right[0:PATCHES] = pad_right(do)
        lane = lax.broadcasted_iota(jnp.int32, (PATCHES, WIDE), 1) % 128
        right[PATCHES:] = jnp.where(lane < HEAD_DIM, q_ref[i].astype(F32), 0.0).astype(BF16)
        kt_ref[i] = jnp.transpose(unpad_heads(k_ref[i].astype(F32))).astype(BF16)
        low = first_slot(i)
        near = (cs_col >= low) & (cs_col <= i)
        dqs = []
        for h in range(GROUP):
            cols = slice(h * 128, (h + 1) * 128)
            s = jnp.where(near, nt(kc_ref[:, cols], q_ref[i, :, cols]), NEG)
            pt = jnp.exp(s - lse_ref[i, h : h + 1, :])
            dst = (pt * (nt(vc_ref[:, cols], right[0:PATCHES, cols]) - deltas[h])).astype(BF16)
            accc[:, cols] += nn(jnp.concatenate([pt.astype(BF16), dst], axis=1), right[:, cols])
            dqs.append(nn(kct[h * HEAD_DIM : (h + 1) * HEAD_DIM], dst))

        def step(j, dqs):
            new = []
            for h in range(GROUP):
                cols = slice(h * 128, (h + 1) * 128)
                pt = jnp.exp(nt(k_ref[j, :, cols], q_ref[i, :, cols]) - lse_ref[i, h : h + 1, :])
                dst = (pt * (nt(v_ref[j, :, cols], right[0:PATCHES, cols]) - deltas[h])).astype(BF16)
                acc[j, :, cols] += nn(jnp.concatenate([pt.astype(BF16), dst], axis=1), right[:, cols])
                new.append(dqs[h] + nn(kt_ref[j, h * HEAD_DIM : (h + 1) * HEAD_DIM, :], dst))
            return new

        dqs = lax.fori_loop(low, i + 1, step, dqs)
        dq = jnp.transpose(jnp.concatenate(dqs, axis=0)) * 0.125
        cosine = cg_ref[...] + ct_ref[pl.ds(i, 1), :]
        sine = sg_ref[...] + st_ref[pl.ds(i, 1), :]
        dq = turn(dq, cosine, -sine).astype(BF16).reshape(STREAMS, PART, GW)
        g_ref[:, pl.ds(start, PART), 0:GW] = dq

    def sweep(i, carry):
        slot(i)
        reducer.tick(i + 2)
        return carry

    lax.fori_loop(0, FRAMES, sweep, 0)

    doc = do_ref[:, VIS:, :].reshape(PART, GW)
    oc = o_ref[:, VIS:, :].reshape(PART, GW)
    docp = pad_right(doc)
    lane = lax.broadcasted_iota(jnp.int32, (PART, WIDE), 1) % 128
    qcl = jnp.where(lane < HEAD_DIM, qc_ref[...].astype(F32), 0.0).astype(BF16)
    prod = doc.astype(F32) * oc.astype(F32)
    lo_col = first_slot(cs_col)
    near = (cs_row >= lo_col) & (cs_row <= cs_col)
    deltas = [
        jnp.sum(prod[:, h * HEAD_DIM : (h + 1) * HEAD_DIM], axis=1, keepdims=True) for h in range(GROUP)
    ]
    lses = [lsec_ref[:, h : h + 1] for h in range(GROUP)]
    dqs = []
    for h in range(GROUP):
        cols = slice(h * 128, (h + 1) * 128)
        s = jnp.where(near, nt(qc_ref[:, cols], kc_ref[:, cols]), NEG)
        pt = jnp.exp(s - lses[h])
        dst = pt * (nt(docp[:, cols], vc_ref[:, cols]) - deltas[h])
        accc[:, cols] += nn(jnp.transpose(pt).astype(BF16), docp[:, cols]) + nn(
            jnp.transpose(dst).astype(BF16), qcl[:, cols]
        )
        dqs.append(nn(dst.astype(BF16), kc_ref[:, cols]))

    def cond_step(j, dqs):
        near = (lo_col <= j) & (cs_col >= j)
        new = []
        for h in range(GROUP):
            cols = slice(h * 128, (h + 1) * 128)
            s = jnp.where(near, nt(qc_ref[:, cols], k_ref[j, :, cols]), NEG)
            pt = jnp.exp(s - lses[h])
            dst = pt * (nt(docp[:, cols], v_ref[j, :, cols]) - deltas[h])
            acc[j, :, cols] += nn(jnp.transpose(pt).astype(BF16), docp[:, cols]) + nn(
                jnp.transpose(dst).astype(BF16), qcl[:, cols]
            )
            new.append(dqs[h] + nn(dst.astype(BF16), k_ref[j, :, cols]))
        return new

    dqs = lax.fori_loop(0, FRAMES, cond_step, dqs)
    cosine, sine = cond_tables(cs_col, ct_ref[...], st_ref[...])
    valid = cs_col < FRAMES
    dq = jnp.concatenate([t[:, :HEAD_DIM] for t in dqs], axis=1) * 0.125
    both = accc[...]
    parts = (turn(dq, cosine, -sine), turn(unpad_heads(both), cosine, -sine), unpad_right(both))
    for part, t in enumerate(parts):
        t = jnp.where(valid, t, 0.0).astype(BF16)
        g_ref[:, VIS:, part * GW : (part + 1) * GW] = t.reshape(STREAMS, CROWS, GW)

    def finish(i, carry):
        start = pl.multiple_of(i * PART, PART)
        cosine = cg_ref[...] + ct_ref[pl.ds(i, 1), :]
        sine = sg_ref[...] + st_ref[pl.ds(i, 1), :]
        both = acc[i]
        dk = turn(unpad_heads(both), cosine, -sine)
        g_ref[:, pl.ds(start, PART), GW : 2 * GW] = dk.astype(BF16).reshape(STREAMS, PART, GW)
        g_ref[:, pl.ds(start, PART), 2 * GW :] = unpad_right(both).astype(BF16).reshape(STREAMS, PART, GW)
        return carry

    lax.fori_loop(0, FRAMES, finish, 0)
    save = pltpu.make_async_copy(g_ref, g_out, isem.at[5])
    save.start()
    lax.fori_loop(10, CHUNKS + 6, reducer.tick, 0)
    fin = reducer.fin
    outs = [pltpu.make_async_copy(fin.at[k], oo_ref.at[k], osem.at[k]) for k in range(4)]
    outs += [
        pltpu.make_async_copy(fin.at[k], oi_ref.at[:, pl.ds((k - 4) * D, D)], osem.at[k]) for k in range(4, 8)
    ]
    outs += [pltpu.make_async_copy(fin.at[8], op_ref, osem.at[8])]
    for copy in outs:
        copy.start()

    reducer.drain()
    save.wait()
    for copy in outs:
        copy.wait()


def unpad_right(t):
    return jnp.concatenate([t[:, h * 128 + HEAD_DIM : (h + 1) * 128] for h in range(GROUP)], axis=1)


def attend_backward(g_out, g_in, g_proj, grad_o, saved, o, tables, meta):
    nx, ny, rb = grid_shape()
    q, k, v, *rest = saved

    def v16(*shape):
        return VM(shape, BF16)

    scratch = [
        v16(*q.shape), v16(*k.shape), v16(*v.shape), v16(*o.shape), v16(*o.shape), v16(STREAMS, ROWS, 3 * GW),
        VM((FRAMES, PATCHES, WIDE), F32), VM((PART, WIDE), F32), v16(FRAMES, GW, PATCHES), v16(2 * PATCHES, WIDE),
        dma(CHUNKS), dma(6),
    ] + Reducer.scratch(CHUNKS, nx, ny, rb)
    outs = (((4, rb, D), F32), ((rb, 4 * D), F32), ((rb, D), F32), ((STREAMS, ROWS, 3 * GW), BF16))
    ops = (
        g_out.reshape(ny, nx, 2, STREAMS, 4, rb, D), g_in.reshape(ny, nx, 2, STREAMS, rb, 4 * D),
        g_proj.reshape(ny, nx, 2, STREAMS, rb, D), grad_o, q, k, v, o,
    )
    return comm_call(
        functools.partial(backward_kernel, nx, ny, rb), "attend_backward", 3, outs, scratch, ops,
        tuple(rest) + tables + (meta,),
    )


def finish_kernel(
    nx, ny, rb,
    f_hbm, xa_hbm, gq_ref, w_hbm, x_hbm, h_hbm, v_ref, gain_ref,
    gx_ref, oq_ref, ov_ref,
    f, xa, w, x_own, h_own, big, near_in, near_out, own, land, tail, tail_out, total,
    q1, rq1a, rq1b, sq1a, sq1b, rq2a, rq2b, sq2, rq3, sq3, vm, vd, vx, vy, vz1, vz2, hold,
    isem, dsend, drecv, send, recv, csend, crecv, lsem,
    qs1a, qr1a, qs1b, qr1b, qs2a, qr2a, qs2b, qr2b, qs3, qr3, qs4, qr4, vs, vr, vsx, vrx, vsy, vry, relay, rsend, rrecv, cols_sum,
):
    at = Place(nx, ny)
    p, c, q, r, z, x, y, hi, lo = at.p, at.c, at.hi, at.lo, at.z, at.x, at.y, at.hi, at.lo
    group = 2 * r + c
    in_pair, inner = q == c, z == 1 + q
    loads = []
    for part in range(3):
        cols = pl.ds(pl.multiple_of(part * D + group * GW, GW), GW)
        loads.append(pltpu.make_async_copy(w_hbm.at[:, cols], w.at[:, pl.ds(part * GW, GW)], isem.at[part]))
    loads.append(pltpu.make_async_copy(f_hbm, f, isem.at[3]))
    loads.append(pltpu.make_async_copy(xa_hbm, xa, isem.at[4]))
    late = [
        pltpu.make_async_copy(gq_ref, q1, isem.at[5]),
        pltpu.make_async_copy(x_hbm, x_own, isem.at[6]),
        pltpu.make_async_copy(h_hbm, h_own, isem.at[7]),
    ]
    for copy in loads + late:
        copy.start()
    at.greet()
    rows = pl.ds(pl.multiple_of(c * HALF, HALF), HALF)
    rest = pl.ds(pl.multiple_of((1 - c) * HALF, HALF), HALF)
    last = pl.ds(VIS, CROWS)
    qa, qb = pl.ds(0, QCUT), pl.ds(QCUT, QCUT)

    def q1a(n):
        return remote(q1.at[:, at.along_x(n), :, :, qa], rq1a.at[n - 1], qs1a.at[n - 1], qr1a.at[n - 1], at.x_device(n))

    def q1b(n):
        return remote(q1.at[at.along_y(n), :, :, :, qb], rq1b.at[n - 1], qs1b.at[n - 1], qr1b.at[n - 1], at.y_device(n))

    def q2a(n):
        return remote(sq1a.at[at.along_y(n)], rq2a.at[n - 1], qs2a.at[n - 1], qr2a.at[n - 1], at.y_device(n))

    def q2b(n):
        return remote(sq1b.at[at.along_x(n)], rq2b.at[n - 1], qs2b.at[n - 1], qr2b.at[n - 1], at.x_device(n))

    def q3():
        return remote(sq2.at[:, 1 - hi], rq3, qs3, qr3, at.z_two)

    mates = [(at.near, 1, 0), (at.z_one, 0, 1), (at.slant, 1, 1)]

    def q4(n, part):
        device, core, side = mates[n]
        to_core = c + core - 2 * c * core
        to_side = lo + side - 2 * lo * side
        place = pl.ds(pl.multiple_of(part * D + group * GW, GW), GW)
        return remote(
            sq3.at[to_core, to_side, :, pl.ds(part * GW, GW)], oq_ref.at[:, place],
            qs4.at[n, part], qr4.at[n, part], device,
        )

    def q4_own(part):
        place = pl.ds(pl.multiple_of(part * D + group * GW, GW), GW)
        return pltpu.make_async_copy(sq3.at[c, lo, :, pl.ds(part * GW, GW)], oq_ref.at[:, place], lsem.at[2 + part])

    def v_core():
        return remote(vm.at[0], vd, vs.at[0], vr.at[0], at.near)

    def v_x(n):
        return remote(vm.at[1], vx.at[n - 1], vsx.at[n - 1], vrx.at[n - 1], at.x_device(n))

    def v_y(n):
        return remote(vm.at[2], vy.at[n - 1], vsy.at[n - 1], vry.at[n - 1], at.y_device(n))

    def v_z1():
        return remote(vm.at[3], vz1, vs.at[1], vr.at[1], at.z_one)

    def v_z2():
        return remote(vm.at[4], vz2, vs.at[2], vr.at[2], at.z_two)

    def near_copy(s):
        return remote(near_out.at[s], near_in.at[s], dsend.at[s], drecv.at[s], at.near)

    def row_copy(s):
        mark = jnp.where(s // 2 == q, r, 0)
        return remote(own.at[s], land.at[mark, rows], send.at[s], recv.at[mark, c], (2 * p + q, s))

    def row_own(s):
        return pltpu.make_async_copy(own.at[s], land.at[r, rows], lsem.at[0])

    def relay_copy(n, s):
        return remote(own.at[s], relay.at[n], rsend.at[n], rrecv.at[n], at.z_one)

    def tail_copy(s):
        return remote(tail_out.at[s], tail.at[group], csend.at[s], crecv.at[group], (2 * p + q, s))

    def tail_own(s):
        return pltpu.make_async_copy(tail_out.at[s], tail.at[group], lsem.at[1])

    def mine(s):
        return (q == c) & (s == z)

    def go(s, far, near):
        @pl.when(mine(s))
        def _():
            near(s)

        @pl.when(jnp.logical_not(mine(s)))
        def _():
            far(s)

    late[0].wait()
    for n in range(1, nx):
        q1a(n).start()
    for n in range(1, ny):
        q1b(n).start()
    for copy in loads:
        copy.wait()
    hold[...] = jnp.zeros_like(hold)
    cols_sum[...] = jnp.zeros_like(cols_sum)

    far = (STREAMS - 1 - z, z + 2 - 4 * hi, z + 1 - 2 * lo, z)

    @pl.when(jnp.logical_not(in_pair))
    def _():
        land[1] = jnp.zeros_like(land[1])

    def combine(s):
        near_copy(s).wait_recv()
        for t in range(HALF // 64):
            part = pl.ds(t * 64, 64)
            own[s, part] = add_up(near_in[s, part], own[s, part]).astype(BF16)

    def pass_on(n):
        s = far[n]
        combine(s)
        if n >= 2:
            go(s, lambda s: row_copy(s).start(), lambda s: row_own(s).start())
        else:
            @pl.when(jnp.logical_not(inner))
            def _():
                relay_copy(n, s).start()

    def pass_far(n):
        s = far[1 - n]

        @pl.when(inner)
        def _():
            relay_copy(n, s).wait_recv()
            for t in range(HALF // 64):
                part = pl.ds(t * 64, 64)
                own[s, part] = add_up(relay[n, part], own[s, part]).astype(BF16)
            row_copy(s).start()

    def partial_rows(t, carry):
        s = jnp.where(t == 0, far[0], jnp.where(t == 1, far[1], jnp.where(t == 2, far[2], far[3])))
        big[...] = nt(f[s], w[...])
        near_out[s] = big[rest].astype(BF16)
        near_copy(s).start()
        own[s] = big[rows].astype(BF16)
        tail_out[s] = big[last].astype(BF16)
        go(s, lambda s: tail_copy(s).start(), lambda s: tail_own(s).start())
        for e in range(ROWS // 48):
            part = pl.ds(e * 48, 48)
            values = xa[s, part].astype(F32)
            centre = values - jnp.mean(values, axis=1, keepdims=True)
            scale = lax.rsqrt(jnp.mean(centre * centre, axis=1, keepdims=True) + EPS)
            g = big[part]
            gh = g * (centre * scale)
            flat = f[s, part].astype(F32)
            for m in range(6):
                cols_sum[...] += flat[m * 8 : m * 8 + 8]
                hold[0] += gh[m * 8 : m * 8 + 8]
                hold[1] += g[m * 8 : m * 8 + 8]

        for n in range(STREAMS - 1):
            @pl.when(t == n + 1)
            def _():
                pass_on(n)

        return carry

    lax.fori_loop(0, STREAMS, partial_rows, 0)
    pass_on(STREAMS - 1)
    vm[0] = v_ref[...]
    vm[0, 0:1] = jnp.sum(hold[0], axis=0, keepdims=True)
    vm[0, 1:2] = jnp.sum(hold[1], axis=0, keepdims=True)
    for part in range(3):
        place = pl.ds(pl.multiple_of(group * GW, GW), GW)
        vm[0, 2 + part : 3 + part, place] = jnp.sum(cols_sum[:, part * GW : (part + 1) * GW], axis=0, keepdims=True)
    v_core().start()

    for n in range(1, nx):
        q1a(n).wait_recv()
    for n in range(1, ny):
        q1b(n).wait_recv()
    for b in range(ny):
        sq1a[b] = add_up(q1[b, x, :, :, 0:QCUT], *[rq1a[n, b] for n in range(nx - 1)]).astype(BF16)
    for n in range(1, ny):
        q2a(n).start()
    for b in range(nx):
        sq1b[b] = add_up(q1[y, b, :, :, QCUT:], *[rq1b[n, b] for n in range(ny - 1)]).astype(BF16)
    for n in range(1, nx):
        q2b(n).start()
    v_core().wait_recv()
    vm[1] = vm[0] + vd[...]
    for n in range(1, nx):
        v_x(n).start()
    pass_far(0)
    for n in range(1, ny):
        q2a(n).wait_recv()
    for n in range(1, nx):
        q2b(n).wait_recv()
    left = add_up(sq1a[y], *[rq2a[n] for n in range(ny - 1)]).astype(BF16)
    right = add_up(sq1b[x], *[rq2b[n] for n in range(nx - 1)]).astype(BF16)
    sq2[:, :, :, :, 0:QCUT] = left.reshape(2, 2, 2, rb, QCUT)
    sq2[:, :, :, :, QCUT:] = right.reshape(2, 2, 2, rb, QCUT)
    q3().start()
    for n in range(1, nx):
        v_x(n).wait_recv()
    vm[2] = add_up(vm[1], *[vx[n] for n in range(nx - 1)])
    for n in range(1, ny):
        v_y(n).start()
    for n in range(1, ny):
        v_y(n).wait_recv()
    vm[3] = add_up(vm[2], *[vy[n] for n in range(ny - 1)])
    v_z1().start()
    pass_far(1)
    q3().wait_recv()
    sq3[...] = add_up(sq2[:, hi], rq3[...])
    for part in range(3):
        for n in range(3):
            q4(n, part).start()
        q4_own(part).start()
    v_z1().wait_recv()
    vm[4] = vm[3] + vz1[...]
    v_z2().start()

    late[1].wait()
    late[2].wait()
    for side in range(2):
        for core in range(2):
            part = pl.ds(core * HALF, HALF)
            g = 2 * side + core
            self_made = (core == c) & (2 * c + side == z)

            @pl.when(jnp.logical_not(self_made))
            def _():
                remote(tail_out.at[0], tail.at[g], csend.at[0], crecv.at[g], at.near).wait_recv()

            @pl.when(jnp.logical_not(self_made) & (in_pair | (side == 0)))
            def _():
                remote(own.at[0], land.at[side, part], send.at[0], recv.at[side, core], at.near).wait_recv()

            @pl.when(self_made)
            def _():
                row_own(0).wait()
                tail_own(0).wait()

    gain = gain_ref[0:1]

    def back(dst, grad):
        values = x_own[dst].astype(F32)
        centre = values - jnp.mean(values, axis=1, keepdims=True)
        scale = lax.rsqrt(jnp.mean(centre * centre, axis=1, keepdims=True) + EPS)
        normed = centre * scale
        g = grad * gain
        total[dst] = h_own[dst] + scale * (
            g - jnp.mean(g, axis=1, keepdims=True) - normed * jnp.mean(g * normed, axis=1, keepdims=True)
        )

    def back_rows(t, carry):
        part = pl.ds(pl.multiple_of(t * 64, 64), 64)
        back(part, add_up(land[0, part], land[1, part]))
        return carry

    lax.fori_loop(0, VIS // 64, back_rows, 0)
    back(last, add_up(tail[0], tail[1], tail[2], tail[3]))
    done = pltpu.make_async_copy(total, gx_ref, lsem.at[5])
    done.start()
    v_z2().wait_recv()
    vm[5] = vm[4] + vz2[...]
    v_done = pltpu.make_async_copy(vm.at[5], ov_ref, lsem.at[6])
    v_done.start()
    for n in range(1, nx):
        q1a(n).wait_send()
        q2b(n).wait_send()
        v_x(n).wait_send()
    for n in range(1, ny):
        q1b(n).wait_send()
        q2a(n).wait_send()
        v_y(n).wait_send()
    q3().wait_send()
    v_core().wait_send()
    v_z1().wait_send()
    v_z2().wait_send()
    for n in range(STREAMS):
        s = far[n]
        near_copy(s).wait_send()
        if n < 2:
            @pl.when(inner)
            def _():
                row_copy(s).wait_send()

            @pl.when(jnp.logical_not(inner))
            def _():
                relay_copy(n, s).wait_send()

            tail_copy(s).wait_send()
        else:
            @pl.when(jnp.logical_not(mine(s)))
            def _():
                row_copy(s).wait_send()
                tail_copy(s).wait_send()
    for part in range(3):
        q4_own(part).wait()
        for n in range(3):
            q4(n, part).wait_send()
            q4(n, part).wait_recv()
    done.wait()
    v_done.wait()


def finish_rows(flat, x_all, g_qkv, w_qkv, x, h, vectors, gain):
    nx, ny, rb = grid_shape()

    def v(*shape):
        return VM(shape, BF16)

    def vf(*shape):
        return VM(shape, F32)

    scratch = [
        v(STREAMS, ROWS, 3 * GW), v(STREAMS, ROWS, D), v(D, 3 * GW), v(ROWS, D), vf(ROWS, D), vf(ROWS, D),
        v(STREAMS, HALF, D), v(STREAMS, HALF, D), v(STREAMS, HALF, D), v(2, VIS, D), v(4, CROWS, D), v(4, CROWS, D),
        vf(ROWS, D),
        v(ny, nx, 8, rb, 3 * GW), v(nx - 1, ny, 8, rb, QCUT), v(ny - 1, nx, 8, rb, QCUT),
        v(ny, 8, rb, QCUT), v(nx, 8, rb, QCUT), v(ny - 1, 8, rb, QCUT), v(nx - 1, 8, rb, QCUT),
        v(2, 2, 2, rb, 3 * GW), v(2, 2, rb, 3 * GW), vf(2, 2, rb, 3 * GW),
        vf(6, 16, D), vf(16, D), vf(nx - 1, 16, D), vf(ny - 1, 16, D), vf(16, D), vf(16, D), vf(2, 8, D),
        dma(8), dma(4), dma(4), dma(4), dma(2, 2), dma(4), dma(4), dma(7),
        dma(nx - 1), dma(nx - 1), dma(ny - 1), dma(ny - 1), dma(ny - 1), dma(ny - 1), dma(nx - 1), dma(nx - 1),
        pltpu.SemaphoreType.DMA, pltpu.SemaphoreType.DMA, dma(3, 3), dma(3, 3),
        dma(3), dma(3), dma(nx - 1), dma(nx - 1), dma(ny - 1), dma(ny - 1),
        v(2, HALF, D), dma(2), dma(2), vf(8, 3 * GW),
    ]
    outs = (((ROWS, D), F32), ((rb, 3 * D), F32), ((16, D), F32))
    ops = (flat, x_all, g_qkv.reshape(ny, nx, 8, rb, 3 * GW), w_qkv, x, h)
    return comm_call(
        functools.partial(finish_kernel, nx, ny, rb), "finish_rows", 4, outs, scratch, ops, (vectors, gain)
    )


TILE = 48
TILES = ROWS // TILE


def tn(a, b):
    return lax.dot_general(a, b, (((0,), (0,)), ((), ())), preferred_element_type=F32)


def mlp_kernel(
    win_hbm, wout_hbm, att_ref, x_ref, dy_ref, wp_ref, par_ref,
    do_out, gi_out, go_out, gp_out, y_ref, gh_ref, vec_ref,
    wi, wo, n_ref, h_ref, buf, dbuf, hid, du, yacc, dn, dhb, do_ref, stage, sums,
    isem, ssem, hs, hr, hl,
):
    p, c, q, r, z = where_am_i()

    def fetch(t, slot):
        cols = pl.ds(pl.multiple_of(t * D, D), D)
        return (
            pltpu.make_async_copy(win_hbm.at[:, cols], wi.at[slot], isem.at[0, slot]),
            pltpu.make_async_copy(wout_hbm.at[cols, :], wo.at[slot], isem.at[1, slot]),
        )

    for copy in fetch(0, 0):
        copy.start()
    greet_column()
    sums[...] = jnp.zeros_like(sums)
    for j in range(2):
        cols = slice(j * CUT, (j + 1) * CUT)
        buf[:, cols] = nn(att_ref[...], wp_ref[:, cols])

    def tile(t):
        return pl.ds(pl.multiple_of(t * TILE, 16), TILE)

    def fold(row, values):
        total = values[0:8]
        for m in range(1, TILE // 8):
            total = total + values[m * 8 : m * 8 + 8]
        sums[row] += total

    def enter(t, carry):
        rows = tile(t)
        h = x_ref[rows].astype(F32) + buf[rows] + par_ref[9:10]
        h_ref[rows] = h
        centre = h - jnp.mean(h, axis=1, keepdims=True)
        scale = lax.rsqrt(jnp.mean(centre * centre, axis=1, keepdims=True) + EPS)
        n_ref[rows] = (centre * scale * par_ref[10:11] + par_ref[11:12]).astype(BF16)
        return carry

    lax.fori_loop(0, TILES, enter, 0)

    def block(t, carry):
        slot = t % 2
        for copy in fetch(t, slot):
            copy.wait()

        @pl.when(t < 3)
        def _():
            for copy in fetch(t + 1, 1 - slot):
                copy.start()

        for j in range(2):
            cols = slice(j * CUT, (j + 1) * CUT)
            buf[:, cols] = nn(n_ref[...], wi[slot, :, cols])
            dbuf[:, cols] = nt(dy_ref[...], wo[slot, cols, :])
        place = pl.ds(pl.multiple_of(t * D, D), D)

        def act(e, carry):
            rows = tile(e)
            for j in range(4):
                cols = slice(j * 256, (j + 1) * 256)
                u = buf[rows, cols] + par_ref[pl.ds(5 + t, 1), cols]
                phi = 0.5 * (1.0 + lax.erf(u * (2.0**-0.5)))
                hid[rows, pl.ds(pl.multiple_of(t * D + j * 256, 256), 256)] = (u * phi).astype(BF16)
                slope = phi + u * (jnp.exp(-0.5 * u * u) * ((2.0 * math.pi) ** -0.5))
                g = (dbuf[rows, cols] * slope).astype(BF16)
                du[rows, pl.ds(pl.multiple_of(t * D + j * 256, 256), 256)] = g
                g = g.astype(F32)
                total = g[0:8]
                for m in range(1, TILE // 8):
                    total = total + g[m * 8 : m * 8 + 8]
                sums[t, :, cols] += total
            return carry

        lax.fori_loop(0, TILES, act, 0)
        for j in range(2):
            cols = slice(j * CUT, (j + 1) * CUT)
            more = nn(hid[:, place], wo[slot, :, cols])
            back = nt(du[:, place], wi[slot, cols, :])

            @pl.when(t == 0)
            def _():
                yacc[:, cols] = more
                dn[:, cols] = back

            @pl.when(t > 0)
            def _():
                yacc[:, cols] += more
                dn[:, cols] += back

        return carry

    lax.fori_loop(0, 4, block, 0)

    def leave(t, carry):
        rows = tile(t)
        h = h_ref[rows]
        y_ref[rows] = (h + yacc[rows] + par_ref[12:13]).astype(BF16)
        centre = h - jnp.mean(h, axis=1, keepdims=True)
        scale = lax.rsqrt(jnp.mean(centre * centre, axis=1, keepdims=True) + EPS)
        normed = centre * scale
        grad = dn[rows]
        dy = dy_ref[rows].astype(F32)
        fold(5, grad * normed)
        fold(6, grad)
        fold(7, dy)
        g = grad * par_ref[10:11]
        gh = dy + scale * (
            g - jnp.mean(g, axis=1, keepdims=True) - normed * jnp.mean(g * normed, axis=1, keepdims=True)
        )
        gh_ref[rows] = gh
        low = gh.astype(BF16)
        dhb[rows] = low
        fold(4, low.astype(F32))
        return carry

    lax.fori_loop(0, TILES, leave, 0)
    for j in range(2):
        rows = slice(j * CUT, (j + 1) * CUT)
        do_ref[:, rows] = nt(dhb[...], wp_ref[rows, :]).astype(BF16)

    def heads_copy(g):
        device = (2 * p + g % 2, 2 * c + g // 2)
        return remote(do_ref.at[:, pl.ds(g * GW, GW)], do_out.at[z], hs.at[g], hr.at[z], device)

    def heads_own(g):
        return pltpu.make_async_copy(do_ref.at[:, pl.ds(g * GW, GW)], do_out.at[z], hl)

    for g in range(4):
        self_made = (g % 2 == c) & (2 * c + g // 2 == z)

        @pl.when(self_made)
        def _():
            heads_own(g).start()

        @pl.when(jnp.logical_not(self_made))
        def _():
            heads_copy(g).start()

    vec_ref[...] = jnp.zeros_like(vec_ref)
    for n in range(8):
        vec_ref[5 + n : 6 + n] = jnp.sum(sums[n], axis=0, keepdims=True)

    def in_save(t):
        return pltpu.make_async_copy(stage.at[0], gi_out.at[:, pl.ds(pl.multiple_of(t * D, D), D)], ssem.at[0])

    def out_save(t):
        return pltpu.make_async_copy(stage.at[1], go_out.at[pl.ds(pl.multiple_of(t * D, D), D), :], ssem.at[1])

    def weights(t, carry):
        @pl.when(t > 0)
        def _():
            in_save(t - 1).wait()

        for m in range(2):
            half = pl.ds(m * CUT, CUT)
            place = pl.ds(pl.multiple_of(t * D, D), D)
            stage[0, half, :] = tn(n_ref[:, half], du[:, place]).astype(BF16)
        in_save(t).start()

        @pl.when(t > 0)
        def _():
            out_save(t - 1).wait()

        for m in range(2):
            half = pl.ds(m * CUT, CUT)
            place = pl.ds(pl.multiple_of(t * D + m * CUT, CUT), CUT)
            stage[1, half, :] = tn(hid[:, place], dy_ref[...]).astype(BF16)
        out_save(t).start()
        return carry

    lax.fori_loop(0, 4, weights, 0)
    in_save(3).wait()
    for m in range(2):
        half = pl.ds(m * CUT, CUT)
        stage[0, half, :] = tn(att_ref[:, half], dhb[...]).astype(BF16)
    proj_save = pltpu.make_async_copy(stage.at[0], gp_out, ssem.at[0])
    proj_save.start()
    for g in range(4):
        self_made = (g % 2 == c) & (2 * c + g // 2 == z)

        @pl.when(self_made)
        def _():
            heads_own(g).wait()

        @pl.when(jnp.logical_not(self_made))
        def _():
            heads_copy(g).wait_send()
    for s in range(STREAMS):
        @pl.when((q != c) | (s != z))
        def _():
            remote(do_ref.at[:, pl.ds(0, GW)], do_out.at[s], hs.at[0], hr.at[s], (2 * p + 1 - c, z)).wait_recv()
    out_save(3).wait()
    proj_save.wait()


def mlp(w_in, w_out, attended, x, dy, w_proj, params):
    def v16(*shape):
        return VM(shape, BF16)

    def vf(*shape):
        return VM(shape, F32)

    scratch = [
        v16(2, D, D), v16(2, D, D), v16(ROWS, D), vf(ROWS, D), vf(ROWS, D), vf(ROWS, D),
        v16(ROWS, 4 * D), v16(ROWS, 4 * D), vf(ROWS, D), vf(ROWS, D), v16(ROWS, D), v16(ROWS, D),
        v16(2, D, D), vf(8, 8, D),
        dma(2, 2), dma(2), dma(4), dma(4), pltpu.SemaphoreType.DMA,
    ]
    outs = (((STREAMS, ROWS, GW), BF16), ((D, 4 * D), BF16), ((4 * D, D), BF16), ((D, D), BF16))
    near_outs = (((ROWS, D), BF16), ((ROWS, D), F32), ((16, D), F32))
    return comm_call(
        mlp_kernel, "mlp", 1, outs, scratch, (w_in, w_out), (attended, x, dy, w_proj, params), near_outs
    )


def own_meta(lengths, mask):
    frames = jnp.arange(FRAMES, dtype=jnp.int32)
    ends = jnp.cumsum(lengths)
    reached = ends[None, :] <= frames[:, None]
    begin = jnp.sum(jnp.where(reached, lengths[None, :], 0), axis=1)
    episode = jnp.sum(reached, axis=1)[:, None] == jnp.arange(lengths.shape[0])[None, :]
    length = jnp.sum(jnp.where(episode, lengths[None, :], 0), axis=1)
    base = jnp.where(length == MOST, 0, jnp.where(length == MIDDLE - MOST, MOST, MIDDLE))
    slot = base + frames - begin
    perm = jnp.sum(jnp.where(slot[:, None] == frames[None, :], frames[:, None], 0), axis=0)
    stream = jnp.arange(STREAMS)[:, None]
    row = jnp.arange(CROWS)[None, :]
    part = FRAMES // STREAMS
    frame = jnp.where(row < part * COND, part * stream + row // COND, FRAMES)
    cslot = jnp.sum(jnp.where(frame[..., None] == frames, slot[None, None, :], 0), axis=-1)
    cslot = jnp.where(frame < FRAMES, cslot, 99).reshape(1, PART)
    hidden = jnp.where(mask == 1, 0.0, NEG).astype(F32)
    bias = jnp.sum(jnp.where((perm[:, None] == frames[None, :])[:, :, None], hidden[None], 0.0), axis=1)
    line = jnp.pad(cslot.astype(F32), ((0, 7), (0, PATCHES - PART)))
    return perm.astype(jnp.int32), slot.astype(jnp.int32), jnp.concatenate([bias, line], axis=0)


def per_device(
    visual, conditioning, d_visual, d_conditioning, episode_frames, patch_mask,
    ln1_gain, ln1_bias, w_qkv, b_qkv, w_proj, b_proj, ln2_gain, ln2_bias, w_in, b_in, w_out, b_out,
):
    d, z = lax.axis_index("dp"), lax.axis_index("stream")
    extra = conditioning.shape[1] * COND
    perm, slot, own = own_meta(episode_frames[0], patch_mask[0])
    x, dy = place_rows(perm, visual, conditioning, d_visual, d_conditioning)
    params = jnp.concatenate(
        [ln1_gain, ln1_bias, b_qkv, b_in, b_proj, ln2_gain, ln2_bias, b_out, jnp.zeros((3 * D,), BF16)]
    ).astype(F32).reshape(16, D)
    tables = tuple(jnp.asarray(t) for t in rope_constants())
    attended, x_all, a, q, k, v, o, meta, *rest = attend_forward(x, w_qkv, own, params, tables)
    grad_heads, grad_w_in, grad_w_out, grad_w_proj, output, grad_h, vectors = mlp(
        w_in, w_out, attended, x, dy, w_proj, params
    )
    red_out, red_in, red_proj, grad_qkv = attend_backward(
        grad_w_out, grad_w_in, grad_w_proj, grad_heads, (q, k, v, *rest), o, tables, meta
    )
    role_grad = jnp.einsum(
        "rd,re->de", a.reshape(STREAMS * ROWS, D), grad_qkv.reshape(STREAMS * ROWS, 3 * GW), preferred_element_type=F32
    )
    grad_x, red_qkv, sums = finish_rows(
        grad_qkv, x_all, role_grad.astype(BF16), w_qkv, x, grad_h, vectors, params
    )
    out_visual, grad_visual = restore_rows(slot, output, grad_x)
    owner = d * STREAMS + z
    owners = lax.axis_size("dp") * STREAMS

    def share(start, rows):
        size = rows * D // owners
        return lax.dynamic_slice_in_dim(sums[start : start + rows].reshape(-1), owner * size, size, 0)

    return (
        out_visual.reshape(visual.shape), output[VIS : VIS + extra].reshape(conditioning.shape),
        grad_visual.reshape(visual.shape), grad_x[VIS : VIS + extra].reshape(conditioning.shape),
        share(0, 1), share(1, 1), red_qkv, share(2, 2), share(4, 1), red_proj, share(9, 1), share(10, 1), share(11, 1),
        red_in, share(5, 4), red_out.reshape(-1, D), share(12, 1),
    )


def solution(mesh):
    rows = P("dp", None, "stream", None)
    extra = P("dp", "stream", None, None)
    vector = P(("dp", "stream"))
    matrix = P(("dp", "stream"), None)
    in_specs = (rows, extra, rows, extra, P("dp", None), P("dp", None, None)) + (P(),) * 12
    out_specs = (
        rows, extra, rows, extra, vector, vector, matrix, vector, vector, matrix, vector, vector, vector, matrix,
        vector, matrix, vector,
    )
    return jax.shard_map(per_device, mesh=mesh, in_specs=in_specs, out_specs=out_specs, check_vma=False)
```

time: 2110 us -> 367 us (0.17)
  waiting for transfers between devices: 1400 us -> 0 us
  matrix products: 399 us -> 8.31 us
  Pallas kernels: 0 us -> 338 us
  local copies, waits for them, and re-layouts: 103 us -> 15.3 us
  other arithmetic: 81.3 us -> 3.51 us
  loops' own time: 52.7 us -> 0 us
  blocking collectives: 41 us -> 0 us
    reduce_scatter x4 -> x0, waiting for transfers between devices: 894 us -> none  [the longest x1 366 us: per_device(): lax.psum_scatter(grad_w_in, ('dp', 'stream'), scatter_dimension=0, tiled=...]
    dot_general x124 -> x1, matrix products: 399 us -> 8.31 us  [per_device(): jnp.einsum('rd,re->de', a.reshape(STREAMS * ROWS, D), grad_qkv.reshape(ST...]
    pallas_call x0 -> x6, Pallas kernels: none -> 338 us  [the longest x4 330 us: comm_call(): pl.pallas_call(kernel, name=name, out_shape=tuple((jax.ShapeDtypeStruct(s...]
    unnamed x8 -> x0, waiting for transfers between devices: 294 us -> none
    all_gather x2 -> x0, waiting for transfers between devices: 210 us -> none  [the longest x1 136 us: per_device(): lax.all_gather(keys_own, 'stream', axis=1, tiled=True)]
    another operation x2 -> x0, loops' own time: 52.7 us -> none  [the longest x1 41.9 us: per_device(): lax.map(attend_backward, jnp.arange(HEADS, dtype=jnp.int32))]
    another operation x11 -> x1, other arithmetic: 42 us -> 0.87 us
    unnamed x1 -> x0, blocking collectives: 41 us -> none
  transfers between devices with their start and end apart: 7 -> 0, of which waited for: 7 -> 0; matrix products, arithmetic and copies ran while one was open for 7% -> 0% of each run, Pallas kernels for 0% -> 0%
where the time goes in v3:
time: 367 us; the launch traced here: 366 us
  Pallas kernels  338 us (92%)
  local copies, waits for them, and re-layouts  15.3 us (4%)
  matrix products  8.31 us (2%)
    pallas_call x4, Pallas kernels, comm_call(): pl.pallas_call(kernel, name=name, out_shape=tuple((jax.ShapeDtypeStruct(s...  330 us
    dot_general x1, matrix products, per_device(): jnp.einsum('rd,re->de', a.reshape(STREAMS * ROWS, D), grad_qkv.reshape(ST...  8.31 us

profile of v3, /device:TPU:0, one launch (start us, length us, event | category | flops | bytes accessed | tf_op | source)
XLA Modules:
  0.0 366.2 jit_solution(7033071483173010492)
XLA Ops:
  0.7 0.9 reduce-window.8
  1.7 0.7 select_reduce_fusion.4
  3.0 0.7 select_bitcast_fusion
  3.8 0.6 select_maximum_fusion.m_hbm
  4.4 1.3 reshape.318.xc_ref
  5.7 1.3 reshape.320.dc_ref
  7.0 3.8 %place_rows.1 = (bf16[528,1024]{1,0:T(8,128)(2,1)}, bf16[528,1024]{1,0:T(8,128)(2,1)}) custom-call(s32[8]{0:T(128)} %copy-done.13, bf16[8,64,1024]{2,1,0:T(8,128)(2,1)} %bitcast.46, bf16[4,1024]{1,0:T(4,128)(2,1)} %reshape.318.xc_ref, bf16[8,64,1024]{2,1,0:T(8,128)(2,1)} %bitcast.47, bf16[4,1024]{1,0:T(4,128)(2,1)} %reshape.320.dc_ref), custom_call_target="tpu_custom_call" | custom-call | tf_op jit(solution)/shard_map/place_rows/pallas_call | solution.py:148
  11.0 0.6 reshape.333.par_ref.gain_ref
  11.6 96.9 %attend_forward.1 = (bf16[528,1024]{1,0:T(8,128)(2,1)}, bf16[4,528,1024]{2,1,0:T(8,128)(2,1)}, bf16[4,528,1024]{2,1,0:T(8,128)(2,1)}, bf16[8,256,512]{2,1,0:T(8,...) custom-call(bf16[528,1024]{1,0:T(8,128)(2,1)} %get-tuple-element.48., ...), custom_call_target="tpu_custom_call" | custom-call | tf_op jit(solution)/shard_map/attend_forward/pallas_call | solution.py:209
  108.5 62.8 %mlp.1 = (bf16[4,528,256]{2,1,0:T(8,128)(2,1)}, bf16[1024,4096]{1,0:T(8,128)(2,1)}, bf16[4096,1024]{1,0:T(8,128)(2,1)}, bf16[1024,1024]{1,0:T(8,128)(2,1)}, bf16...) custom-call(bf16[1024,4096]{1,0:T(8,128)(2,1)} %win_hbm.1, bf16[4096,1024]{1,0:T(8,128)(2,1)} %wout_hbm.1, ...), custom_call_target="tpu_custom_call" | custom-call | tf_op jit(solution)/shard_map/mlp/pallas_call | solution.py:209
  171.3 111.7 %attend_backward.1 = (f32[4,32,1024]{2,1,0:T(8,128)}, f32[32,4096]{1,0:T(8,128)}, f32[32,1024]{1,0:T(8,128)}, bf16[4,528,768]{2,1,0:T(8,128)(2,1)}) custom-call(bf16[2,2,2,4,4,32,1024]{6,5,4,3,2,1,0:T(8,128)(2,1)} %bitcast.43, bf16[2,2,2,4,32,4096]{5,4,3,2,1,0:T(8,128)(2,1)} %bitcast.42, bf16[2,2,2,4,32,1024]{5,4,3,2,1,0:T(8,128)(2,1)} %bitcast.44, ...), custom_call_target="tpu_custom_call" | custom-call | tf_op jit(solution)/shard_map/attend_backward/pallas_call | solution.py:209
  283.0 8.3 %bitcast_convert_fusion = bf16[1024,768]{1,0:T(8,128)(2,1)} fusion(bf16[4,528,1024]{2,1,0:T(8,128)(2,1)} %get-tuple-element.68, bf16[4,528,768]{2,1,0:T(8,128)(2,1)} %get-tuple-element.66.f_hbm), kind=kOutput, calls=%fused_computation | convolution fusion | flops 3322675200 | bytes 9142272 | tf_op jit(solution)/shard_map/rd,re->de/dot_general | solution.py:1618
  291.3 58.5 %finish_rows.1 = (f32[528,1024]{1,0:T(8,128)}, f32[32,3072]{1,0:T(8,128)}, f32[16,1024]{1,0:T(8,128)}) custom-call(bf16[4,528,768]{2,1,0:T(8,128)(2,1)} %get-tuple-element.66.f_hbm, bf16[4,528,1024]{2,1,0:T(8,128)(2,1)} %get-tuple-element.67.xa_hbm, bf16[2,2,8,32,768]{4,3,2,1,0:T(8,128)(2,1)} %bitcast.45, bf16[1024,3072]{1,0:T(8,128)(2,1)} %w_hbm.3, ...), custom_call_target="tpu_custom_call" | custom-call | tf_op jit(solution)/shard_map/finish_rows/pallas_call | solution.py:209
  349.8 1.0 fusion.9
  352.6 4.5 %restore_rows.1 = (bf16[8,64,1024]{2,1,0:T(8,128)(2,1)}, f32[8,64,1024]{2,1,0:T(8,128)}) custom-call(s32[8]{0:T(128)} %copy-done.12, bf16[528,1024]{1,0:T(8,128)(2,1)} %get-tuple-element.51.y_ref, f32[528,1024]{1,0:T(8,128)} %get-tuple-element.71.g_ref), custom_call_target="tpu_custom_call" | custom-call | tf_op jit(solution)/shard_map/restore_rows/pallas_call | solution.py:172
  357.1 0.8 slice_bitcast_fusion
  359.1 0.8 slice_bitcast_fusion.1
  360.5 0.8 slice.34
  361.2 0.6 reshape.328
  361.9 0.7 slice.33
  363.2 0.7 copy.57
  364.0 0.7 copy.58
  364.6 0.8 copy.59
  365.4 0.8 copy.60
  (58 shorter events, 4.9 us)
Async XLA Ops:
  0.7 10.2 %copy-start.6 = (bf16[1024]{0:T(1024)(128)(2,1)S(1)}, bf16[1024]{0:T(1024)(128)(2,1)}, u32[]{:S(2)}) copy-start(bf16[1024]{0:T(1024)(128)(2,1)} %param.28) | copy-start | bytes 6148
  0.7 10.2 %copy-start.7 = (bf16[1024]{0:T(1024)(128)(2,1)S(1)}, bf16[1024]{0:T(1024)(128)(2,1)}, u32[]{:S(2)}) copy-start(bf16[1024]{0:T(1024)(128)(2,1)} %param.29) | copy-start | bytes 6148
  0.7 10.2 %copy-start.5 = (bf16[3072]{0:T(1024)(128)(2,1)S(1)}, bf16[3072]{0:T(1024)(128)(2,1)}, u32[]{:S(2)}) copy-start(bf16[3072]{0:T(1024)(128)(2,1)} %param.31) | copy-start | bytes 18436
  0.7 10.2 %copy-start.4 = (bf16[4096]{0:T(1024)(128)(2,1)S(1)}, bf16[4096]{0:T(1024)(128)(2,1)}, u32[]{:S(2)}) copy-start(bf16[4096]{0:T(1024)(128)(2,1)} %param.37) | copy-start | bytes 24580
  0.7 10.2 %copy-start.8 = (bf16[1024]{0:T(1024)(128)(2,1)S(1)}, bf16[1024]{0:T(1024)(128)(2,1)}, u32[]{:S(2)}) copy-start(bf16[1024]{0:T(1024)(128)(2,1)} %param.33) | copy-start | bytes 6148
  0.7 10.2 %copy-start.9 = (bf16[1024]{0:T(1024)(128)(2,1)S(1)}, bf16[1024]{0:T(1024)(128)(2,1)}, u32[]{:S(2)}) copy-start(bf16[1024]{0:T(1024)(128)(2,1)} %param.34) | copy-start | bytes 6148
  0.7 10.2 %copy-start.10 = (bf16[1024]{0:T(1024)(128)(2,1)S(1)}, bf16[1024]{0:T(1024)(128)(2,1)}, u32[]{:S(2)}) copy-start(bf16[1024]{0:T(1024)(128)(2,1)} %param.35) | copy-start | bytes 6148
  0.7 10.2 %copy-start.11 = (bf16[1024]{0:T(1024)(128)(2,1)S(1)}, bf16[1024]{0:T(1024)(128)(2,1)}, u32[]{:S(2)}) copy-start(bf16[1024]{0:T(1024)(128)(2,1)} %param.39) | copy-start | bytes 6148
  2.4 106.1 %copy-start.12 = (s32[8]{0:T(128)}, s32[8]{0:T(128)S(1)}, u32[]{:S(2)}) copy-start(s32[8]{0:T(128)S(1)} %fusion.8.slot) | copy-start | bytes 100
  2.9 4.1 %copy-start.13 = (s32[8]{0:T(128)}, s32[8]{0:T(128)S(1)}, u32[]{:S(2)}) copy-start(s32[8]{0:T(128)S(1)} %select_reduce_fusion.2.perm) | copy-start | bytes 100
  349.8 13.4 %copy-start.2 = (f32[32,3072]{1,0:T(8,128)S(1)}, f32[32,3072]{1,0:T(8,128)}, u32[]{:S(2)}) copy-start(f32[32,3072]{1,0:T(8,128)} %get-tuple-element.117) | copy-start | bytes 1179652
  350.8 13.1 %copy-start.3 = (f32[32,1024]{1,0:T(8,128)S(1)}, f32[32,1024]{1,0:T(8,128)}, u32[]{:S(2)}) copy-start(f32[32,1024]{1,0:T(8,128)} %get-tuple-element.120) | copy-start | bytes 393220
  352.6 12.0 %copy-start.1 = (f32[32,4096]{1,0:T(8,128)S(1)}, f32[32,4096]{1,0:T(8,128)}, u32[]{:S(2)}) copy-start(f32[32,4096]{1,0:T(8,128)} %get-tuple-element.124) | copy-start | bytes 1572868
  352.6 12.8 %copy-start = (f32[4,32,1024]{2,1,0:T(8,128)S(1)}, f32[4,32,1024]{2,1,0:T(8,128)}, u32[]{:S(2)}) copy-start(f32[4,32,1024]{2,1,0:T(8,128)} %get-tuple-element.78) | copy-start | bytes 1572868

commit v4 on v3

--- a/solution.py
+++ b/solution.py
@@ -465,17 +465,15 @@
 
         def step(j, state):
             tops, totals, blends = state
-            new = ([], [], [])
-            for h in range(GROUP):
-                s = nt(k_ref[j, :, h * 128 : (h + 1) * 128], q_ref[i, :, h * 128 : (h + 1) * 128])
-                top = jnp.maximum(tops[h], jnp.max(s, axis=0, keepdims=True))
-                pt = jnp.exp(s - top)
-                stay = jnp.exp(tops[h] - top)
-                new[0].append(top)
-                new[1].append(totals[h] * stay + jnp.sum(pt, axis=0, keepdims=True))
-                vt = vt_ref[j, h * HEAD_DIM : (h + 1) * HEAD_DIM, :]
-                new[2].append(blends[h] * stay + nn(vt, pt.astype(BF16)))
-            return new
+            cols = [slice(h * 128, (h + 1) * 128) for h in range(GROUP)]
+            scores = [nt(k_ref[j, :, w], q_ref[i, :, w]) for w in cols]
+            peaks = [jnp.maximum(tops[h], jnp.max(scores[h], axis=0, keepdims=True)) for h in range(GROUP)]
+            pts = [jnp.exp(scores[h] - peaks[h]) for h in range(GROUP)]
+            stay = [jnp.exp(tops[h] - peaks[h]) for h in range(GROUP)]
+            sums = [totals[h] * stay[h] + jnp.sum(pts[h], axis=0, keepdims=True) for h in range(GROUP)]
+            lows = [pt.astype(BF16) for pt in pts]
+            more = [nn(vt_ref[j, h * HEAD_DIM : (h + 1) * HEAD_DIM, :], lows[h]) for h in range(GROUP)]
+            return peaks, sums, [blends[h] * stay[h] + more[h] for h in range(GROUP)]
 
         tops, totals, blends = lax.fori_loop(low, i + 1, step, (tops, totals, blends))
         o = jnp.transpose(jnp.concatenate([blends[h] / totals[h] for h in range(GROUP)], axis=0))
@@ -606,6 +604,9 @@
         forward_kernel, "attend_forward", 0, outs, scratch, (x, w_qkv, meta), (params,) + tables, near_outs
     )
 CHUNKS = 9
+EARLY = 3
+LATE = 4
+LAST = CHUNKS - EARLY - LATE
 CUT = D // 2
 QCUT = 3 * GW // 2
 
@@ -663,8 +664,8 @@
 
 
 class Reducer:
-    def __init__(self, at, rb, count, sources, refs):
-        self.at, self.rb, self.count, self.sources = at, rb, count, sources
+    def __init__(self, at, rb, count, sources, refs, ahead=True):
+        self.at, self.rb, self.count, self.sources, self.ahead = at, rb, count, sources, ahead
         (self.mine, self.rd, self.r2a, self.r2b, self.r3a, self.r3b, self.s3, self.r4, self.s4, self.r5, self.fin,
          self.lsem, self.ds, self.dr, self.as2, self.ar2, self.bs2, self.br2, self.as3, self.ar3, self.bs3, self.br3,
          self.s4s, self.s4r, self.s5s, self.s5r) = refs
@@ -728,15 +729,23 @@
         return remote(self.s4.at[k, 1 - self.at.hi], self.r5.at[k], self.s5s.at[k], self.s5r.at[k], self.at.z_two)
 
     def tick(self, t, carry=0):
+        self.run(t, t - 2, t - 4, t - 5, t - 6)
+        return carry
+
+    def run(self, *turns):
         at, rb, count = self.at, self.rb, self.count
         nx, ny, x, y = at.nx, at.ny, at.x, at.y
 
-        @pl.when(t < count)
-        def _():
-            k = t
+        def on(turn, body):
+            k = turns[turn]
+            if k is not None:
+                pl.when((k >= 0) & (k < count))(lambda: body(k))
+
+        def first(k):
             pltpu.make_async_copy(self.rd.at[k], self.mine.at[k], self.lsem.at[k]).wait()
             self.core(k).wait_recv()
-            self.issue(k + 2)
+            if self.ahead:
+                self.issue(k + 2)
             for b in range(ny):
                 for e in range(nx):
                     self.mine[k, b, e] = add_up(self.mine[k, b, e], self.rd[k, b, e]).astype(BF16)
@@ -745,9 +754,7 @@
             for n in range(1, ny):
                 self.b2(k, n).start()
 
-        @pl.when((t >= 2) & (t < count + 2))
-        def _():
-            k = t - 2
+        def second(k):
             for n in range(1, nx):
                 self.a2(k, n).wait_recv()
             for b in range(ny):
@@ -765,9 +772,7 @@
             for n in range(1, nx):
                 self.b3(k, n).start()
 
-        @pl.when((t >= 4) & (t < count + 4))
-        def _():
-            k = t - 4
+        def third(k):
             for n in range(1, ny):
                 self.a3(k, n).wait_recv()
             for n in range(1, nx):
@@ -778,20 +783,17 @@
             self.s3[k, :, :, :, CUT:] = right.reshape(2, 2, rb, CUT)
             self.c4(k).start()
 
-        @pl.when((t >= 5) & (t < count + 5))
-        def _():
-            k = t - 5
+        def fourth(k):
             self.c4(k).wait_recv()
             self.s4[k] = add_up(self.s3[k, :, at.lo], self.r4[k]).astype(BF16)
             self.c5(k).start()
 
-        @pl.when((t >= 6) & (t < count + 6))
-        def _():
-            k = t - 6
+        def fifth(k):
             self.c5(k).wait_recv()
             self.fin[k] = add_up(self.s4[k, at.hi], self.r5[k])
 
-        return carry
+        for turn, body in enumerate((first, second, third, fourth, fifth)):
+            on(turn, body)
 
     def start(self):
         self.issue(0)
@@ -815,21 +817,19 @@
 
 def backward_kernel(
     nx, ny, rb,
-    go_ref, gi_ref, gp_ref, d_ref, q_hbm, k_hbm, v_hbm, o_hbm,
+    go_ref, d_ref, q_hbm, k_hbm, v_hbm, o_hbm,
     qc_ref, kc_ref, vc_ref, lse_ref, lsec_ref, cg_ref, sg_ref, ct_ref, st_ref, meta_ref,
-    oo_ref, oi_ref, op_ref, g_out,
-    q_ref, k_ref, v_ref, o_ref, do_ref, g_ref, acc, accc, kt_ref, right,
+    oo_ref, g_out,
+    q_ref, k_ref, v_ref, o_ref, do_ref, g_ref, acc, accc, kt_ref, right, dqc,
     osem, isem, *refs,
 ):
     at = Place(nx, ny)
     p, c, q, r, z = at.p, at.c, at.hi, at.lo, at.z
     at.greet()
     reducer = Reducer(
-        at, rb, CHUNKS,
+        at, rb, LATE,
         (
-            (4, lambda t, core: go_ref.at[:, :, core, :, t]),
-            (4, lambda t, core: gi_ref.at[:, :, core, :, :, pl.ds(pl.multiple_of(t * D, D), D)]),
-            (1, lambda t, core: gp_ref.at[:, :, core]),
+            (LATE, lambda t, core: go_ref.at[:, :, core, :, t]),
         ),
         refs,
     )
@@ -840,13 +840,54 @@
     for copy in loads:
         copy.start()
 
-    lax.fori_loop(0, 2, reducer.tick, 0)
+    reducer.tick(0)
     cs_col, cs_row, _ = read_meta(meta_ref)
     acc[...] = jnp.zeros_like(acc)
     accc[...] = jnp.zeros_like(accc)
     kct = jnp.transpose(unpad_heads(kc_ref[...].astype(F32))).astype(BF16)
     for copy in loads:
         copy.wait()
+    doc = do_ref[:, VIS:, :].reshape(PART, GW)
+    oc = o_ref[:, VIS:, :].reshape(PART, GW)
+    docp = pad_right(doc)
+    lane = lax.broadcasted_iota(jnp.int32, (PART, WIDE), 1) % 128
+    qcl = jnp.where(lane < HEAD_DIM, qc_ref[...].astype(F32), 0.0).astype(BF16)
+    prod = doc.astype(F32) * oc.astype(F32)
+    lo_col = first_slot(cs_col)
+    near = (cs_row >= lo_col) & (cs_row <= cs_col)
+    deltas = [
+        jnp.sum(prod[:, h * HEAD_DIM : (h + 1) * HEAD_DIM], axis=1, keepdims=True) for h in range(GROUP)
+    ]
+    lses = [lsec_ref[:, h : h + 1] for h in range(GROUP)]
+    dqs = []
+    for h in range(GROUP):
+        cols = slice(h * 128, (h + 1) * 128)
+        s = jnp.where(near, nt(qc_ref[:, cols], kc_ref[:, cols]), NEG)
+        pt = jnp.exp(s - lses[h])
+        dst = pt * (nt(docp[:, cols], vc_ref[:, cols]) - deltas[h])
+        accc[:, cols] += nn(jnp.transpose(pt).astype(BF16), docp[:, cols]) + nn(
+            jnp.transpose(dst).astype(BF16), qcl[:, cols]
+        )
+        dqs.append(nn(dst.astype(BF16), kc_ref[:, cols]))
+
+    def cond_step(j, dqs):
+        near = (lo_col <= j) & (cs_col >= j)
+        new = []
+        for h in range(GROUP):
+            cols = slice(h * 128, (h + 1) * 128)
+            s = jnp.where(near, nt(qc_ref[:, cols], k_ref[j, :, cols]), NEG)
+            pt = jnp.exp(s - lses[h])
+            dst = pt * (nt(docp[:, cols], v_ref[j, :, cols]) - deltas[h])
+            acc[j, :, cols] += nn(jnp.transpose(pt).astype(BF16), docp[:, cols]) + nn(
+                jnp.transpose(dst).astype(BF16), qcl[:, cols]
+            )
+            new.append(dqs[h] + nn(dst.astype(BF16), k_ref[j, :, cols]))
+        return new
+
+    dqs = lax.fori_loop(0, FRAMES, cond_step, dqs)
+    dqc[...] = jnp.concatenate([t[:, :HEAD_DIM] for t in dqs], axis=1) * 0.125
+    reducer.tick(1)
+
     def slot(i):
         start = pl.multiple_of(i * PART, PART)
         do = do_ref[:, pl.ds(start, PART), :].reshape(PATCHES, GW)
@@ -871,14 +912,15 @@
             dqs.append(nn(kct[h * HEAD_DIM : (h + 1) * HEAD_DIM], dst))
 
         def step(j, dqs):
-            new = []
+            cols = [slice(h * 128, (h + 1) * 128) for h in range(GROUP)]
+            scores = [nt(k_ref[j, :, w], q_ref[i, :, w]) for w in cols]
+            grads = [nt(v_ref[j, :, w], right[0:PATCHES, w]) for w in cols]
+            pts = [jnp.exp(scores[h] - lse_ref[i, h : h + 1, :]) for h in range(GROUP)]
+            dsts = [(pts[h] * (grads[h] - deltas[h])).astype(BF16) for h in range(GROUP)]
+            both = [jnp.concatenate([pts[h].astype(BF16), dsts[h]], axis=1) for h in range(GROUP)]
             for h in range(GROUP):
-                cols = slice(h * 128, (h + 1) * 128)
-                pt = jnp.exp(nt(k_ref[j, :, cols], q_ref[i, :, cols]) - lse_ref[i, h : h + 1, :])
-                dst = (pt * (nt(v_ref[j, :, cols], right[0:PATCHES, cols]) - deltas[h])).astype(BF16)
-                acc[j, :, cols] += nn(jnp.concatenate([pt.astype(BF16), dst], axis=1), right[:, cols])
-                new.append(dqs[h] + nn(kt_ref[j, h * HEAD_DIM : (h + 1) * HEAD_DIM, :], dst))
-            return new
+                acc[j, :, cols[h]] += nn(both[h], right[:, cols[h]])
+            return [dqs[h] + nn(kt_ref[j, h * HEAD_DIM : (h + 1) * HEAD_DIM, :], dsts[h]) for h in range(GROUP)]
 
         dqs = lax.fori_loop(low, i + 1, step, dqs)
         dq = jnp.transpose(jnp.concatenate(dqs, axis=0)) * 0.125
@@ -894,47 +936,9 @@
 
     lax.fori_loop(0, FRAMES, sweep, 0)
 
-    doc = do_ref[:, VIS:, :].reshape(PART, GW)
-    oc = o_ref[:, VIS:, :].reshape(PART, GW)
-    docp = pad_right(doc)
-    lane = lax.broadcasted_iota(jnp.int32, (PART, WIDE), 1) % 128
-    qcl = jnp.where(lane < HEAD_DIM, qc_ref[...].astype(F32), 0.0).astype(BF16)
-    prod = doc.astype(F32) * oc.astype(F32)
-    lo_col = first_slot(cs_col)
-    near = (cs_row >= lo_col) & (cs_row <= cs_col)
-    deltas = [
-        jnp.sum(prod[:, h * HEAD_DIM : (h + 1) * HEAD_DIM], axis=1, keepdims=True) for h in range(GROUP)
-    ]
-    lses = [lsec_ref[:, h : h + 1] for h in range(GROUP)]
-    dqs = []
-    for h in range(GROUP):
-        cols = slice(h * 128, (h + 1) * 128)
-        s = jnp.where(near, nt(qc_ref[:, cols], kc_ref[:, cols]), NEG)
-        pt = jnp.exp(s - lses[h])
-        dst = pt * (nt(docp[:, cols], vc_ref[:, cols]) - deltas[h])
-        accc[:, cols] += nn(jnp.transpose(pt).astype(BF16), docp[:, cols]) + nn(
-            jnp.transpose(dst).astype(BF16), qcl[:, cols]
-        )
-        dqs.append(nn(dst.astype(BF16), kc_ref[:, cols]))
-
-    def cond_step(j, dqs):
-        near = (lo_col <= j) & (cs_col >= j)
-        new = []
-        for h in range(GROUP):
-            cols = slice(h * 128, (h + 1) * 128)
-            s = jnp.where(near, nt(qc_ref[:, cols], k_ref[j, :, cols]), NEG)
-            pt = jnp.exp(s - lses[h])
-            dst = pt * (nt(docp[:, cols], v_ref[j, :, cols]) - deltas[h])
-            acc[j, :, cols] += nn(jnp.transpose(pt).astype(BF16), docp[:, cols]) + nn(
-                jnp.transpose(dst).astype(BF16), qcl[:, cols]
-            )
-            new.append(dqs[h] + nn(dst.astype(BF16), k_ref[j, :, cols]))
-        return new
-
-    dqs = lax.fori_loop(0, FRAMES, cond_step, dqs)
     cosine, sine = cond_tables(cs_col, ct_ref[...], st_ref[...])
     valid = cs_col < FRAMES
-    dq = jnp.concatenate([t[:, :HEAD_DIM] for t in dqs], axis=1) * 0.125
+    dq = dqc[...]
     both = accc[...]
     parts = (turn(dq, cosine, -sine), turn(unpad_heads(both), cosine, -sine), unpad_right(both))
     for part, t in enumerate(parts):
@@ -954,13 +958,8 @@
     lax.fori_loop(0, FRAMES, finish, 0)
     save = pltpu.make_async_copy(g_ref, g_out, isem.at[5])
     save.start()
-    lax.fori_loop(10, CHUNKS + 6, reducer.tick, 0)
     fin = reducer.fin
     outs = [pltpu.make_async_copy(fin.at[k], oo_ref.at[k], osem.at[k]) for k in range(4)]
-    outs += [
-        pltpu.make_async_copy(fin.at[k], oi_ref.at[:, pl.ds((k - 4) * D, D)], osem.at[k]) for k in range(4, 8)
-    ]
-    outs += [pltpu.make_async_copy(fin.at[8], op_ref, osem.at[8])]
     for copy in outs:
         copy.start()
 
@@ -974,7 +973,7 @@
     return jnp.concatenate([t[:, h * 128 + HEAD_DIM : (h + 1) * 128] for h in range(GROUP)], axis=1)
 
 
-def attend_backward(g_out, g_in, g_proj, grad_o, saved, o, tables, meta):
+def attend_backward(g_out, grad_o, saved, o, tables, meta):
     nx, ny, rb = grid_shape()
     q, k, v, *rest = saved
 
@@ -984,13 +983,11 @@
     scratch = [
         v16(*q.shape), v16(*k.shape), v16(*v.shape), v16(*o.shape), v16(*o.shape), v16(STREAMS, ROWS, 3 * GW),
         VM((FRAMES, PATCHES, WIDE), F32), VM((PART, WIDE), F32), v16(FRAMES, GW, PATCHES), v16(2 * PATCHES, WIDE),
-        dma(CHUNKS), dma(6),
-    ] + Reducer.scratch(CHUNKS, nx, ny, rb)
-    outs = (((4, rb, D), F32), ((rb, 4 * D), F32), ((rb, D), F32), ((STREAMS, ROWS, 3 * GW), BF16))
-    ops = (
-        g_out.reshape(ny, nx, 2, STREAMS, 4, rb, D), g_in.reshape(ny, nx, 2, STREAMS, rb, 4 * D),
-        g_proj.reshape(ny, nx, 2, STREAMS, rb, D), grad_o, q, k, v, o,
-    )
+        VM((PART, GW), F32),
+        dma(LATE), dma(6),
+    ] + Reducer.scratch(LATE, nx, ny, rb)
+    outs = (((4, rb, D), F32), ((STREAMS, ROWS, 3 * GW), BF16))
+    ops = (g_out.reshape(ny, nx, 2, STREAMS, 4, rb, D), grad_o, q, k, v, o)
     return comm_call(
         functools.partial(backward_kernel, nx, ny, rb), "attend_backward", 3, outs, scratch, ops,
         tuple(rest) + tables + (meta,),
@@ -999,17 +996,23 @@
 
 def finish_kernel(
     nx, ny, rb,
-    f_hbm, xa_hbm, gq_ref, w_hbm, x_hbm, h_hbm, v_ref, gain_ref,
-    gx_ref, oq_ref, ov_ref,
+    f_hbm, xa_hbm, gq_ref, w_hbm, x_hbm, h_hbm, gi_ref, gp_ref, v_ref, gain_ref,
+    gx_ref, oq_ref, ov_ref, oi_ref, op_ref,
     f, xa, w, x_own, h_own, big, near_in, near_out, own, land, tail, tail_out, total,
     q1, rq1a, rq1b, sq1a, sq1b, rq2a, rq2b, sq2, rq3, sq3, vm, vd, vx, vy, vz1, vz2, hold,
     isem, dsend, drecv, send, recv, csend, crecv, lsem,
-    qs1a, qr1a, qs1b, qr1b, qs2a, qr2a, qs2b, qr2b, qs3, qr3, qs4, qr4, vs, vr, vsx, vrx, vsy, vry, relay, rsend, rrecv, cols_sum,
+    qs1a, qr1a, qs1b, qr1b, qs2a, qr2a, qs2b, qr2b, qs3, qr3, qs4, qr4, vs, vr, vsx, vrx, vsy, vry, relay, rsend, rrecv, cols_sum, osem,
+    *refs,
 ):
     at = Place(nx, ny)
     p, c, q, r, z, x, y, hi, lo = at.p, at.c, at.hi, at.lo, at.z, at.x, at.y, at.hi, at.lo
     group = 2 * r + c
     in_pair, inner = q == c, z == 1 + q
+    reducer = Reducer(
+        at, rb, LAST,
+        ((LAST - 1, lambda t, core: gi_ref.at[:, :, core]), (1, lambda t, core: gp_ref.at[:, :, core])),
+        refs, ahead=False,
+    )
     loads = []
     for part in range(3):
         cols = pl.ds(pl.multiple_of(part * D + group * GW, GW), GW)
@@ -1106,6 +1109,8 @@
         def _():
             far(s)
 
+    for k in range(LAST):
+        reducer.issue(jnp.int32(k))
     late[0].wait()
     for n in range(1, nx):
         q1a(n).start()
@@ -1179,6 +1184,15 @@
 
     lax.fori_loop(0, STREAMS, partial_rows, 0)
     pass_on(STREAMS - 1)
+
+    def move(turn):
+        def one(k, carry):
+            reducer.run(*[k if n == turn else None for n in range(5)])
+            return carry
+
+        lax.fori_loop(0, LAST, one, 0)
+
+    move(0)
     vm[0] = v_ref[...]
     vm[0, 0:1] = jnp.sum(hold[0], axis=0, keepdims=True)
     vm[0, 1:2] = jnp.sum(hold[1], axis=0, keepdims=True)
@@ -1204,6 +1218,7 @@
     for n in range(1, nx):
         v_x(n).start()
     pass_far(0)
+    move(1)
     for n in range(1, ny):
         q2a(n).wait_recv()
     for n in range(1, nx):
@@ -1223,6 +1238,7 @@
     vm[3] = add_up(vm[2], *[vy[n] for n in range(ny - 1)])
     v_z1().start()
     pass_far(1)
+    move(2)
     q3().wait_recv()
     sq3[...] = add_up(sq2[:, hi], rq3[...])
     for part in range(3):
@@ -1232,6 +1248,7 @@
     v_z1().wait_recv()
     vm[4] = vm[3] + vz1[...]
     v_z2().start()
+    move(3)
 
     late[1].wait()
     late[2].wait()
@@ -1275,6 +1292,13 @@
     back(last, add_up(tail[0], tail[1], tail[2], tail[3]))
     done = pltpu.make_async_copy(total, gx_ref, lsem.at[5])
     done.start()
+    move(4)
+    outs = [
+        pltpu.make_async_copy(reducer.fin.at[k], oi_ref.at[:, pl.ds(k * D, D)], osem.at[k]) for k in range(LAST - 1)
+    ]
+    outs += [pltpu.make_async_copy(reducer.fin.at[LAST - 1], op_ref, osem.at[LAST - 1])]
+    for copy in outs:
+        copy.start()
     v_z2().wait_recv()
     vm[5] = vm[4] + vz2[...]
     v_done = pltpu.make_async_copy(vm.at[5], ov_ref, lsem.at[6])
@@ -1314,11 +1338,14 @@
         for n in range(3):
             q4(n, part).wait_send()
             q4(n, part).wait_recv()
+    reducer.drain()
+    for copy in outs:
+        copy.wait()
     done.wait()
     v_done.wait()
 
 
-def finish_rows(flat, x_all, g_qkv, w_qkv, x, h, vectors, gain):
+def finish_rows(flat, x_all, g_qkv, w_qkv, x, h, g_in, g_proj, vectors, gain):
     nx, ny, rb = grid_shape()
 
     def v(*shape):
@@ -1339,10 +1366,15 @@
         dma(nx - 1), dma(nx - 1), dma(ny - 1), dma(ny - 1), dma(ny - 1), dma(ny - 1), dma(nx - 1), dma(nx - 1),
         pltpu.SemaphoreType.DMA, pltpu.SemaphoreType.DMA, dma(3, 3), dma(3, 3),
         dma(3), dma(3), dma(nx - 1), dma(nx - 1), dma(ny - 1), dma(ny - 1),
-        v(2, HALF, D), dma(2), dma(2), vf(8, 3 * GW),
-    ]
-    outs = (((ROWS, D), F32), ((rb, 3 * D), F32), ((16, D), F32))
-    ops = (flat, x_all, g_qkv.reshape(ny, nx, 8, rb, 3 * GW), w_qkv, x, h)
+        v(2, HALF, D), dma(2), dma(2), vf(8, 3 * GW), dma(LAST),
+    ] + Reducer.scratch(LAST, nx, ny, rb)
+    outs = (
+        ((ROWS, D), F32), ((rb, 3 * D), F32), ((16, D), F32), ((rb, (LAST - 1) * D), F32), ((rb, D), F32),
+    )
+    ops = (
+        flat, x_all, g_qkv.reshape(ny, nx, 8, rb, 3 * GW), w_qkv, x, h,
+        g_in.reshape(ny, nx, 2, STREAMS, rb, (LAST - 1) * D), g_proj.reshape(ny, nx, 2, STREAMS, rb, D),
+    )
     return comm_call(
         functools.partial(finish_kernel, nx, ny, rb), "finish_rows", 4, outs, scratch, ops, (vectors, gain)
     )
@@ -1357,12 +1389,15 @@
 
 
 def mlp_kernel(
+    nx, ny, rb,
     win_hbm, wout_hbm, att_ref, x_ref, dy_ref, wp_ref, par_ref,
-    do_out, gi_out, go_out, gp_out, y_ref, gh_ref, vec_ref,
+    do_out, gi_out, go_out, gp_out, oi_ref, y_ref, gh_ref, vec_ref,
     wi, wo, n_ref, h_ref, buf, dbuf, hid, du, yacc, dn, dhb, do_ref, stage, sums,
-    isem, ssem, hs, hr, hl,
+    gi, isem, ssem, hs, hr, hl, osem, *refs,
 ):
-    p, c, q, r, z = where_am_i()
+    at = Place(nx, ny)
+    p, c, q, r, z = at.p, at.c, at.hi, at.lo, at.z
+    reducer = Reducer(at, rb, EARLY, ((EARLY, lambda t, core: gi.at[t, :, :, core]),), refs, ahead=False)
 
     def fetch(t, slot):
         cols = pl.ds(pl.multiple_of(t * D, D), D)
@@ -1373,7 +1408,7 @@
 
     for copy in fetch(0, 0):
         copy.start()
-    greet_column()
+    at.greet()
     sums[...] = jnp.zeros_like(sums)
     for j in range(2):
         cols = slice(j * CUT, (j + 1) * CUT)
@@ -1409,6 +1444,7 @@
             for copy in fetch(t + 1, 1 - slot):
                 copy.start()
 
+        reducer.run(t - 1, None, t - 2, None, t - 3)
         for j in range(2):
             cols = slice(j * CUT, (j + 1) * CUT)
             buf[:, cols] = nn(n_ref[...], wi[slot, :, cols])
@@ -1424,7 +1460,7 @@
                 hid[rows, pl.ds(pl.multiple_of(t * D + j * 256, 256), 256)] = (u * phi).astype(BF16)
                 slope = phi + u * (jnp.exp(-0.5 * u * u) * ((2.0 * math.pi) ** -0.5))
                 g = (dbuf[rows, cols] * slope).astype(BF16)
-                du[rows, pl.ds(pl.multiple_of(t * D + j * 256, 256), 256)] = g
+                du[rows, cols] = g
                 g = g.astype(F32)
                 total = g[0:8]
                 for m in range(1, TILE // 8):
@@ -1433,10 +1469,19 @@
             return carry
 
         lax.fori_loop(0, TILES, act, 0)
+
+        @pl.when(t < EARLY)
+        def _():
+            for b in range(ny):
+                block_rows = tn(n_ref[:, b * (D // ny) : (b + 1) * (D // ny)], du[...])
+                gi[t, b] = block_rows.astype(BF16).reshape(nx, 2, STREAMS, rb, D)
+            reducer.issue(t)
+
+        reducer.run(None, t - 1, None, t - 2, None)
         for j in range(2):
             cols = slice(j * CUT, (j + 1) * CUT)
             more = nn(hid[:, place], wo[slot, :, cols])
-            back = nt(du[:, place], wi[slot, cols, :])
+            back = nt(du[...], wi[slot, cols, :])
 
             @pl.when(t == 0)
             def _():
@@ -1451,6 +1496,7 @@
         return carry
 
     lax.fori_loop(0, 4, block, 0)
+    reducer.run(None, None, EARLY - 1, None, EARLY - 2)
 
     def leave(t, carry):
         rows = tile(t)
@@ -1475,6 +1521,7 @@
         return carry
 
     lax.fori_loop(0, TILES, leave, 0)
+    reducer.run(None, None, None, EARLY - 1, None)
     for j in range(2):
         rows = slice(j * CUT, (j + 1) * CUT)
         do_ref[:, rows] = nt(dhb[...], wp_ref[rows, :]).astype(BF16)
@@ -1501,41 +1548,39 @@
     for n in range(8):
         vec_ref[5 + n : 6 + n] = jnp.sum(sums[n], axis=0, keepdims=True)
 
-    def in_save(t):
-        return pltpu.make_async_copy(stage.at[0], gi_out.at[:, pl.ds(pl.multiple_of(t * D, D), D)], ssem.at[0])
-
-    def out_save(t):
-        return pltpu.make_async_copy(stage.at[1], go_out.at[pl.ds(pl.multiple_of(t * D, D), D), :], ssem.at[1])
+    def out_save(t, slot):
+        return pltpu.make_async_copy(stage.at[slot], go_out.at[pl.ds(pl.multiple_of(t * D, D), D), :], ssem.at[slot])
 
     def weights(t, carry):
-        @pl.when(t > 0)
+        slot = t % 2
+
+        @pl.when(t > 1)
         def _():
-            in_save(t - 1).wait()
-
-        for m in range(2):
-            half = pl.ds(m * CUT, CUT)
-            place = pl.ds(pl.multiple_of(t * D, D), D)
-            stage[0, half, :] = tn(n_ref[:, half], du[:, place]).astype(BF16)
-        in_save(t).start()
-
-        @pl.when(t > 0)
-        def _():
-            out_save(t - 1).wait()
+            out_save(t - 2, slot).wait()
 
         for m in range(2):
             half = pl.ds(m * CUT, CUT)
             place = pl.ds(pl.multiple_of(t * D + m * CUT, CUT), CUT)
-            stage[1, half, :] = tn(hid[:, place], dy_ref[...]).astype(BF16)
-        out_save(t).start()
+            stage[slot, half, :] = tn(hid[:, place], dy_ref[...]).astype(BF16)
+        out_save(t, slot).start()
         return carry
 
     lax.fori_loop(0, 4, weights, 0)
-    in_save(3).wait()
-    for m in range(2):
-        half = pl.ds(m * CUT, CUT)
-        stage[0, half, :] = tn(att_ref[:, half], dhb[...]).astype(BF16)
-    proj_save = pltpu.make_async_copy(stage.at[0], gp_out, ssem.at[0])
-    proj_save.start()
+    saves = []
+    for slot, (lhs, rhs, out) in enumerate(((att_ref, dhb, gp_out), (n_ref, du, gi_out))):
+        out_save(2 + slot, slot).wait()
+        for m in range(2):
+            half = pl.ds(m * CUT, CUT)
+            stage[slot, half, :] = tn(lhs[:, half], rhs[...]).astype(BF16)
+        saves.append(pltpu.make_async_copy(stage.at[slot], out, ssem.at[slot]))
+        saves[-1].start()
+    reducer.run(None, None, None, None, EARLY - 1)
+    fin_saves = [
+        pltpu.make_async_copy(reducer.fin.at[k], oi_ref.at[:, pl.ds(k * D, D)], osem.at[k]) for k in range(EARLY)
+    ]
+    for copy in fin_saves:
+        copy.start()
+    reducer.drain()
     for g in range(4):
         self_made = (g % 2 == c) & (2 * c + g // 2 == z)
 
@@ -1550,11 +1595,13 @@
         @pl.when((q != c) | (s != z))
         def _():
             remote(do_ref.at[:, pl.ds(0, GW)], do_out.at[s], hs.at[0], hr.at[s], (2 * p + 1 - c, z)).wait_recv()
-    out_save(3).wait()
-    proj_save.wait()
+    for copy in saves + fin_saves:
+        copy.wait()
 
 
 def mlp(w_in, w_out, attended, x, dy, w_proj, params):
+    nx, ny, rb = grid_shape()
+
     def v16(*shape):
         return VM(shape, BF16)
 
@@ -1563,14 +1610,17 @@
 
     scratch = [
         v16(2, D, D), v16(2, D, D), v16(ROWS, D), vf(ROWS, D), vf(ROWS, D), vf(ROWS, D),
-        v16(ROWS, 4 * D), v16(ROWS, 4 * D), vf(ROWS, D), vf(ROWS, D), v16(ROWS, D), v16(ROWS, D),
-        v16(2, D, D), vf(8, 8, D),
-        dma(2, 2), dma(2), dma(4), dma(4), pltpu.SemaphoreType.DMA,
-    ]
-    outs = (((STREAMS, ROWS, GW), BF16), ((D, 4 * D), BF16), ((4 * D, D), BF16), ((D, D), BF16))
+        v16(ROWS, 4 * D), v16(ROWS, D), vf(ROWS, D), vf(ROWS, D), v16(ROWS, D), v16(ROWS, D),
+        v16(2, D, D), vf(8, 8, D), v16(EARLY, ny, nx, 2, STREAMS, rb, D),
+        dma(2, 2), dma(2), dma(4), dma(4), pltpu.SemaphoreType.DMA, dma(EARLY),
+    ] + Reducer.scratch(EARLY, nx, ny, rb)
+    outs = (
+        ((STREAMS, ROWS, GW), BF16), ((D, (4 - EARLY) * D), BF16), ((4 * D, D), BF16), ((D, D), BF16),
+        ((rb, EARLY * D), F32),
+    )
     near_outs = (((ROWS, D), BF16), ((ROWS, D), F32), ((16, D), F32))
     return comm_call(
-        mlp_kernel, "mlp", 1, outs, scratch, (w_in, w_out), (attended, x, dy, w_proj, params), near_outs
+        functools.partial(mlp_kernel, nx, ny, rb), "mlp", 1, outs, scratch, (w_in, w_out), (attended, x, dy, w_proj, params), near_outs
     )
 
 
@@ -1609,18 +1659,17 @@
     ).astype(F32).reshape(16, D)
     tables = tuple(jnp.asarray(t) for t in rope_constants())
     attended, x_all, a, q, k, v, o, meta, *rest = attend_forward(x, w_qkv, own, params, tables)
-    grad_heads, grad_w_in, grad_w_out, grad_w_proj, output, grad_h, vectors = mlp(
+    grad_heads, grad_w_in, grad_w_out, grad_w_proj, red_in, output, grad_h, vectors = mlp(
         w_in, w_out, attended, x, dy, w_proj, params
     )
-    red_out, red_in, red_proj, grad_qkv = attend_backward(
-        grad_w_out, grad_w_in, grad_w_proj, grad_heads, (q, k, v, *rest), o, tables, meta
-    )
+    red_out, grad_qkv = attend_backward(grad_w_out, grad_heads, (q, k, v, *rest), o, tables, meta)
     role_grad = jnp.einsum(
         "rd,re->de", a.reshape(STREAMS * ROWS, D), grad_qkv.reshape(STREAMS * ROWS, 3 * GW), preferred_element_type=F32
     )
-    grad_x, red_qkv, sums = finish_rows(
-        grad_qkv, x_all, role_grad.astype(BF16), w_qkv, x, grad_h, vectors, params
-    )
+    grad_x, red_qkv, sums, red_in_last, red_proj = finish_rows(
+        grad_qkv, x_all, role_grad.astype(BF16), w_qkv, x, grad_h, grad_w_in, grad_w_proj, vectors, params
+    )
+    red_in = jnp.concatenate([red_in, red_in_last], axis=1)
     out_visual, grad_visual = restore_rows(slot, output, grad_x)
     owner = d * STREAMS + z
     owners = lax.axis_size("dp") * STREAMS

time: 367 us -> 342 us (0.932)
  Pallas kernels: 338 us -> 311 us
    pallas_call x4, Pallas kernels: 330 us -> 303 us  [comm_call(): pl.pallas_call(kernel, name=name, out_shape=tuple((jax.ShapeDtypeStruct(s...]
where the time goes in v4:
time: 342 us; the launch traced here: 340 us
  Pallas kernels  311 us (91%)
  local copies, waits for them, and re-layouts  14.6 us (4%)
  matrix products  8.31 us (2%)
  other arithmetic  5.3 us (2%)
    pallas_call x4, Pallas kernels, comm_call(): pl.pallas_call(kernel, name=name, out_shape=tuple((jax.ShapeDtypeStruct(s...  303 us
    dot_general x1, matrix products, per_device(): jnp.einsum('rd,re->de', a.reshape(STREAMS * ROWS, D), grad_qkv.reshape(ST...  8.31 us

profile of v4, /device:TPU:0, one launch (start us, length us, event | category | flops | bytes accessed | tf_op | source)
XLA Modules:
  0.0 340.3 jit_solution(6402888770759692205)
XLA Ops:
  0.7 0.9 reduce-window.8
  1.7 0.7 select_reduce_fusion.4
  3.0 0.7 select_bitcast_fusion
  3.8 0.6 select_maximum_fusion.m_hbm
  4.4 1.3 reshape.318.xc_ref
  5.7 1.3 reshape.320.dc_ref
  7.0 3.8 %place_rows.1 = (bf16[528,1024]{1,0:T(8,128)(2,1)}, bf16[528,1024]{1,0:T(8,128)(2,1)}) custom-call(s32[8]{0:T(128)} %copy-done.13, bf16[8,64,1024]{2,1,0:T(8,128)(2,1)} %bitcast.46, bf16[4,1024]{1,0:T(4,128)(2,1)} %reshape.318.xc_ref, bf16[8,64,1024]{2,1,0:T(8,128)(2,1)} %bitcast.47, bf16[4,1024]{1,0:T(4,128)(2,1)} %reshape.320.dc_ref), custom_call_target="tpu_custom_call" | custom-call | tf_op jit(solution)/shard_map/place_rows/pallas_call | solution.py:148
  11.0 0.6 reshape.333.par_ref.gain_ref
  11.7 85.1 %attend_forward.1 = (bf16[528,1024]{1,0:T(8,128)(2,1)}, bf16[4,528,1024]{2,1,0:T(8,128)(2,1)}, bf16[4,528,1024]{2,1,0:T(8,128)(2,1)}, bf16[8,256,512]{2,1,0:T(8,...) custom-call(bf16[528,1024]{1,0:T(8,128)(2,1)} %get-tuple-element.49., ...), custom_call_target="tpu_custom_call" | custom-call | tf_op jit(solution)/shard_map/attend_forward/pallas_call | solution.py:209
  96.8 74.7 %mlp.1 = (bf16[4,528,256]{2,1,0:T(8,128)(2,1)}, bf16[1024,1024]{1,0:T(8,128)(2,1)}, bf16[4096,1024]{1,0:T(8,128)(2,1)}, bf16[1024,1024]{1,0:T(8,128)(2,1)}, f32[...) custom-call(bf16[1024,4096]{1,0:T(8,128)(2,1)} %win_hbm.1, ...), custom_call_target="tpu_custom_call" | custom-call | tf_op jit(solution)/shard_map/mlp/pallas_call | solution.py:209
  171.5 78.6 %attend_backward.1 = (f32[4,32,1024]{2,1,0:T(8,128)}, bf16[4,528,768]{2,1,0:T(8,128)(2,1)}) custom-call(bf16[2,2,2,4,4,32,1024]{6,5,4,3,2,1,0:T(8,128)(2,1)} %bitcast.42, bf16[4,528,256]{2,1,0:T(8,128)(2,1)} %get-tuple-element.54.d_ref, bf16[8,256,512]{2,1,0:T(8,128)(2,1)} %get-tuple-element.55.q_hbm, bf16[8,256,512]{2,1,0:T(8,128)(2,1)} %get-tuple-element.56.k_hbm, ...), custom_call_target="tpu_custom_call" | custom-call | tf_op jit(solution)/shard_map/attend_backward/pallas_call | solution.py:209
  250.1 8.3 %bitcast_convert_fusion = bf16[1024,768]{1,0:T(8,128)(2,1)} fusion(bf16[4,528,1024]{2,1,0:T(8,128)(2,1)} %get-tuple-element.67, bf16[4,528,768]{2,1,0:T(8,128)(2,1)} %get-tuple-element.65.f_hbm), kind=kOutput, calls=%fused_computation | convolution fusion | flops 3322675200 | bytes 9142272 | tf_op jit(solution)/shard_map/rd,re->de/dot_general | solution.py:1666
  258.4 64.4 %finish_rows.1 = (f32[528,1024]{1,0:T(8,128)}, f32[32,3072]{1,0:T(8,128)}, f32[16,1024]{1,0:T(8,128)}, f32[32,1024]{1,0:T(8,128)}, f32[32,1024]{1,0:T(8,128)}) custom-call(bf16[4,528,768]{2,1,0:T(8,128)(2,1)} %get-tuple-element.65.f_hbm, bf16[4,528,1024]{2,1,0:T(8,128)(2,1)} %get-tuple-element.66.xa_hbm, bf16[2,2,8,32,768]{4,3,2,1,0:T(8,128)(2,1)} %bitcast.45, ...), custom_call_target="tpu_custom_call" | custom-call | tf_op jit(solution)/shard_map/finish_rows/pallas_call | solution.py:209
  322.9 1.8 pad_maximum_fusion
  324.6 1.1 fusion.9
  327.5 4.5 %restore_rows.1 = (bf16[8,64,1024]{2,1,0:T(8,128)(2,1)}, f32[8,64,1024]{2,1,0:T(8,128)}) custom-call(s32[8]{0:T(128)} %copy-done.12, bf16[528,1024]{1,0:T(8,128)(2,1)} %get-tuple-element.52.y_ref, f32[528,1024]{1,0:T(8,128)} %get-tuple-element.72.g_ref), custom_call_target="tpu_custom_call" | custom-call | tf_op jit(solution)/shard_map/restore_rows/pallas_call | solution.py:172
  332.0 0.8 slice_bitcast_fusion
  334.0 0.8 slice_bitcast_fusion.1
  335.3 0.8 slice.34
  336.1 0.6 reshape.328
  336.7 0.7 slice.33
  338.1 0.7 copy.56
  338.8 0.7 copy.57
  339.5 0.8 copy.58
  (58 shorter events, 4.9 us)
Async XLA Ops:
  0.7 10.2 %copy-start.6 = (bf16[1024]{0:T(1024)(128)(2,1)S(1)}, bf16[1024]{0:T(1024)(128)(2,1)}, u32[]{:S(2)}) copy-start(bf16[1024]{0:T(1024)(128)(2,1)} %param.28) | copy-start | bytes 6148
  0.7 10.2 %copy-start.7 = (bf16[1024]{0:T(1024)(128)(2,1)S(1)}, bf16[1024]{0:T(1024)(128)(2,1)}, u32[]{:S(2)}) copy-start(bf16[1024]{0:T(1024)(128)(2,1)} %param.29) | copy-start | bytes 6148
  0.7 10.2 %copy-start.5 = (bf16[3072]{0:T(1024)(128)(2,1)S(1)}, bf16[3072]{0:T(1024)(128)(2,1)}, u32[]{:S(2)}) copy-start(bf16[3072]{0:T(1024)(128)(2,1)} %param.31) | copy-start | bytes 18436
  0.7 10.2 %copy-start.4 = (bf16[4096]{0:T(1024)(128)(2,1)S(1)}, bf16[4096]{0:T(1024)(128)(2,1)}, u32[]{:S(2)}) copy-start(bf16[4096]{0:T(1024)(128)(2,1)} %param.37) | copy-start | bytes 24580
  0.7 10.2 %copy-start.8 = (bf16[1024]{0:T(1024)(128)(2,1)S(1)}, bf16[1024]{0:T(1024)(128)(2,1)}, u32[]{:S(2)}) copy-start(bf16[1024]{0:T(1024)(128)(2,1)} %param.33) | copy-start | bytes 6148
  0.7 10.2 %copy-start.9 = (bf16[1024]{0:T(1024)(128)(2,1)S(1)}, bf16[1024]{0:T(1024)(128)(2,1)}, u32[]{:S(2)}) copy-start(bf16[1024]{0:T(1024)(128)(2,1)} %param.34) | copy-start | bytes 6148
  0.7 10.3 %copy-start.10 = (bf16[1024]{0:T(1024)(128)(2,1)S(1)}, bf16[1024]{0:T(1024)(128)(2,1)}, u32[]{:S(2)}) copy-start(bf16[1024]{0:T(1024)(128)(2,1)} %param.35) | copy-start | bytes 6148
  0.7 10.3 %copy-start.11 = (bf16[1024]{0:T(1024)(128)(2,1)S(1)}, bf16[1024]{0:T(1024)(128)(2,1)}, u32[]{:S(2)}) copy-start(bf16[1024]{0:T(1024)(128)(2,1)} %param.39) | copy-start | bytes 6148
  2.4 94.3 %copy-start.12 = (s32[8]{0:T(128)}, s32[8]{0:T(128)S(1)}, u32[]{:S(2)}) copy-start(s32[8]{0:T(128)S(1)} %fusion.8.slot) | copy-start | bytes 100
  2.9 4.1 %copy-start.13 = (s32[8]{0:T(128)}, s32[8]{0:T(128)S(1)}, u32[]{:S(2)}) copy-start(s32[8]{0:T(128)S(1)} %select_reduce_fusion.2.perm) | copy-start | bytes 100
  258.4 64.4 %copy-start.2 = (f32[32,3072]{1,0:T(8,128)S(1)}, f32[32,3072]{1,0:T(8,128)}, u32[]{:S(2)}) copy-start(f32[32,3072]{1,0:T(8,128)} %get-tuple-element.78) | copy-start | bytes 1179652
  322.8 15.2 %copy-start.1 = (f32[32,3072]{1,0:T(8,128)S(1)}, f32[32,3072]{1,0:T(8,128)}, u32[]{:S(2)}) copy-start(f32[32,3072]{1,0:T(8,128)} %get-tuple-element.119) | copy-start | bytes 1179652
  325.7 13.1 %copy-start.3 = (f32[32,1024]{1,0:T(8,128)S(1)}, f32[32,1024]{1,0:T(8,128)}, u32[]{:S(2)}) copy-start(f32[32,1024]{1,0:T(8,128)} %get-tuple-element.122) | copy-start | bytes 393220
  327.5 12.0 %copy-start = (f32[4,32,1024]{2,1,0:T(8,128)S(1)}, f32[4,32,1024]{2,1,0:T(8,128)}, u32[]{:S(2)}) copy-start(f32[4,32,1024]{2,1,0:T(8,128)} %get-tuple-element.80) | copy-start | bytes 1572868

commit v5 on v4

--- a/solution.py
+++ b/solution.py
@@ -139,7 +139,8 @@
         copy.start()
     for extra, out in ((xc_ref, x_ref), (dc_ref, dy_ref)):
         out[VIS:, :] = jnp.zeros((CROWS, D), BF16)
-        out[VIS : VIS + extra.shape[0], :] = extra[...]
+        for n in range(extra.shape[0]):
+            out[VIS + n * COND : VIS + (n + 1) * COND, :] = extra[n]
     for copy in copies:
         copy.wait()
 
@@ -152,30 +153,44 @@
         in_specs=[pl.BlockSpec(memory_space=pltpu.SMEM), ANYM, FULL, ANYM, FULL],
         out_specs=(FULL, FULL),
         scratch_shapes=[pltpu.SemaphoreType.DMA((2, FRAMES))],
-    )(perm, visual.reshape(FRAMES, PART, D), extra.reshape(-1, D), d_visual.reshape(FRAMES, PART, D), d_extra.reshape(-1, D))
-
-
-def restore_kernel(slot, y_ref, g_ref, yo_ref, go_ref, sem):
+    )(perm, visual.reshape(FRAMES, PART, D), extra[0], d_visual.reshape(FRAMES, PART, D), d_extra[0])
+
+
+def restore_kernel(slot, y_ref, g_ref, yo_ref, go_ref, yc_ref, gc_ref, yt, gt, sem):
     copies = []
     for f in range(FRAMES):
         rows = pl.ds(pl.multiple_of(slot[f] * PART, PART), PART)
         copies.append(pltpu.make_async_copy(y_ref.at[rows], yo_ref.at[f], sem.at[0, f]))
         copies.append(pltpu.make_async_copy(g_ref.at[rows], go_ref.at[f], sem.at[1, f]))
-    for copy in copies:
+    last = pl.ds(VIS, CROWS)
+    tails = [
+        pltpu.make_async_copy(y_ref.at[last], yt, sem.at[0, FRAMES]),
+        pltpu.make_async_copy(g_ref.at[last], gt, sem.at[1, FRAMES]),
+    ]
+    for copy in copies + tails:
         copy.start()
+    for copy in tails:
+        copy.wait()
+    for n in range(yc_ref.shape[0]):
+        yc_ref[n] = yt[n * COND : (n + 1) * COND]
+        gc_ref[n] = gt[n * COND : (n + 1) * COND]
     for copy in copies:
         copy.wait()
 
 
-def restore_rows(slot, y, g):
+def restore_rows(slot, y, g, parts):
     shape = (FRAMES, PART, D)
+    small = (parts, COND, D)
     return pl.pallas_call(
         restore_kernel,
         name="restore_rows",
-        out_shape=(jax.ShapeDtypeStruct(shape, BF16), jax.ShapeDtypeStruct(shape, F32)),
+        out_shape=(
+            jax.ShapeDtypeStruct(shape, BF16), jax.ShapeDtypeStruct(shape, F32),
+            jax.ShapeDtypeStruct(small, BF16), jax.ShapeDtypeStruct(small, F32),
+        ),
         in_specs=[pl.BlockSpec(memory_space=pltpu.SMEM), ANYM, ANYM],
-        out_specs=(FULL, FULL),
-        scratch_shapes=[pltpu.SemaphoreType.DMA((2, FRAMES))],
+        out_specs=(FULL,) * 4,
+        scratch_shapes=[VM((CROWS, D), BF16), VM((CROWS, D), F32), pltpu.SemaphoreType.DMA((2, FRAMES + 1))],
     )(slot, y, g)
 
 
@@ -1626,7 +1641,8 @@
 
 def own_meta(lengths, mask):
     frames = jnp.arange(FRAMES, dtype=jnp.int32)
-    ends = jnp.cumsum(lengths)
+    order = jnp.arange(lengths.shape[0])
+    ends = jnp.sum(jnp.where(order[:, None] <= order[None, :], lengths[:, None], 0), axis=0)
     reached = ends[None, :] <= frames[:, None]
     begin = jnp.sum(jnp.where(reached, lengths[None, :], 0), axis=1)
     episode = jnp.sum(reached, axis=1)[:, None] == jnp.arange(lengths.shape[0])[None, :]
@@ -1651,7 +1667,6 @@
     ln1_gain, ln1_bias, w_qkv, b_qkv, w_proj, b_proj, ln2_gain, ln2_bias, w_in, b_in, w_out, b_out,
 ):
     d, z = lax.axis_index("dp"), lax.axis_index("stream")
-    extra = conditioning.shape[1] * COND
     perm, slot, own = own_meta(episode_frames[0], patch_mask[0])
     x, dy = place_rows(perm, visual, conditioning, d_visual, d_conditioning)
     params = jnp.concatenate(
@@ -1670,7 +1685,7 @@
         grad_qkv, x_all, role_grad.astype(BF16), w_qkv, x, grad_h, grad_w_in, grad_w_proj, vectors, params
     )
     red_in = jnp.concatenate([red_in, red_in_last], axis=1)
-    out_visual, grad_visual = restore_rows(slot, output, grad_x)
+    out_visual, grad_visual, out_extra, grad_extra = restore_rows(slot, output, grad_x, conditioning.shape[1])
     owner = d * STREAMS + z
     owners = lax.axis_size("dp") * STREAMS
 
@@ -1679,8 +1694,8 @@
         return lax.dynamic_slice_in_dim(sums[start : start + rows].reshape(-1), owner * size, size, 0)
 
     return (
-        out_visual.reshape(visual.shape), output[VIS : VIS + extra].reshape(conditioning.shape),
-        grad_visual.reshape(visual.shape), grad_x[VIS : VIS + extra].reshape(conditioning.shape),
+        out_visual.reshape(visual.shape), out_extra.reshape(conditioning.shape),
+        grad_visual.reshape(visual.shape), grad_extra.reshape(conditioning.shape),
         share(0, 1), share(1, 1), red_qkv, share(2, 2), share(4, 1), red_proj, share(9, 1), share(10, 1), share(11, 1),
         red_in, share(5, 4), red_out.reshape(-1, D), share(12, 1),
     )

time: 342 us -> 336 us (0.982)
  local copies, waits for them, and re-layouts: 14.6 us -> 9.23 us
    reshape x4 -> x0, local copies, waits for them, and re-layouts: 3.85 us -> none  [the longest x1 1.3 us: place_rows(): extra.reshape(-1, D)]
where the time goes in v5:
time: 336 us; the launch traced here: 335 us
  Pallas kernels  311 us (93%)
  local copies, waits for them, and re-layouts  9.23 us (3%)
  matrix products  8.31 us (2%)
  other arithmetic  5.21 us (2%)
    pallas_call x4, Pallas kernels, comm_call(): pl.pallas_call(kernel, name=name, out_shape=tuple((jax.ShapeDtypeStruct(s...  303 us
    dot_general x1, matrix products, per_device(): jnp.einsum('rd,re->de', a.reshape(STREAMS * ROWS, D), grad_qkv.reshape(ST...  8.31 us

profile of v5, /device:TPU:0, one launch (start us, length us, event | category | flops | bytes accessed | tf_op | source)
XLA Modules:
  0.0 334.8 jit_solution(295062822590851494)
XLA Ops:
  0.7 0.8 select_reduce_fusion.5
  1.6 0.7 select_reduce_fusion.4
  2.9 0.7 select_bitcast_fusion
  3.7 0.6 select_maximum_fusion.m_hbm
  4.3 3.8 %place_rows.1 = (bf16[528,1024]{1,0:T(8,128)(2,1)}, bf16[528,1024]{1,0:T(8,128)(2,1)}) custom-call(s32[8]{0:T(128)} %copy-done.13, bf16[8,64,1024]{2,1,0:T(8,128)(2,1)} %bitcast.48, bf16[2,2,1024]{2,1,0:T(2,128)(2,1)} %bitcast.52, bf16[8,64,1024]{2,1,0:T(8,128)(2,1)} %bitcast.49, bf16[2,2,1024]{2,1,0:T(2,128)(2,1)} %bitcast.53), custom_call_target="tpu_custom_call" | custom-call | tf_op jit(solution)/shard_map/place_rows/pallas_call | solution.py:149
  8.3 0.6 reshape.301.par_ref.gain_ref
  8.9 85.1 %attend_forward.1 = (bf16[528,1024]{1,0:T(8,128)(2,1)}, bf16[4,528,1024]{2,1,0:T(8,128)(2,1)}, bf16[4,528,1024]{2,1,0:T(8,128)(2,1)}, bf16[8,256,512]{2,1,0:T(8,...) custom-call(bf16[528,1024]{1,0:T(8,128)(2,1)} %get-tuple-element.51., ...), custom_call_target="tpu_custom_call" | custom-call | tf_op jit(solution)/shard_map/attend_forward/pallas_call | solution.py:224
  94.1 74.7 %mlp.1 = (bf16[4,528,256]{2,1,0:T(8,128)(2,1)}, bf16[1024,1024]{1,0:T(8,128)(2,1)}, bf16[4096,1024]{1,0:T(8,128)(2,1)}, bf16[1024,1024]{1,0:T(8,128)(2,1)}, f32[...) custom-call(bf16[1024,4096]{1,0:T(8,128)(2,1)} %win_hbm.1, ...), custom_call_target="tpu_custom_call" | custom-call | tf_op jit(solution)/shard_map/mlp/pallas_call | solution.py:224
  168.8 78.6 %attend_backward.1 = (f32[4,32,1024]{2,1,0:T(8,128)}, bf16[4,528,768]{2,1,0:T(8,128)(2,1)}) custom-call(bf16[2,2,2,4,4,32,1024]{6,5,4,3,2,1,0:T(8,128)(2,1)} %bitcast.44, bf16[4,528,256]{2,1,0:T(8,128)(2,1)} %get-tuple-element.56.d_ref, bf16[8,256,512]{2,1,0:T(8,128)(2,1)} %get-tuple-element.57.q_hbm, bf16[8,256,512]{2,1,0:T(8,128)(2,1)} %get-tuple-element.58.k_hbm, ...), custom_call_target="tpu_custom_call" | custom-call | tf_op jit(solution)/shard_map/attend_backward/pallas_call | solution.py:224
  247.4 8.3 %bitcast_convert_fusion = bf16[1024,768]{1,0:T(8,128)(2,1)} fusion(bf16[4,528,1024]{2,1,0:T(8,128)(2,1)} %get-tuple-element.69, bf16[4,528,768]{2,1,0:T(8,128)(2,1)} %get-tuple-element.67.f_hbm), kind=kOutput, calls=%fused_computation | convolution fusion | flops 3322675200 | bytes 9142272 | tf_op jit(solution)/shard_map/rd,re->de/dot_general | solution.py:1681
  255.7 64.4 %finish_rows.1 = (f32[528,1024]{1,0:T(8,128)}, f32[32,3072]{1,0:T(8,128)}, f32[16,1024]{1,0:T(8,128)}, f32[32,1024]{1,0:T(8,128)}, f32[32,1024]{1,0:T(8,128)}) custom-call(bf16[4,528,768]{2,1,0:T(8,128)(2,1)} %get-tuple-element.67.f_hbm, bf16[4,528,1024]{2,1,0:T(8,128)(2,1)} %get-tuple-element.68.xa_hbm, bf16[2,2,8,32,768]{4,3,2,1,0:T(8,128)(2,1)} %bitcast.47, ...), custom_call_target="tpu_custom_call" | custom-call | tf_op jit(solution)/shard_map/finish_rows/pallas_call | solution.py:224
  320.1 1.8 pad_maximum_fusion
  321.9 1.1 fusion.9
  323.0 0.6 fusion.4
  323.6 0.6 fusion.2
  324.2 0.6 fusion
  324.8 4.5 %restore_rows.1 = (bf16[8,64,1024]{2,1,0:T(8,128)(2,1)}, f32[8,64,1024]{2,1,0:T(8,128)}, bf16[2,2,1024]{2,1,0:T(2,128)(2,1)}, f32[2,2,1024]{2,1,0:T(2,128)}) custom-call(s32[8]{0:T(128)} %copy-done.12, bf16[528,1024]{1,0:T(8,128)(2,1)} %get-tuple-element.54.y_ref, f32[528,1024]{1,0:T(8,128)} %get-tuple-element.74.g_ref), custom_call_target="tpu_custom_call" | custom-call | tf_op jit(solution)/shard_map/restore_rows/pallas_call | solution.py:184
  329.3 0.8 slice_bitcast_fusion
  330.1 0.6 dynamic_slice.54
  331.3 0.8 slice_bitcast_fusion.1
  332.0 0.6 dynamic_slice.45
  332.6 0.7 copy.56
  333.4 0.7 copy.57
  334.0 0.8 copy.58
  (52 shorter events, 1.4 us)
Async XLA Ops:
  0.7 7.4 %copy-start.6 = (bf16[1024]{0:T(1024)(128)(2,1)S(1)}, bf16[1024]{0:T(1024)(128)(2,1)}, u32[]{:S(2)}) copy-start(bf16[1024]{0:T(1024)(128)(2,1)} %param.28) | copy-start | bytes 6148
  0.7 7.5 %copy-start.7 = (bf16[1024]{0:T(1024)(128)(2,1)S(1)}, bf16[1024]{0:T(1024)(128)(2,1)}, u32[]{:S(2)}) copy-start(bf16[1024]{0:T(1024)(128)(2,1)} %param.29) | copy-start | bytes 6148
  0.7 7.5 %copy-start.5 = (bf16[3072]{0:T(1024)(128)(2,1)S(1)}, bf16[3072]{0:T(1024)(128)(2,1)}, u32[]{:S(2)}) copy-start(bf16[3072]{0:T(1024)(128)(2,1)} %param.31) | copy-start | bytes 18436
  0.7 7.5 %copy-start.4 = (bf16[4096]{0:T(1024)(128)(2,1)S(1)}, bf16[4096]{0:T(1024)(128)(2,1)}, u32[]{:S(2)}) copy-start(bf16[4096]{0:T(1024)(128)(2,1)} %param.37) | copy-start | bytes 24580
  0.7 7.5 %copy-start.8 = (bf16[1024]{0:T(1024)(128)(2,1)S(1)}, bf16[1024]{0:T(1024)(128)(2,1)}, u32[]{:S(2)}) copy-start(bf16[1024]{0:T(1024)(128)(2,1)} %param.33) | copy-start | bytes 6148
  0.7 7.5 %copy-start.9 = (bf16[1024]{0:T(1024)(128)(2,1)S(1)}, bf16[1024]{0:T(1024)(128)(2,1)}, u32[]{:S(2)}) copy-start(bf16[1024]{0:T(1024)(128)(2,1)} %param.34) | copy-start | bytes 6148
  0.7 7.5 %copy-start.10 = (bf16[1024]{0:T(1024)(128)(2,1)S(1)}, bf16[1024]{0:T(1024)(128)(2,1)}, u32[]{:S(2)}) copy-start(bf16[1024]{0:T(1024)(128)(2,1)} %param.35) | copy-start | bytes 6148
  0.7 7.5 %copy-start.11 = (bf16[1024]{0:T(1024)(128)(2,1)S(1)}, bf16[1024]{0:T(1024)(128)(2,1)}, u32[]{:S(2)}) copy-start(bf16[1024]{0:T(1024)(128)(2,1)} %param.39) | copy-start | bytes 6148
  2.4 91.7 %copy-start.12 = (s32[8]{0:T(128)}, s32[8]{0:T(128)S(1)}, u32[]{:S(2)}) copy-start(s32[8]{0:T(128)S(1)} %fusion.8.slot) | copy-start | bytes 100
  2.8 1.5 copy-start.13
  255.7 64.4 %copy-start.2 = (f32[32,3072]{1,0:T(8,128)S(1)}, f32[32,3072]{1,0:T(8,128)}, u32[]{:S(2)}) copy-start(f32[32,3072]{1,0:T(8,128)} %get-tuple-element.82) | copy-start | bytes 1179652
  320.1 12.5 %copy-start.1 = (f32[32,3072]{1,0:T(8,128)S(1)}, f32[32,3072]{1,0:T(8,128)}, u32[]{:S(2)}) copy-start(f32[32,3072]{1,0:T(8,128)} %get-tuple-element.123) | copy-start | bytes 1179652
  321.9 11.5 %copy-start.3 = (f32[32,1024]{1,0:T(8,128)S(1)}, f32[32,1024]{1,0:T(8,128)}, u32[]{:S(2)}) copy-start(f32[32,1024]{1,0:T(8,128)} %get-tuple-element.126) | copy-start | bytes 393220
  324.7 9.3 %copy-start = (f32[4,32,1024]{2,1,0:T(8,128)S(1)}, f32[4,32,1024]{2,1,0:T(8,128)}, u32[]{:S(2)}) copy-start(f32[4,32,1024]{2,1,0:T(8,128)} %get-tuple-element.84) | copy-start | bytes 1572868

commit v6 on v5

--- a/solution.py
+++ b/solution.py
@@ -901,7 +901,6 @@
 
     dqs = lax.fori_loop(0, FRAMES, cond_step, dqs)
     dqc[...] = jnp.concatenate([t[:, :HEAD_DIM] for t in dqs], axis=1) * 0.125
-    reducer.tick(1)
 
     def slot(i):
         start = pl.multiple_of(i * PART, PART)
@@ -946,7 +945,7 @@
 
     def sweep(i, carry):
         slot(i)
-        reducer.tick(i + 2)
+        reducer.tick(i + 1)
         return carry
 
     lax.fori_loop(0, FRAMES, sweep, 0)
@@ -973,6 +972,7 @@
     lax.fori_loop(0, FRAMES, finish, 0)
     save = pltpu.make_async_copy(g_ref, g_out, isem.at[5])
     save.start()
+    reducer.tick(LATE + 5)
     fin = reducer.fin
     outs = [pltpu.make_async_copy(fin.at[k], oo_ref.at[k], osem.at[k]) for k in range(4)]
     for copy in outs:
@@ -1011,12 +1011,12 @@
 
 def finish_kernel(
     nx, ny, rb,
-    f_hbm, xa_hbm, gq_ref, w_hbm, x_hbm, h_hbm, gi_ref, gp_ref, v_ref, gain_ref,
+    f_hbm, xa_hbm, gq_ref, w_hbm, x_hbm, h_hbm, gi_ref, gp_ref, ri_hbm, v_ref, gain_ref,
     gx_ref, oq_ref, ov_ref, oi_ref, op_ref,
     f, xa, w, x_own, h_own, big, near_in, near_out, own, land, tail, tail_out, total,
     q1, rq1a, rq1b, sq1a, sq1b, rq2a, rq2b, sq2, rq3, sq3, vm, vd, vx, vy, vz1, vz2, hold,
     isem, dsend, drecv, send, recv, csend, crecv, lsem,
-    qs1a, qr1a, qs1b, qr1b, qs2a, qr2a, qs2b, qr2b, qs3, qr3, qs4, qr4, vs, vr, vsx, vrx, vsy, vry, relay, rsend, rrecv, cols_sum, osem,
+    qs1a, qr1a, qs1b, qr1b, qs2a, qr2a, qs2b, qr2b, qs3, qr3, qs4, qr4, vs, vr, vsx, vrx, vsy, vry, relay, rsend, rrecv, cols_sum, osem, kept, ksem,
     *refs,
 ):
     at = Place(nx, ny)
@@ -1039,7 +1039,8 @@
         pltpu.make_async_copy(x_hbm, x_own, isem.at[6]),
         pltpu.make_async_copy(h_hbm, h_own, isem.at[7]),
     ]
-    for copy in loads + late:
+    keep = pltpu.make_async_copy(ri_hbm, kept, ksem.at[0])
+    for copy in loads + late + [keep]:
         copy.start()
     at.greet()
     rows = pl.ds(pl.multiple_of(c * HALF, HALF), HALF)
@@ -1309,9 +1310,12 @@
     done.start()
     move(4)
     outs = [
-        pltpu.make_async_copy(reducer.fin.at[k], oi_ref.at[:, pl.ds(k * D, D)], osem.at[k]) for k in range(LAST - 1)
+        pltpu.make_async_copy(reducer.fin.at[k], oi_ref.at[:, pl.ds((EARLY + k) * D, D)], osem.at[k])
+        for k in range(LAST - 1)
     ]
     outs += [pltpu.make_async_copy(reducer.fin.at[LAST - 1], op_ref, osem.at[LAST - 1])]
+    keep.wait()
+    outs += [pltpu.make_async_copy(kept, oi_ref.at[:, pl.ds(0, EARLY * D)], ksem.at[1])]
     for copy in outs:
         copy.start()
     v_z2().wait_recv()
@@ -1360,7 +1364,7 @@
     v_done.wait()
 
 
-def finish_rows(flat, x_all, g_qkv, w_qkv, x, h, g_in, g_proj, vectors, gain):
+def finish_rows(flat, x_all, g_qkv, w_qkv, x, h, g_in, g_proj, red_in, vectors, gain):
     nx, ny, rb = grid_shape()
 
     def v(*shape):
@@ -1381,14 +1385,15 @@
         dma(nx - 1), dma(nx - 1), dma(ny - 1), dma(ny - 1), dma(ny - 1), dma(ny - 1), dma(nx - 1), dma(nx - 1),
         pltpu.SemaphoreType.DMA, pltpu.SemaphoreType.DMA, dma(3, 3), dma(3, 3),
         dma(3), dma(3), dma(nx - 1), dma(nx - 1), dma(ny - 1), dma(ny - 1),
-        v(2, HALF, D), dma(2), dma(2), vf(8, 3 * GW), dma(LAST),
+        v(2, HALF, D), dma(2), dma(2), vf(8, 3 * GW), dma(LAST), vf(rb, EARLY * D), dma(2),
     ] + Reducer.scratch(LAST, nx, ny, rb)
     outs = (
-        ((ROWS, D), F32), ((rb, 3 * D), F32), ((16, D), F32), ((rb, (LAST - 1) * D), F32), ((rb, D), F32),
+        ((ROWS, D), F32), ((rb, 3 * D), F32), ((16, D), F32), ((rb, 4 * D), F32), ((rb, D), F32),
     )
     ops = (
         flat, x_all, g_qkv.reshape(ny, nx, 8, rb, 3 * GW), w_qkv, x, h,
         g_in.reshape(ny, nx, 2, STREAMS, rb, (LAST - 1) * D), g_proj.reshape(ny, nx, 2, STREAMS, rb, D),
+        red_in,
     )
     return comm_call(
         functools.partial(finish_kernel, nx, ny, rb), "finish_rows", 4, outs, scratch, ops, (vectors, gain)
@@ -1681,10 +1686,9 @@
     role_grad = jnp.einsum(
         "rd,re->de", a.reshape(STREAMS * ROWS, D), grad_qkv.reshape(STREAMS * ROWS, 3 * GW), preferred_element_type=F32
     )
-    grad_x, red_qkv, sums, red_in_last, red_proj = finish_rows(
-        grad_qkv, x_all, role_grad.astype(BF16), w_qkv, x, grad_h, grad_w_in, grad_w_proj, vectors, params
+    grad_x, red_qkv, sums, red_in, red_proj = finish_rows(
+        grad_qkv, x_all, role_grad.astype(BF16), w_qkv, x, grad_h, grad_w_in, grad_w_proj, red_in, vectors, params
     )
-    red_in = jnp.concatenate([red_in, red_in_last], axis=1)
     out_visual, grad_visual, out_extra, grad_extra = restore_rows(slot, output, grad_x, conditioning.shape[1])
     owner = d * STREAMS + z
     owners = lax.axis_size("dp") * STREAMS

time: 336 us -> 336 us (level)
  no operation moved by 1% of the time
where the time goes in v6:
time: 336 us
  Pallas kernels  313 us (93%)
  local copies, waits for them, and re-layouts  9.91 us (3%)
  matrix products  8.3 us (2%)
  other arithmetic  3.43 us (1%)
    pallas_call x4, Pallas kernels, comm_call(): pl.pallas_call(kernel, name=name, out_shape=tuple((jax.ShapeDtypeStruct(s...  305 us
    dot_general x1, matrix products, per_device(): jnp.einsum('rd,re->de', a.reshape(STREAMS * ROWS, D), grad_qkv.reshape(ST...  8.3 us

profile of v6, /device:TPU:0, one launch (start us, length us, event | category | flops | bytes accessed | tf_op | source)
XLA Modules:
  0.0 335.7 jit_solution(18028494410022124848)
XLA Ops:
  0.7 0.8 select_reduce_fusion.5
  1.6 0.7 select_reduce_fusion.4
  2.9 0.7 select_bitcast_fusion
  3.7 0.6 select_maximum_fusion.m_hbm
  4.3 3.8 %place_rows.1 = (bf16[528,1024]{1,0:T(8,128)(2,1)}, bf16[528,1024]{1,0:T(8,128)(2,1)}) custom-call(s32[8]{0:T(128)} %copy-done.13, bf16[8,64,1024]{2,1,0:T(8,128)(2,1)} %bitcast.48, bf16[2,2,1024]{2,1,0:T(2,128)(2,1)} %bitcast.52, bf16[8,64,1024]{2,1,0:T(8,128)(2,1)} %bitcast.49, bf16[2,2,1024]{2,1,0:T(2,128)(2,1)} %bitcast.53), custom_call_target="tpu_custom_call" | custom-call | tf_op jit(solution)/shard_map/place_rows/pallas_call | solution.py:149
  8.3 0.6 reshape.301.par_ref.gain_ref
  8.9 85.1 %attend_forward.1 = (bf16[528,1024]{1,0:T(8,128)(2,1)}, bf16[4,528,1024]{2,1,0:T(8,128)(2,1)}, bf16[4,528,1024]{2,1,0:T(8,128)(2,1)}, bf16[8,256,512]{2,1,0:T(8,...) custom-call(bf16[528,1024]{1,0:T(8,128)(2,1)} %get-tuple-element.51., ...), custom_call_target="tpu_custom_call" | custom-call | tf_op jit(solution)/shard_map/attend_forward/pallas_call | solution.py:224
  94.1 74.7 %mlp.1 = (bf16[4,528,256]{2,1,0:T(8,128)(2,1)}, bf16[1024,1024]{1,0:T(8,128)(2,1)}, bf16[4096,1024]{1,0:T(8,128)(2,1)}, bf16[1024,1024]{1,0:T(8,128)(2,1)}, f32[...) custom-call(bf16[1024,4096]{1,0:T(8,128)(2,1)} %win_hbm.1, ...), custom_call_target="tpu_custom_call" | custom-call | tf_op jit(solution)/shard_map/mlp/pallas_call | solution.py:224
  168.8 77.0 %attend_backward.1 = (f32[4,32,1024]{2,1,0:T(8,128)}, bf16[4,528,768]{2,1,0:T(8,128)(2,1)}) custom-call(bf16[2,2,2,4,4,32,1024]{6,5,4,3,2,1,0:T(8,128)(2,1)} %bitcast.44, bf16[4,528,256]{2,1,0:T(8,128)(2,1)} %get-tuple-element.56.d_ref, bf16[8,256,512]{2,1,0:T(8,128)(2,1)} %get-tuple-element.57.q_hbm, bf16[8,256,512]{2,1,0:T(8,128)(2,1)} %get-tuple-element.58.k_hbm, ...), custom_call_target="tpu_custom_call" | custom-call | tf_op jit(solution)/shard_map/attend_backward/pallas_call | solution.py:224
  245.7 8.3 %bitcast_convert_fusion = bf16[1024,768]{1,0:T(8,128)(2,1)} fusion(bf16[4,528,1024]{2,1,0:T(8,128)(2,1)} %get-tuple-element.69, bf16[4,528,768]{2,1,0:T(8,128)(2,1)} %get-tuple-element.67.f_hbm), kind=kOutput, calls=%fused_computation | convolution fusion | flops 3322675200 | bytes 9142272 | tf_op jit(solution)/shard_map/rd,re->de/dot_general | solution.py:1686
  254.0 68.0 %finish_rows.1 = (f32[528,1024]{1,0:T(8,128)}, f32[32,3072]{1,0:T(8,128)}, f32[16,1024]{1,0:T(8,128)}, f32[32,4096]{1,0:T(8,128)}, f32[32,1024]{1,0:T(8,128)}) custom-call(bf16[4,528,768]{2,1,0:T(8,128)(2,1)} %get-tuple-element.67.f_hbm, bf16[4,528,1024]{2,1,0:T(8,128)(2,1)} %get-tuple-element.68.xa_hbm, bf16[2,2,8,32,768]{4,3,2,1,0:T(8,128)(2,1)} %bitcast.47, ...), custom_call_target="tpu_custom_call" | custom-call | tf_op jit(solution)/shard_map/finish_rows/pallas_call | solution.py:224
  322.1 0.9 fusion.9
  323.0 0.6 fusion.4
  323.6 0.6 fusion.2
  324.2 0.6 fusion
  324.8 4.5 %restore_rows.1 = (bf16[8,64,1024]{2,1,0:T(8,128)(2,1)}, f32[8,64,1024]{2,1,0:T(8,128)}, bf16[2,2,1024]{2,1,0:T(2,128)(2,1)}, f32[2,2,1024]{2,1,0:T(2,128)}) custom-call(s32[8]{0:T(128)} %copy-done.12, bf16[528,1024]{1,0:T(8,128)(2,1)} %get-tuple-element.54.y_ref, f32[528,1024]{1,0:T(8,128)} %get-tuple-element.75.g_ref), custom_call_target="tpu_custom_call" | custom-call | tf_op jit(solution)/shard_map/restore_rows/pallas_call | solution.py:184
  329.3 0.8 slice_bitcast_fusion
  330.2 0.6 dynamic_slice.54
  331.3 0.8 slice_bitcast_fusion.1
  332.1 0.6 dynamic_slice.45
  332.7 0.7 copy.57
  333.4 0.7 copy.58
  334.1 0.8 copy.59
  334.9 0.8 copy.60
  (52 shorter events, 1.4 us)
Async XLA Ops:
  0.7 7.4 %copy-start.6 = (bf16[1024]{0:T(1024)(128)(2,1)S(1)}, bf16[1024]{0:T(1024)(128)(2,1)}, u32[]{:S(2)}) copy-start(bf16[1024]{0:T(1024)(128)(2,1)} %param.28) | copy-start | bytes 6148
  0.7 7.5 %copy-start.7 = (bf16[1024]{0:T(1024)(128)(2,1)S(1)}, bf16[1024]{0:T(1024)(128)(2,1)}, u32[]{:S(2)}) copy-start(bf16[1024]{0:T(1024)(128)(2,1)} %param.29) | copy-start | bytes 6148
  0.7 7.5 %copy-start.5 = (bf16[3072]{0:T(1024)(128)(2,1)S(1)}, bf16[3072]{0:T(1024)(128)(2,1)}, u32[]{:S(2)}) copy-start(bf16[3072]{0:T(1024)(128)(2,1)} %param.31) | copy-start | bytes 18436
  0.7 7.5 %copy-start.4 = (bf16[4096]{0:T(1024)(128)(2,1)S(1)}, bf16[4096]{0:T(1024)(128)(2,1)}, u32[]{:S(2)}) copy-start(bf16[4096]{0:T(1024)(128)(2,1)} %param.37) | copy-start | bytes 24580
  0.7 7.5 %copy-start.8 = (bf16[1024]{0:T(1024)(128)(2,1)S(1)}, bf16[1024]{0:T(1024)(128)(2,1)}, u32[]{:S(2)}) copy-start(bf16[1024]{0:T(1024)(128)(2,1)} %param.33) | copy-start | bytes 6148
  0.7 7.5 %copy-start.9 = (bf16[1024]{0:T(1024)(128)(2,1)S(1)}, bf16[1024]{0:T(1024)(128)(2,1)}, u32[]{:S(2)}) copy-start(bf16[1024]{0:T(1024)(128)(2,1)} %param.34) | copy-start | bytes 6148
  0.7 7.5 %copy-start.10 = (bf16[1024]{0:T(1024)(128)(2,1)S(1)}, bf16[1024]{0:T(1024)(128)(2,1)}, u32[]{:S(2)}) copy-start(bf16[1024]{0:T(1024)(128)(2,1)} %param.35) | copy-start | bytes 6148
  0.7 7.5 %copy-start.11 = (bf16[1024]{0:T(1024)(128)(2,1)S(1)}, bf16[1024]{0:T(1024)(128)(2,1)}, u32[]{:S(2)}) copy-start(bf16[1024]{0:T(1024)(128)(2,1)} %param.39) | copy-start | bytes 6148
  2.4 91.7 %copy-start.12 = (s32[8]{0:T(128)}, s32[8]{0:T(128)S(1)}, u32[]{:S(2)}) copy-start(s32[8]{0:T(128)S(1)} %fusion.8.slot) | copy-start | bytes 100
  2.8 1.5 copy-start.13
  322.1 10.6 %copy-start.2 = (f32[32,3072]{1,0:T(8,128)S(1)}, f32[32,3072]{1,0:T(8,128)}, u32[]{:S(2)}) copy-start(f32[32,3072]{1,0:T(8,128)} %get-tuple-element.123) | copy-start | bytes 1179652
  322.1 11.3 %copy-start.3 = (f32[32,1024]{1,0:T(8,128)S(1)}, f32[32,1024]{1,0:T(8,128)}, u32[]{:S(2)}) copy-start(f32[32,1024]{1,0:T(8,128)} %get-tuple-element.126) | copy-start | bytes 393220
  324.8 9.3 %copy-start.1 = (f32[32,4096]{1,0:T(8,128)S(1)}, f32[32,4096]{1,0:T(8,128)}, u32[]{:S(2)}) copy-start(f32[32,4096]{1,0:T(8,128)} %get-tuple-element.130) | copy-start | bytes 1572868
  324.8 10.1 %copy-start = (f32[4,32,1024]{2,1,0:T(8,128)S(1)}, f32[4,32,1024]{2,1,0:T(8,128)}, u32[]{:S(2)}) copy-start(f32[4,32,1024]{2,1,0:T(8,128)} %get-tuple-element.84) | copy-start | bytes 1572868
